TPU v7x, 32 devices: a whole 2x2x4 slice. The times are simulated.
32 devices in a mesh: section: 4 (over y, x), slab: 8 (over z, core).
Axes of the slice: x: 2, y: 2, z: 4, core: 2. Of those that a mesh axis runs over, the one named last changes fastest.
Arguments:
- features_in: bfloat16 [2, 256, 8, 2, 64], P(None, None, 'slab'), may hold values from -6 to 6
- labels: int32 [2, 8, 2, 64], P(None, 'slab'), may hold values from 0 to 5
- offsets: int32 [3, 3], replicated, may hold values from -1 to 1, as said below
- conv_weight: bfloat16 [4, 3, 3, 3, 256, 256], P('section'), may hold values from -0.078125 to 0.078125
- branch_weight: bfloat16 [4, 256, 256], P('section'), may hold values from -0.375 to 0.375
- head_weight: bfloat16 [256, 3], replicated, may hold values from -0.375 to 0.375
Outputs:
- loss: float32 [], replicated
- grad_conv: float32 [4, 3, 3, 3, 256, 256], P('section')
- grad_branch: float32 [4, 256, 256], P('section')
- grad_head: float32 [256, 3], replicated
Inputs may be any that keep to these rules, and one draw needn't show every extreme that they name: Row j of the offsets has a nonzero entry j.
All inputs are finite; a program needn't handle non-finite values.
Results may differ from a plain program's by a relative error of at most 0.0023.
Values may be sent and summed in bfloat16 or wider, within the bound.
No kernel may reach another device: no remote copies, remote signals or barrier semaphores. Data moves between devices by JAX's collectives and lax.ppermute only.
A program may use at most 64 MiB of HBM per device.

v0:
```python
import jax
import jax.numpy as jnp
from jax import lax
from jax.sharding import PartitionSpec as P

loss_scale = 1024.0


def extended(block, sides, width):
    for axis, dim in sides:
        count = lax.axis_size(axis)
        forward = [(i, i + 1) for i in range(count - 1)]
        backward = [(target, source) for source, target in forward]
        low = lax.ppermute(
            lax.slice_in_dim(block, block.shape[dim] - width, None, axis=dim), axis, forward
        )
        high = lax.ppermute(lax.slice_in_dim(block, 0, width, axis=dim), axis, backward)
        block = jnp.concatenate([low, block, high], axis=dim)
    return block


def from_behind(x, axis, by):
    peers = lax.axis_size(axis)
    pairs = [(i, i + by) for i in range(peers) if 0 <= i + by < peers]
    return lax.ppermute(x, axis, pairs)


def partner(block, axis, apart):
    count = lax.axis_size(axis)
    route = []
    for low in range(count):
        high = low | 1 << apart
        if high != low and high < count:
            route += [(low, high), (high, low)]
    return lax.ppermute(block, axis, route)


def conv_local(padded, kernel):
    result = lax.conv_general_dilated(
        padded[None],
        kernel,
        (1, 1, 1),
        ((0, 0), (1, 1), (1, 1)),
        dimension_numbers=("NCDHW", "DHWIO", "NCDHW"),
        preferred_element_type=jnp.float32,
    )
    return result[0]


def weight_grad(padded, cotangent):
    result = lax.conv_general_dilated(
        padded[:, None],
        cotangent[:, None],
        (1, 1, 1),
        ((0, 0), (1, 1), (1, 1)),
        dimension_numbers=("NCDHW", "OIDHW", "NCDHW"),
        preferred_element_type=jnp.float32,
    )
    return jnp.transpose(result, (2, 3, 4, 0, 1))


def silu_slope(preact):
    logistic = jax.nn.sigmoid(preact)
    return logistic * (1.0 + preact * (1.0 - logistic))


def with_faces(volume):
    return extended(volume, (("slab", 1),), 1)


def pass_along(volume, hops):
    return from_behind(volume, "section", hops)


def mirror(volume):
    section_count = lax.axis_size("section")
    bit_count = section_count.bit_length() - 1
    bit_order = list(range(bit_count))
    for bit_number in bit_order:
        volume = partner(volume, "section", bit_number)
    return volume


def take_slot(buffer, slot_id):
    return lax.dynamic_index_in_dim(buffer, slot_id, 0, keepdims=False)


def put_slot(buffer, slot_id, value, active):
    previous = take_slot(buffer, slot_id)
    return lax.dynamic_update_index_in_dim(buffer, jnp.where(active, value, previous), slot_id, 0)


def body(features_in, labels, offsets, conv_weight, branch_weight, head_weight):
    sections = lax.axis_size("section")
    half = sections // 2
    section = lax.axis_index("section")
    encoder = section < half
    final_section = section == sections - 1
    micro = features_in.shape[0]
    moments = micro + sections - 1
    kernel = conv_weight[0]
    flipped = jnp.swapaxes(jnp.flip(kernel, (0, 1, 2)), 3, 4)
    mixing = branch_weight[0]
    act_shape = features_in.shape[1:]
    depth = act_shape[1]
    padded_shape = (act_shape[0], depth + 2, act_shape[2], act_shape[3])
    zero_act = jnp.zeros(act_shape, jnp.bfloat16)
    pads = jnp.zeros((micro,) + padded_shape, jnp.bfloat16)
    branches = jnp.zeros((micro,) + act_shape, jnp.bfloat16)
    outputs = jnp.zeros((micro,) + act_shape, jnp.bfloat16)
    skips = jnp.zeros((micro,) + act_shape, jnp.bfloat16)
    preacts = jnp.zeros((micro,) + act_shape, jnp.float32)

    def forward_step(moment, loop_state):
        incoming, skips, pads, branches, preacts, outputs = loop_state
        micro_id = moment - section
        active = (micro_id >= 0) & (micro_id < micro)
        slot_id = jnp.clip(micro_id, 0, micro - 1)
        current = jnp.where(section == 0, take_slot(features_in, slot_id), incoming)
        branch = jnp.where(encoder, current, take_slot(skips, slot_id))
        padded = with_faces(current)
        preact = conv_local(padded, kernel) + jnp.einsum(
            "io,izyx->ozyx", mixing, branch, preferred_element_type=jnp.float32
        )
        output = jax.nn.silu(preact).astype(jnp.bfloat16)
        pads = put_slot(pads, slot_id, padded, active)
        branches = put_slot(branches, slot_id, branch, active)
        outputs = put_slot(outputs, slot_id, output, active)
        preacts = put_slot(preacts, slot_id, preact, active)
        incoming = pass_along(output, 1)
        arrived = mirror(output)
        partner_id = moment - (sections - 1 - section)
        landing = jnp.logical_not(encoder) & (partner_id >= 0) & (partner_id < micro)
        skips = put_slot(skips, jnp.clip(partner_id, 0, micro - 1), arrived, landing)
        return (incoming, skips, pads, branches, preacts, outputs)

    loop_state = (zero_act, skips, pads, branches, preacts, outputs)
    loop_state = lax.fori_loop(0, moments, forward_step, loop_state)
    skips, pads, branches, preacts, outputs = (
        loop_state[1],
        loop_state[2],
        loop_state[3],
        loop_state[4],
        loop_state[5],
    )
    count = micro * offsets.shape[0] * depth * act_shape[2] * act_shape[3] * lax.axis_size("slab")
    logits = jnp.einsum("co,mczyx->mozyx", head_weight, outputs, preferred_element_type=jnp.float32)
    label_pad = extended(labels, (("slab", 1),), 1)
    label_pad = jnp.pad(label_pad, ((0, 0), (0, 0), (1, 1), (1, 1)))
    zero_index = jnp.zeros((), jnp.int32)
    target_maps = []
    for channel in range(offsets.shape[0]):
        neighbor = lax.dynamic_slice(
            label_pad,
            (zero_index, 1 + offsets[channel, 0], 1 + offsets[channel, 1], 1 + offsets[channel, 2]),
            labels.shape,
        )
        same = (neighbor == labels) & (labels != 0)
        target_maps.append(jnp.where(same, 1.0, 0.0).astype(jnp.float32))
    targets = jnp.stack(target_maps, axis=1)
    loss_part = jnp.where(final_section, jnp.sum(jax.nn.softplus(logits) - targets * logits), 0.0)
    logit_grad = (loss_scale * (jax.nn.sigmoid(logits) - targets) / count).astype(jnp.bfloat16)
    head_part = jnp.einsum(
        "mczyx,mozyx->co", outputs, logit_grad, preferred_element_type=jnp.float32
    )
    head_part = jnp.where(final_section, head_part, 0.0)
    loss_sum, grad_head = lax.psum((loss_part, head_part), ("section", "slab"))
    head_cotangent = jnp.einsum(
        "co,mozyx->mczyx", head_weight, logit_grad, preferred_element_type=jnp.float32
    )

    def backward_step(moment, loop_state):
        incoming, skip_grads, grad_kernel, grad_mixing = loop_state
        micro_id = moment - (sections - 1 - section)
        active = (micro_id >= 0) & (micro_id < micro)
        slot_id = jnp.clip(micro_id, 0, micro - 1)
        from_skip = jnp.where(encoder, take_slot(skip_grads, slot_id).astype(jnp.float32), 0.0)
        upstream = jnp.where(
            final_section,
            take_slot(head_cotangent, slot_id),
            incoming.astype(jnp.float32) + from_skip,
        )
        padded = take_slot(pads, slot_id)
        branch = take_slot(branches, slot_id)
        preact = take_slot(preacts, slot_id)
        pre_grad = (upstream * silu_slope(preact)).astype(jnp.bfloat16)
        grad_kernel = grad_kernel + jnp.where(active, weight_grad(padded, pre_grad), 0.0)
        grad_mixing = grad_mixing + jnp.where(
            active,
            jnp.einsum("izyx,ozyx->io", branch, pre_grad, preferred_element_type=jnp.float32),
            0.0,
        )
        branch_grad = jnp.einsum(
            "io,ozyx->izyx", mixing, pre_grad, preferred_element_type=jnp.float32
        )
        input_grad = conv_local(with_faces(pre_grad), flipped)
        sent_down = jnp.where(encoder, input_grad + branch_grad, input_grad).astype(jnp.bfloat16)
        incoming = pass_along(sent_down, -1)
        arrived = mirror(branch_grad.astype(jnp.bfloat16))
        partner_id = moment - section
        landing = encoder & (partner_id >= 0) & (partner_id < micro)
        skip_grads = put_slot(skip_grads, jnp.clip(partner_id, 0, micro - 1), arrived, landing)
        return (incoming, skip_grads, grad_kernel, grad_mixing)

    loop_state = (
        zero_act,
        jnp.zeros((micro,) + act_shape, jnp.bfloat16),
        jnp.zeros(kernel.shape, jnp.float32),
        jnp.zeros(mixing.shape, jnp.float32),
    )
    loop_state = lax.fori_loop(0, moments, backward_step, loop_state)
    grad_kernel, grad_mixing = lax.psum((loop_state[2], loop_state[3]), "slab")
    return (loss_sum / count, grad_kernel[None], grad_mixing[None], grad_head)


def solution(mesh):
    placed = (
        P(None, None, "slab", None, None),
        P(None, "slab", None, None),
        P(),
        P("section", None, None, None, None, None),
        P("section", None, None),
        P(),
    )
    return jax.shard_map(
        body,
        mesh=mesh,
        in_specs=placed,
        out_specs=(P(), P("section", None, None, None, None, None), P("section", None, None), P()),
        check_vma=False,
    )
```

profile of v0, /device:TPU:3, one launch (start us, length us, event | category | flops | bytes accessed | tf_op | source)
XLA Modules:
  0.0 494.2 jit_solution(3545565926020276218)
XLA Ops:
  7.2 2.6 collective-permute-start.11
  9.8 3.1 collective-permute-start.10
  26.1 6.2 %copy.35 = bf16[1,3,3,3,256,256]{4,5,3,2,1,0:T(8,128)(2,1)} copy(bf16[1,3,3,3,256,256]{5,4,3,2,1,0:T(8,128)(2,1)} %param.13) | data formatting | bytes 7077888 | tf_op args[3]
  32.3 4.1 reverse_bitcast_fusion
  42.6 121.5 %while.45 = (s32[]{:T(128)}, bf16[256,1,2,64]{0,3,2,1:T(8,128)(2,1)}, bf16[2,256,1,2,64]{1,4,3,2,0:T(8,128)(2,1)}, bf16[2,256,3,2,64]{1,4,3,2,0:T(8,128)(2,1)}, ...) while((s32[]{:T(128)}, ...), condition=%wide.region_1.2_spmd, body=%wide.region_0.1_spmd.sunk | while | flops 358838272 | bytes 16402240 | solution.py:138
  45.1 2.4 collective-permute-start.1
  47.5 2.5 collective-permute-start
  57.8 4.1 collective-permute-start.2
  63.0 2.4 collective-permute-done.4
  68.5 4.2 collective-permute-start.1
  72.8 1.9 collective-permute-start
  82.9 3.5 collective-permute-start.2
  87.9 2.1 collective-permute-done.4
  93.2 4.1 collective-permute-start.1
  97.4 1.9 collective-permute-start
  107.6 3.4 collective-permute-start.2
  112.2 2.1 collective-permute-done.4
  117.5 4.4 collective-permute-start.1
  132.2 3.4 collective-permute-start.2
  136.8 2.1 collective-permute-done.4
  142.1 4.4 collective-permute-start.1
  156.8 3.2 collective-permute-start.2
  161.2 2.1 collective-permute-done.4
  166.7 154.8 %while.46 = (s32[]{:T(128)}, bf16[256,1,2,64]{0,3,2,1:T(8,128)(2,1)S(1)}, bf16[2,256,1,2,64]{1,4,3,2,0:T(8,128)(2,1)S(1)}, f32[3,3,3,256,256]{4,3,2,1,0:T(8,128)...) while((s32[]{:T(128)}, ...), condition=%wide.region_5.6_spmd.clone, body=%wide.region_4.5_spmd.clone.sunk | while | flops 679309312 | bytes 41564916 | solution.py:211
  168.3 4.6 collective-permute-start.6
  175.9 6.6 %select_add_fusion.2 = f32[3,3,3,256,256]{4,3,2,1,0:T(8,128)} fusion(f32[3,3,3,256,256]{4,3,2,1,0:T(8,128)} %get-tuple-element.1035, pred[]{:T(512)S(6)} %compare.26, pred[]{:T(512)S(6)} %and.78, bf16[256,1,3,2,64]{0,4,3,2,1:T(8,128)(2,1)S(1)} %dynamic-slice_bitcast_fusion.2, bf16[256,1,1,2,64]{0,4,3,2,1:T(8,128)(2,1)} %bitcast.308), kind=kOutput, calls=%fused_computation.37.clone.1 | convolution fusion | flops 304152576 | bytes 14417922 | tf_op jit(solution)/shard_map/while/body/eval_jaxpr/transpose | solution.py:59
  186.9 2.0 collective-permute-done.8
  188.9 3.1 collective-permute-start.7
  192.0 2.8 collective-permute-done.7
  196.4 6.0 %collective-permute-start.6 = (bf16[256,1,2,64]{0,3,2,1:T(8,128)(2,1)}, bf16[256,1,2,64]{0,3,2,1:T(8,128)(2,1)S(1)}, u32[]{:S(2)}, u32[]{:S(2)}) collective-permute-start(bf16[256,1,2,64]{0,3,2,1:T(8,128)(2,1)} %fusion.90), channel_id=1, source_target_pairs={{0,1},{1,2},{2,3},{3,4},{4,5},{5,6},{6,7},{8,9},{9,10},{10,11},{11... | collective-permute-start | bytes 196616 | tf_op jit(solution)/shard_map/while/body/eval_jaxpr/ppermute | solution.py:14
  205.3 8.8 %select_add_fusion.2 = f32[3,3,3,256,256]{4,3,2,1,0:T(8,128)} fusion(f32[3,3,3,256,256]{4,3,2,1,0:T(8,128)} %get-tuple-element.1035, pred[]{:T(512)S(6)} %compare.26, pred[]{:T(512)S(6)} %and.78, bf16[256,1,3,2,64]{0,4,3,2,1:T(8,128)(2,1)S(1)} %dynamic-slice_bitcast_fusion.2, bf16[256,1,1,2,64]{0,4,3,2,1:T(8,128)(2,1)} %bitcast.308), kind=kOutput, calls=%fused_computation.37.clone.1 | convolution fusion | flops 304152576 | bytes 14417922 | tf_op jit(solution)/shard_map/while/body/eval_jaxpr/transpose | solution.py:59
  220.8 2.6 collective-permute-start.7
  224.5 2.2 collective-permute-done.7
  228.3 5.6 %collective-permute-start.6 = (bf16[256,1,2,64]{0,3,2,1:T(8,128)(2,1)}, bf16[256,1,2,64]{0,3,2,1:T(8,128)(2,1)S(1)}, u32[]{:S(2)}, u32[]{:S(2)}) collective-permute-start(bf16[256,1,2,64]{0,3,2,1:T(8,128)(2,1)} %fusion.90), channel_id=1, source_target_pairs={{0,1},{1,2},{2,3},{3,4},{4,5},{5,6},{6,7},{8,9},{9,10},{10,11},{11... | collective-permute-start | bytes 196616 | tf_op jit(solution)/shard_map/while/body/eval_jaxpr/ppermute | solution.py:14
  236.9 8.8 %select_add_fusion.2 = f32[3,3,3,256,256]{4,3,2,1,0:T(8,128)} fusion(f32[3,3,3,256,256]{4,3,2,1,0:T(8,128)} %get-tuple-element.1035, pred[]{:T(512)S(6)} %compare.26, pred[]{:T(512)S(6)} %and.78, bf16[256,1,3,2,64]{0,4,3,2,1:T(8,128)(2,1)S(1)} %dynamic-slice_bitcast_fusion.2, bf16[256,1,1,2,64]{0,4,3,2,1:T(8,128)(2,1)} %bitcast.308), kind=kOutput, calls=%fused_computation.37.clone.1 | convolution fusion | flops 304152576 | bytes 14417922 | tf_op jit(solution)/shard_map/while/body/eval_jaxpr/transpose | solution.py:59
  252.1 3.4 collective-permute-start.7
  256.1 1.9 collective-permute-done.7
  259.6 5.9 %collective-permute-start.6 = (bf16[256,1,2,64]{0,3,2,1:T(8,128)(2,1)}, bf16[256,1,2,64]{0,3,2,1:T(8,128)(2,1)S(1)}, u32[]{:S(2)}, u32[]{:S(2)}) collective-permute-start(bf16[256,1,2,64]{0,3,2,1:T(8,128)(2,1)} %fusion.90), channel_id=1, source_target_pairs={{0,1},{1,2},{2,3},{3,4},{4,5},{5,6},{6,7},{8,9},{9,10},{10,11},{11... | collective-permute-start | bytes 196616 | tf_op jit(solution)/shard_map/while/body/eval_jaxpr/ppermute | solution.py:14
  268.5 8.8 %select_add_fusion.2 = f32[3,3,3,256,256]{4,3,2,1,0:T(8,128)} fusion(f32[3,3,3,256,256]{4,3,2,1,0:T(8,128)} %get-tuple-element.1035, pred[]{:T(512)S(6)} %compare.26, pred[]{:T(512)S(6)} %and.78, bf16[256,1,3,2,64]{0,4,3,2,1:T(8,128)(2,1)S(1)} %dynamic-slice_bitcast_fusion.2, bf16[256,1,1,2,64]{0,4,3,2,1:T(8,128)(2,1)} %bitcast.308), kind=kOutput, calls=%fused_computation.37.clone.1 | convolution fusion | flops 304152576 | bytes 14417922 | tf_op jit(solution)/shard_map/while/body/eval_jaxpr/transpose | solution.py:59
  284.0 2.8 collective-permute-start.7
  287.8 2.1 collective-permute-done.7
  291.5 5.6 %collective-permute-start.6 = (bf16[256,1,2,64]{0,3,2,1:T(8,128)(2,1)}, bf16[256,1,2,64]{0,3,2,1:T(8,128)(2,1)S(1)}, u32[]{:S(2)}, u32[]{:S(2)}) collective-permute-start(bf16[256,1,2,64]{0,3,2,1:T(8,128)(2,1)} %fusion.90), channel_id=1, source_target_pairs={{0,1},{1,2},{2,3},{3,4},{4,5},{5,6},{6,7},{8,9},{9,10},{10,11},{11... | collective-permute-start | bytes 196616 | tf_op jit(solution)/shard_map/while/body/eval_jaxpr/ppermute | solution.py:14
  300.1 8.8 %select_add_fusion.2 = f32[3,3,3,256,256]{4,3,2,1,0:T(8,128)} fusion(f32[3,3,3,256,256]{4,3,2,1,0:T(8,128)} %get-tuple-element.1035, pred[]{:T(512)S(6)} %compare.26, pred[]{:T(512)S(6)} %and.78, bf16[256,1,3,2,64]{0,4,3,2,1:T(8,128)(2,1)S(1)} %dynamic-slice_bitcast_fusion.2, bf16[256,1,1,2,64]{0,4,3,2,1:T(8,128)(2,1)} %bitcast.308), kind=kOutput, calls=%fused_computation.37.clone.1 | convolution fusion | flops 304152576 | bytes 14417922 | tf_op jit(solution)/shard_map/while/body/eval_jaxpr/transpose | solution.py:59
  315.6 3.4 collective-permute-start.7
  319.3 2.2 collective-permute-done.7
  323.2 42.9 %all-reduce.1 = (f32[]{:T(128)}, f32[256,3]{0,1:T(4,128)}) all-reduce(f32[]{:T(128)S(6)} %select_n.311, f32[256,3]{0,1:T(4,128)S(1)} %fusion.48), channel_id=1, replica_groups=mesh['section'=4,'slab'=8] {'section','slab'}, use_global_device_ids=true, to_apply=%region_3.4 | all-reduce | flops 769 | bytes 6152 | tf_op jit(solution)/shard_map/psum | solution.py:167
  366.7 112.0 %all-reduce.5.cloned.1.call-done = (f32[1,3,3,3,256,256]{5,4,3,2,1,0:T(8,128)}, f32[1,256,256]{2,1,0:T(8,128)}) async-done(((f32[1,3,3,3,256,256]{5,4,3,2,1,0:T(8,128)}, f32[1,256,256]{2,1,0:T(8,128)}), (f32[1,3,3,3,256,256]{5,4,3,2,1,0:T(8,128)}, f32[1,256,256]{2,1,0:T(8,128)})) %all-reduce.5.cloned.1.call-update) | async-done | bytes 7340048 | tf_op jit(solution)/shard_map/psum | solution.py:212
  478.8 6.8 %copy.128 = f32[1,3,3,3,256,256]{5,4,3,2,1,0:T(8,128)} copy(f32[1,3,3,3,256,256]{5,4,3,2,1,0:T(8,128)} %get-tuple-element.1073) | data formatting | bytes 14155776
  (386 shorter events, 133.9 us)
Async XLA Ops:
  7.2 471.6 %all-reduce.5.cloned.1.call-start = ((), (), s32[]{:S(2)}) async-start(), calls=%async_computation | async-start | bytes 14680064 | tf_op jit(solution)/shard_map/psum | solution.py:212
  7.2 29.2 %collective-permute-start.11 = (s32[2,1,2,64]{3,2,0,1:T(2,128)}, s32[2,1,2,64]{3,2,0,1:T(2,128)S(1)}, u32[]{:S(2)}, u32[]{:S(2)}) collective-permute-start(s32[2,1,2,64]{3,2,0,1:T(2,128)} %bitcast.327), channel_id=1, source_target_pairs={{1,0},{2,1},{3,2},{4,3},{5,4},{6,5},{7,6},{9,8},{10,9},{11,10},{12... | collective-permute-start | bytes 3080 | tf_op jit(solution)/shard_map/ppermute | solution.py:17
  9.8 26.6 %collective-permute-start.10 = (s32[2,1,2,64]{3,2,0,1:T(2,128)}, s32[2,1,2,64]{3,2,0,1:T(2,128)}, u32[]{:S(2)}, u32[]{:S(2)}) collective-permute-start(s32[2,1,2,64]{3,2,0,1:T(2,128)} %bitcast.328), channel_id=1, source_target_pairs={{0,1},{1,2},{2,3},{3,4},{4,5},{5,6},{6,7},{8,9},{9,10},{10,11},{11... | collective-permute-start | bytes 3080 | tf_op jit(solution)/shard_map/ppermute | solution.py:14
  45.1 7.4 %collective-permute-start.1 = (bf16[256,1,2,64]{0,3,2,1:T(8,128)(2,1)}, bf16[256,1,2,64]{0,3,2,1:T(8,128)(2,1)}, u32[]{:S(2)}, u32[]{:S(2)}) collective-permute-start(bf16[256,1,2,64]{0,3,2,1:T(8,128)(2,1)} %get-tuple-element.930), channel_id=1, source_target_pairs={{0,1},{1,2},{2,3},{3,4},{4,5},{5,6},{6,7},{8,9},{9,10},{10,11},{11... | collective-permute-start | bytes 196616 | tf_op jit(solution)/shard_map/while/body/eval_jaxpr/ppermute | solution.py:14
  47.5 5.9 %collective-permute-start = (bf16[256,1,2,64]{0,3,2,1:T(8,128)(2,1)}, bf16[256,1,2,64]{0,3,2,1:T(8,128)(2,1)}, u32[]{:S(2)}, u32[]{:S(2)}) collective-permute-start(bf16[256,1,2,64]{0,3,2,1:T(8,128)(2,1)} %get-tuple-element.930), channel_id=1, source_target_pairs={{1,0},{2,1},{3,2},{4,3},{5,4},{6,5},{7,6},{9,8},{10,9},{11,10},{12... | collective-permute-start | bytes 196616 | tf_op jit(solution)/shard_map/while/body/eval_jaxpr/ppermute | solution.py:17
  57.5 4.4 collective-permute-start.3
  57.8 7.6 %collective-permute-start.2 = (bf16[256,1,2,64]{0,3,2,1:T(8,128)(2,1)S(1)}, bf16[256,1,2,64]{0,3,2,1:T(8,128)(2,1)S(1)}, u32[]{:S(2)}, u32[]{:S(2)}) collective-permute-start(bf16[256,1,2,64]{0,3,2,1:T(8,128)(2,1)S(1)} %fusion.80), channel_id=1, source_target_pairs={{0,8},{8,16},{16,24},{1,9},{9,17},{17,25},{2,10},{10,18},{18,26},{... | collective-permute-start | bytes 196616 | tf_op jit(solution)/shard_map/while/body/eval_jaxpr/ppermute | solution.py:25
  61.9 3.4 collective-permute-start.4
  68.5 8.7 %collective-permute-start.1 = (bf16[256,1,2,64]{0,3,2,1:T(8,128)(2,1)}, bf16[256,1,2,64]{0,3,2,1:T(8,128)(2,1)}, u32[]{:S(2)}, u32[]{:S(2)}) collective-permute-start(bf16[256,1,2,64]{0,3,2,1:T(8,128)(2,1)} %get-tuple-element.930), channel_id=1, source_target_pairs={{0,1},{1,2},{2,3},{3,4},{4,5},{5,6},{6,7},{8,9},{9,10},{10,11},{11... | collective-permute-start | bytes 196616 | tf_op jit(solution)/shard_map/while/body/eval_jaxpr/ppermute | solution.py:14
  72.8 5.9 %collective-permute-start = (bf16[256,1,2,64]{0,3,2,1:T(8,128)(2,1)}, bf16[256,1,2,64]{0,3,2,1:T(8,128)(2,1)}, u32[]{:S(2)}, u32[]{:S(2)}) collective-permute-start(bf16[256,1,2,64]{0,3,2,1:T(8,128)(2,1)} %get-tuple-element.930), channel_id=1, source_target_pairs={{1,0},{2,1},{3,2},{4,3},{5,4},{6,5},{7,6},{9,8},{10,9},{11,10},{12... | collective-permute-start | bytes 196616 | tf_op jit(solution)/shard_map/while/body/eval_jaxpr/ppermute | solution.py:17
  82.8 4.1 collective-permute-start.3
  82.9 7.2 %collective-permute-start.2 = (bf16[256,1,2,64]{0,3,2,1:T(8,128)(2,1)S(1)}, bf16[256,1,2,64]{0,3,2,1:T(8,128)(2,1)S(1)}, u32[]{:S(2)}, u32[]{:S(2)}) collective-permute-start(bf16[256,1,2,64]{0,3,2,1:T(8,128)(2,1)S(1)} %fusion.80), channel_id=1, source_target_pairs={{0,8},{8,16},{16,24},{1,9},{9,17},{17,25},{2,10},{10,18},{18,26},{... | collective-permute-start | bytes 196616 | tf_op jit(solution)/shard_map/while/body/eval_jaxpr/ppermute | solution.py:25
  93.2 8.6 %collective-permute-start.1 = (bf16[256,1,2,64]{0,3,2,1:T(8,128)(2,1)}, bf16[256,1,2,64]{0,3,2,1:T(8,128)(2,1)}, u32[]{:S(2)}, u32[]{:S(2)}) collective-permute-start(bf16[256,1,2,64]{0,3,2,1:T(8,128)(2,1)} %get-tuple-element.930), channel_id=1, source_target_pairs={{0,1},{1,2},{2,3},{3,4},{4,5},{5,6},{6,7},{8,9},{9,10},{10,11},{11... | collective-permute-start | bytes 196616 | tf_op jit(solution)/shard_map/while/body/eval_jaxpr/ppermute | solution.py:14
  97.4 5.9 %collective-permute-start = (bf16[256,1,2,64]{0,3,2,1:T(8,128)(2,1)}, bf16[256,1,2,64]{0,3,2,1:T(8,128)(2,1)}, u32[]{:S(2)}, u32[]{:S(2)}) collective-permute-start(bf16[256,1,2,64]{0,3,2,1:T(8,128)(2,1)} %get-tuple-element.930), channel_id=1, source_target_pairs={{1,0},{2,1},{3,2},{4,3},{5,4},{6,5},{7,6},{9,8},{10,9},{11,10},{12... | collective-permute-start | bytes 196616 | tf_op jit(solution)/shard_map/while/body/eval_jaxpr/ppermute | solution.py:17
  107.4 3.7 collective-permute-start.3
  107.6 6.7 %collective-permute-start.2 = (bf16[256,1,2,64]{0,3,2,1:T(8,128)(2,1)S(1)}, bf16[256,1,2,64]{0,3,2,1:T(8,128)(2,1)S(1)}, u32[]{:S(2)}, u32[]{:S(2)}) collective-permute-start(bf16[256,1,2,64]{0,3,2,1:T(8,128)(2,1)S(1)} %fusion.80), channel_id=1, source_target_pairs={{0,8},{8,16},{16,24},{1,9},{9,17},{17,25},{2,10},{10,18},{18,26},{... | collective-permute-start | bytes 196616 | tf_op jit(solution)/shard_map/while/body/eval_jaxpr/ppermute | solution.py:25
  111.1 3.2 collective-permute-start.4
  117.5 8.9 %collective-permute-start.1 = (bf16[256,1,2,64]{0,3,2,1:T(8,128)(2,1)}, bf16[256,1,2,64]{0,3,2,1:T(8,128)(2,1)}, u32[]{:S(2)}, u32[]{:S(2)}) collective-permute-start(bf16[256,1,2,64]{0,3,2,1:T(8,128)(2,1)} %get-tuple-element.930), channel_id=1, source_target_pairs={{0,1},{1,2},{2,3},{3,4},{4,5},{5,6},{6,7},{8,9},{9,10},{10,11},{11... | collective-permute-start | bytes 196616 | tf_op jit(solution)/shard_map/while/body/eval_jaxpr/ppermute | solution.py:14
  121.9 5.9 %collective-permute-start = (bf16[256,1,2,64]{0,3,2,1:T(8,128)(2,1)}, bf16[256,1,2,64]{0,3,2,1:T(8,128)(2,1)}, u32[]{:S(2)}, u32[]{:S(2)}) collective-permute-start(bf16[256,1,2,64]{0,3,2,1:T(8,128)(2,1)} %get-tuple-element.930), channel_id=1, source_target_pairs={{1,0},{2,1},{3,2},{4,3},{5,4},{6,5},{7,6},{9,8},{10,9},{11,10},{12... | collective-permute-start | bytes 196616 | tf_op jit(solution)/shard_map/while/body/eval_jaxpr/ppermute | solution.py:17
  131.9 3.8 collective-permute-start.3
  132.2 6.7 %collective-permute-start.2 = (bf16[256,1,2,64]{0,3,2,1:T(8,128)(2,1)S(1)}, bf16[256,1,2,64]{0,3,2,1:T(8,128)(2,1)S(1)}, u32[]{:S(2)}, u32[]{:S(2)}) collective-permute-start(bf16[256,1,2,64]{0,3,2,1:T(8,128)(2,1)S(1)} %fusion.80), channel_id=1, source_target_pairs={{0,8},{8,16},{16,24},{1,9},{9,17},{17,25},{2,10},{10,18},{18,26},{... | collective-permute-start | bytes 196616 | tf_op jit(solution)/shard_map/while/body/eval_jaxpr/ppermute | solution.py:25
  135.7 3.2 collective-permute-start.4
  142.1 8.8 %collective-permute-start.1 = (bf16[256,1,2,64]{0,3,2,1:T(8,128)(2,1)}, bf16[256,1,2,64]{0,3,2,1:T(8,128)(2,1)}, u32[]{:S(2)}, u32[]{:S(2)}) collective-permute-start(bf16[256,1,2,64]{0,3,2,1:T(8,128)(2,1)} %get-tuple-element.930), channel_id=1, source_target_pairs={{0,1},{1,2},{2,3},{3,4},{4,5},{5,6},{6,7},{8,9},{9,10},{10,11},{11... | collective-permute-start | bytes 196616 | tf_op jit(solution)/shard_map/while/body/eval_jaxpr/ppermute | solution.py:14
  146.5 5.9 %collective-permute-start = (bf16[256,1,2,64]{0,3,2,1:T(8,128)(2,1)}, bf16[256,1,2,64]{0,3,2,1:T(8,128)(2,1)}, u32[]{:S(2)}, u32[]{:S(2)}) collective-permute-start(bf16[256,1,2,64]{0,3,2,1:T(8,128)(2,1)} %get-tuple-element.930), channel_id=1, source_target_pairs={{1,0},{2,1},{3,2},{4,3},{5,4},{6,5},{7,6},{9,8},{10,9},{11,10},{12... | collective-permute-start | bytes 196616 | tf_op jit(solution)/shard_map/while/body/eval_jaxpr/ppermute | solution.py:17
  156.5 3.7 collective-permute-start.3
  156.8 6.5 %collective-permute-start.2 = (bf16[256,1,2,64]{0,3,2,1:T(8,128)(2,1)S(1)}, bf16[256,1,2,64]{0,3,2,1:T(8,128)(2,1)S(1)}, u32[]{:S(2)}, u32[]{:S(2)}) collective-permute-start(bf16[256,1,2,64]{0,3,2,1:T(8,128)(2,1)S(1)} %fusion.80), channel_id=1, source_target_pairs={{0,8},{8,16},{16,24},{1,9},{9,17},{17,25},{2,10},{10,18},{18,26},{... | collective-permute-start | bytes 196616 | tf_op jit(solution)/shard_map/while/body/eval_jaxpr/ppermute | solution.py:25
  160.1 3.2 collective-permute-start.4
  168.3 14.2 %collective-permute-start.6 = (bf16[256,1,2,64]{0,3,2,1:T(8,128)(2,1)}, bf16[256,1,2,64]{0,3,2,1:T(8,128)(2,1)S(1)}, u32[]{:S(2)}, u32[]{:S(2)}) collective-permute-start(bf16[256,1,2,64]{0,3,2,1:T(8,128)(2,1)} %fusion.90), channel_id=1, source_target_pairs={{0,1},{1,2},{2,3},{3,4},{4,5},{5,6},{6,7},{8,9},{9,10},{10,11},{11... | collective-permute-start | bytes 196616 | tf_op jit(solution)/shard_map/while/body/eval_jaxpr/ppermute | solution.py:14
  172.9 9.6 %collective-permute-start.5 = (bf16[256,1,2,64]{0,3,2,1:T(8,128)(2,1)}, bf16[256,1,2,64]{0,3,2,1:T(8,128)(2,1)S(1)}, u32[]{:S(2)}, u32[]{:S(2)}) collective-permute-start(bf16[256,1,2,64]{0,3,2,1:T(8,128)(2,1)} %fusion.90), channel_id=1, source_target_pairs={{1,0},{2,1},{3,2},{4,3},{5,4},{6,5},{7,6},{9,8},{10,9},{11,10},{12... | collective-permute-start | bytes 196616 | tf_op jit(solution)/shard_map/while/body/eval_jaxpr/ppermute | solution.py:17
  188.9 5.9 %collective-permute-start.7 = (bf16[256,1,2,64]{0,3,2,1:T(8,128)(2,1)S(1)}, bf16[256,1,2,64]{0,3,2,1:T(8,128)(2,1)S(1)}, u32[]{:S(2)}, u32[]{:S(2)}) collective-permute-start(bf16[256,1,2,64]{0,3,2,1:T(8,128)(2,1)S(1)} %get-tuple-element.950), channel_id=1, source_target_pairs={{8,0},{16,8},{24,16},{9,1},{17,9},{25,17},{10,2},{18,10},{26,18},{... | collective-permute-start | bytes 196616 | tf_op jit(solution)/shard_map/while/body/eval_jaxpr/ppermute | solution.py:25
  196.4 17.8 %collective-permute-start.6 = (bf16[256,1,2,64]{0,3,2,1:T(8,128)(2,1)}, bf16[256,1,2,64]{0,3,2,1:T(8,128)(2,1)S(1)}, u32[]{:S(2)}, u32[]{:S(2)}) collective-permute-start(bf16[256,1,2,64]{0,3,2,1:T(8,128)(2,1)} %fusion.90), channel_id=1, source_target_pairs={{0,1},{1,2},{2,3},{3,4},{4,5},{5,6},{6,7},{8,9},{9,10},{10,11},{11... | collective-permute-start | bytes 196616 | tf_op jit(solution)/shard_map/while/body/eval_jaxpr/ppermute | solution.py:14
  202.4 11.8 %collective-permute-start.5 = (bf16[256,1,2,64]{0,3,2,1:T(8,128)(2,1)}, bf16[256,1,2,64]{0,3,2,1:T(8,128)(2,1)S(1)}, u32[]{:S(2)}, u32[]{:S(2)}) collective-permute-start(bf16[256,1,2,64]{0,3,2,1:T(8,128)(2,1)} %fusion.90), channel_id=1, source_target_pairs={{1,0},{2,1},{3,2},{4,3},{5,4},{6,5},{7,6},{9,8},{10,9},{11,10},{12... | collective-permute-start | bytes 196616 | tf_op jit(solution)/shard_map/while/body/eval_jaxpr/ppermute | solution.py:17
  217.4 3.5 collective-permute-start.8
  220.8 3.7 collective-permute-start.9
  220.8 5.9 %collective-permute-start.7 = (bf16[256,1,2,64]{0,3,2,1:T(8,128)(2,1)S(1)}, bf16[256,1,2,64]{0,3,2,1:T(8,128)(2,1)S(1)}, u32[]{:S(2)}, u32[]{:S(2)}) collective-permute-start(bf16[256,1,2,64]{0,3,2,1:T(8,128)(2,1)S(1)} %get-tuple-element.950), channel_id=1, source_target_pairs={{8,0},{16,8},{24,16},{9,1},{17,9},{25,17},{10,2},{18,10},{26,18},{... | collective-permute-start | bytes 196616 | tf_op jit(solution)/shard_map/while/body/eval_jaxpr/ppermute | solution.py:25
  228.3 17.4 %collective-permute-start.6 = (bf16[256,1,2,64]{0,3,2,1:T(8,128)(2,1)}, bf16[256,1,2,64]{0,3,2,1:T(8,128)(2,1)S(1)}, u32[]{:S(2)}, u32[]{:S(2)}) collective-permute-start(bf16[256,1,2,64]{0,3,2,1:T(8,128)(2,1)} %fusion.90), channel_id=1, source_target_pairs={{0,1},{1,2},{2,3},{3,4},{4,5},{5,6},{6,7},{8,9},{9,10},{10,11},{11... | collective-permute-start | bytes 196616 | tf_op jit(solution)/shard_map/while/body/eval_jaxpr/ppermute | solution.py:14
  234.0 11.8 %collective-permute-start.5 = (bf16[256,1,2,64]{0,3,2,1:T(8,128)(2,1)}, bf16[256,1,2,64]{0,3,2,1:T(8,128)(2,1)S(1)}, u32[]{:S(2)}, u32[]{:S(2)}) collective-permute-start(bf16[256,1,2,64]{0,3,2,1:T(8,128)(2,1)} %fusion.90), channel_id=1, source_target_pairs={{1,0},{2,1},{3,2},{4,3},{5,4},{6,5},{7,6},{9,8},{10,9},{11,10},{12... | collective-permute-start | bytes 196616 | tf_op jit(solution)/shard_map/while/body/eval_jaxpr/ppermute | solution.py:17
  252.1 4.0 collective-permute-start.9
  252.1 5.9 %collective-permute-start.7 = (bf16[256,1,2,64]{0,3,2,1:T(8,128)(2,1)S(1)}, bf16[256,1,2,64]{0,3,2,1:T(8,128)(2,1)S(1)}, u32[]{:S(2)}, u32[]{:S(2)}) collective-permute-start(bf16[256,1,2,64]{0,3,2,1:T(8,128)(2,1)S(1)} %get-tuple-element.950), channel_id=1, source_target_pairs={{8,0},{16,8},{24,16},{9,1},{17,9},{25,17},{10,2},{18,10},{26,18},{... | collective-permute-start | bytes 196616 | tf_op jit(solution)/shard_map/while/body/eval_jaxpr/ppermute | solution.py:25
  259.6 17.7 %collective-permute-start.6 = (bf16[256,1,2,64]{0,3,2,1:T(8,128)(2,1)}, bf16[256,1,2,64]{0,3,2,1:T(8,128)(2,1)S(1)}, u32[]{:S(2)}, u32[]{:S(2)}) collective-permute-start(bf16[256,1,2,64]{0,3,2,1:T(8,128)(2,1)} %fusion.90), channel_id=1, source_target_pairs={{0,1},{1,2},{2,3},{3,4},{4,5},{5,6},{6,7},{8,9},{9,10},{10,11},{11... | collective-permute-start | bytes 196616 | tf_op jit(solution)/shard_map/while/body/eval_jaxpr/ppermute | solution.py:14
  265.6 11.8 %collective-permute-start.5 = (bf16[256,1,2,64]{0,3,2,1:T(8,128)(2,1)}, bf16[256,1,2,64]{0,3,2,1:T(8,128)(2,1)S(1)}, u32[]{:S(2)}, u32[]{:S(2)}) collective-permute-start(bf16[256,1,2,64]{0,3,2,1:T(8,128)(2,1)} %fusion.90), channel_id=1, source_target_pairs={{1,0},{2,1},{3,2},{4,3},{5,4},{6,5},{7,6},{9,8},{10,9},{11,10},{12... | collective-permute-start | bytes 196616 | tf_op jit(solution)/shard_map/while/body/eval_jaxpr/ppermute | solution.py:17
  280.5 3.5 collective-permute-start.8
  284.0 3.8 collective-permute-start.9
  284.0 5.9 %collective-permute-start.7 = (bf16[256,1,2,64]{0,3,2,1:T(8,128)(2,1)S(1)}, bf16[256,1,2,64]{0,3,2,1:T(8,128)(2,1)S(1)}, u32[]{:S(2)}, u32[]{:S(2)}) collective-permute-start(bf16[256,1,2,64]{0,3,2,1:T(8,128)(2,1)S(1)} %get-tuple-element.950), channel_id=1, source_target_pairs={{8,0},{16,8},{24,16},{9,1},{17,9},{25,17},{10,2},{18,10},{26,18},{... | collective-permute-start | bytes 196616 | tf_op jit(solution)/shard_map/while/body/eval_jaxpr/ppermute | solution.py:25
  291.5 17.4 %collective-permute-start.6 = (bf16[256,1,2,64]{0,3,2,1:T(8,128)(2,1)}, bf16[256,1,2,64]{0,3,2,1:T(8,128)(2,1)S(1)}, u32[]{:S(2)}, u32[]{:S(2)}) collective-permute-start(bf16[256,1,2,64]{0,3,2,1:T(8,128)(2,1)} %fusion.90), channel_id=1, source_target_pairs={{0,1},{1,2},{2,3},{3,4},{4,5},{5,6},{6,7},{8,9},{9,10},{10,11},{11... | collective-permute-start | bytes 196616 | tf_op jit(solution)/shard_map/while/body/eval_jaxpr/ppermute | solution.py:14
  297.1 11.8 %collective-permute-start.5 = (bf16[256,1,2,64]{0,3,2,1:T(8,128)(2,1)}, bf16[256,1,2,64]{0,3,2,1:T(8,128)(2,1)S(1)}, u32[]{:S(2)}, u32[]{:S(2)}) collective-permute-start(bf16[256,1,2,64]{0,3,2,1:T(8,128)(2,1)} %fusion.90), channel_id=1, source_target_pairs={{1,0},{2,1},{3,2},{4,3},{5,4},{6,5},{7,6},{9,8},{10,9},{11,10},{12... | collective-permute-start | bytes 196616 | tf_op jit(solution)/shard_map/while/body/eval_jaxpr/ppermute | solution.py:17
  315.3 4.0 collective-permute-start.9
  315.6 5.9 %collective-permute-start.7 = (bf16[256,1,2,64]{0,3,2,1:T(8,128)(2,1)S(1)}, bf16[256,1,2,64]{0,3,2,1:T(8,128)(2,1)S(1)}, u32[]{:S(2)}, u32[]{:S(2)}) collective-permute-start(bf16[256,1,2,64]{0,3,2,1:T(8,128)(2,1)S(1)} %get-tuple-element.950), channel_id=1, source_target_pairs={{8,0},{16,8},{24,16},{9,1},{17,9},{25,17},{10,2},{18,10},{26,18},{... | collective-permute-start | bytes 196616 | tf_op jit(solution)/shard_map/while/body/eval_jaxpr/ppermute | solution.py:25
  (77 other events, 757.2 us)
Sparse Core Ops, SparseCore 0:
  321.6 157.1 all-reduce.4
where the time goes:
time: 500 us; the launch traced here: 494 us
  waiting for transfers between devices  153 us (31%)
  starting transfers between devices  110 us (22%)
  matrix products  71.7 us (14%)
  local copies, waits for them, and re-layouts  54.3 us (11%)
  blocking collectives  42.9 us (9%)
  other arithmetic  32.7 us (7%)
  between operations  28 us (6%)
    psum x1, waiting for transfers between devices, body(): grad_kernel, grad_mixing = lax.psum((loop_state[2], loop_state[3]), 'slab')  112 us
    ppermute x11, starting transfers between devices, extended(): lax.ppermute(lax.slice_in_dim(block, block.shape[dim] - width, None, axis...  50.5 us
    psum x1, blocking collectives, body(): loss_sum, grad_head = lax.psum((loss_part, head_part), ('section', 'slab'))  42.9 us
    transpose x5, matrix products, weight_grad(): return jnp.transpose(result, (2, 3, 4, 0, 1))  42 us
    ppermute x10, starting transfers between devices, from_behind(): return lax.ppermute(x, axis, pairs)  32.9 us
    ppermute x20, waiting for transfers between devices, partner(): return lax.ppermute(block, axis, route)  23.1 us
    ppermute x11, starting transfers between devices, extended(): lax.ppermute(lax.slice_in_dim(block, 0, width, axis=dim), axis, backward)  22.4 us
    dynamic_slice x20, local copies, waits for them, and re-layouts, take_slot(): return lax.dynamic_index_in_dim(buffer, slot_id, 0, keepdims=False)  16.7 us
  transfers between devices with their start and end apart: 53, of which 26 were waited for; matrix products, arithmetic and copies ran while one was open for 17% of the time, Pallas kernels for 0%

commit v1 on v0

v1 whole, which is shorter than its diff:
```python
import functools

import jax
import jax.numpy as jnp
from jax import lax
from jax.experimental import pallas as pl
from jax.experimental.pallas import tpu as pltpu
from jax.sharding import PartitionSpec as P

loss_scale = 1024.0
BF = jnp.bfloat16
F32 = jnp.float32
PAD = 8
VMEM_LIMIT = 56 * 1024 * 1024


class Dims:
    def __init__(self, sections, slabs, micro, channels, depth, rows, cols, offs):
        self.sections, self.half = sections, sections // 2
        self.slabs, self.micro = slabs, micro
        self.C, self.D, self.R, self.W, self.offs = channels, depth, rows, cols, offs
        self.G = depth * rows
        self.parts = slabs // micro
        self.own = cols // self.parts
        self.count = micro * offs * depth * rows * cols

    def fwd(self, t):
        return 2 * (self.sections - 1) - t

    def rows_of(self, k):
        return (self.own + 2 * k) * self.G


def group_mask(dm, kz, ky):
    g = lax.broadcasted_iota(jnp.int32, (1, dm.G, dm.C), 1)
    d = g // dm.R + kz
    r = g % dm.R + ky
    return (d >= 0) & (d < dm.D) & (r >= 0) & (r < dm.R)


def column_mask(dm, base, k, width):
    col = lax.broadcasted_iota(jnp.int32, (width, dm.G, dm.C), 0) + (base - k)
    return (col >= 0) & (col < dm.W)


def spread(dm, xf, x27, width, sign):
    G, C = dm.G, dm.C
    rin = (width + 2) * G
    for kz in range(3):
        for ky in range(3):
            dz, dy = sign * (kz - 1), sign * (ky - 1)
            delta = dz * dm.R + dy
            part = xf[PAD + delta:PAD + delta + rin, :]
            if kz != 1 or ky != 1:
                part = part.reshape(width + 2, G, C)
                part = jnp.where(group_mask(dm, dz, dy), part, 0.0).reshape(rin, C)
            part = part.astype(BF)
            for kx in range(3):
                first = (1 + sign * (kx - 1)) * G
                tap = (kz * 3 + ky) * 3 + kx
                x27[0:width * G, tap * C:(tap + 1) * C] = part[first:first + width * G]


def dot(a, b):
    return lax.dot_general(a, b, (((1,), (0,)), ((), ())), preferred_element_type=F32)


def dot_nt(a, b):
    return lax.dot_general(a, b, (((1,), (1,)), ((), ())), preferred_element_type=F32)


def dot_tn(a, b):
    return lax.dot_general(a, b, (((0,), (0,)), ((), ())), preferred_element_type=F32)


def stage(dm, xf, x, rin):
    xf[PAD:PAD + rin, :] = x.astype(F32)


def preact(dm, t, xf, x27, x_ref, skip_ref, w_ref, b_ref):
    k = dm.fwd(t)
    width = dm.own + 2 * k
    ro, rin = width * dm.G, (width + 2) * dm.G
    stage(dm, xf, x_ref[0:rin, :], rin)
    spread(dm, xf, x27, width, 1)
    branch = x_ref[dm.G:dm.G + ro, :] if t <= dm.half else skip_ref[0:ro, :]
    return dot(x27[0:ro, :], w_ref[...]) + dot(branch, b_ref[...])


def silu_masked(dm, base, k, pre):
    width = dm.own + 2 * k
    value = pre * (1.0 / (1.0 + jnp.exp(-pre)))
    value = value.reshape(width, dm.G, dm.C)
    value = jnp.where(column_mask(dm, base, k, width), value, 0.0)
    return value.reshape(width * dm.G, dm.C).astype(BF)


def pre_gradient(dm, base, k, upstream, pre):
    width = dm.own + 2 * k
    sig = 1.0 / (1.0 + jnp.exp(-pre))
    value = upstream * (sig * (1.0 + pre * (1.0 - sig)))
    value = value.reshape(width, dm.G, dm.C)
    value = jnp.where(column_mask(dm, base, k, width), value, 0.0)
    return value.reshape(width * dm.G, dm.C).astype(BF)


def forward_kernel(dm, t, has_skip_in, has_mirror, *refs):
    refs = list(refs)
    base_ref, x_ref, w_ref, b_ref = refs[:4]
    at = 4
    skip_ref = None
    if has_skip_in:
        skip_ref = refs[at]
        at += 1
    y_ref, pre_ref = refs[at], refs[at + 1]
    at += 2
    if has_mirror:
        mirror_ref = refs[at]
        at += 1
    xf, x27 = refs[at], refs[at + 1]
    base = base_ref[0]
    k = dm.fwd(t)
    pre = preact(dm, t, xf, x27, x_ref, skip_ref, w_ref, b_ref)
    y = silu_masked(dm, base, k, pre)
    y_ref[...] = y
    first = (k - t) * dm.G
    pre_ref[...] = pre[first:first + dm.rows_of(t)]
    if has_mirror:
        keep = dm.fwd(dm.sections - 1 - t)
        first = (k - keep) * dm.G
        mirror_ref[...] = y[first:first + dm.rows_of(keep)]


def back_conv(dm, t, pg, xf, x27, wt_ref, b_ref, msg_ref):
    width = dm.own + 2 * (t - 1)
    stage(dm, xf, pg, dm.rows_of(t))
    spread(dm, xf, x27, width, -1)
    grad = dot(x27[0:width * dm.G, :], wt_ref[...])
    if t <= dm.half:
        grad = grad + dot_nt(pg[dm.G:dm.G + width * dm.G], b_ref[...])
    msg_ref[0:width * dm.G, :] = grad.astype(BF)


def last_kernel(dm, *refs):
    (base_ref, x_ref, w_ref, b_ref, skip_ref, wt_ref, head_ref, head_t_ref, target_ref) = refs[:9]
    msg_ref, pgx_ref, skip_out, xf, x27 = refs[9:]
    t = dm.sections - 1
    base = base_ref[0]
    G, C, own = dm.G, dm.C, dm.own
    ro, mid = dm.rows_of(t), t * G
    pre = preact(dm, t, xf, x27, x_ref, skip_ref, w_ref, b_ref)
    y = silu_masked(dm, base, t, pre)
    logits = dot(y, head_ref[...])
    target = target_ref[...]
    lane = lax.broadcasted_iota(jnp.int32, logits.shape, 1)
    sig = 1.0 / (1.0 + jnp.exp(-logits))
    lg = (loss_scale * (sig - target) / dm.count)
    lg = jnp.where(lane < dm.offs, lg, 0.0).astype(BF)
    own_logits = logits[mid:mid + own * G]
    term = jnp.maximum(own_logits, 0.0) + jnp.log(1.0 + jnp.exp(-jnp.abs(own_logits)))
    term = term - target[mid:mid + own * G] * own_logits
    term = jnp.where(lane[0:own * G] < dm.offs, term, 0.0)
    loss = jnp.sum(jnp.sum(term, axis=0, keepdims=True), axis=1, keepdims=True)
    head_part = dot_tn(lg[mid:mid + own * G], y[mid:mid + own * G])
    row = lax.broadcasted_iota(jnp.int32, (8, C), 0)
    carry = jnp.where(row < dm.offs, head_part[0:8], jnp.where(row == dm.offs, loss, 0.0))
    pieces = []
    for _ in range(3):
        piece = carry.astype(BF).astype(F32)
        pieces.append(piece)
        carry = carry - piece
    carry = jnp.concatenate(pieces + [jnp.zeros((8, C), F32)], axis=0).astype(BF)
    upstream = dot(lg, head_t_ref[...])
    pg = pre_gradient(dm, base, t, upstream, pre)
    pgx_ref[0:own * G, :] = pg[mid:mid + own * G]
    pgx_ref[own * G:own * G + 32, :] = carry
    back_conv(dm, t, pg, xf, x27, wt_ref, b_ref, msg_ref)
    end = dm.rows_of(t - 1)
    msg_ref[end:end + 32, :] = carry
    if t > dm.half:
        m = dm.sections - 1 - t
        first = (t - m) * G
        skip_out[...] = dot_nt(pg[first:first + dm.rows_of(m)], b_ref[...]).astype(BF)


def backward_kernel(dm, t, has_skip_in, *refs):
    refs = list(refs)
    base_ref, down_ref, pre_ref = refs[:3]
    at = 3
    if t > 0:
        wt_ref, b_ref = refs[at:at + 2]
        at += 2
    if has_skip_in:
        skip_ref = refs[at]
        at += 1
    pgx_ref = refs[at]
    at += 1
    if t > 0:
        msg_ref = refs[at]
        at += 1
        if t > dm.half:
            skip_out = refs[at]
            at += 1
        xf, x27 = refs[at:at + 2]
    base = base_ref[0]
    ro = dm.rows_of(t)
    upstream = down_ref[0:ro, :].astype(F32)
    if has_skip_in:
        upstream = upstream + skip_ref[0:ro, :].astype(F32)
    pg = pre_gradient(dm, base, t, upstream, pre_ref[...])
    mid, size = t * dm.G, dm.own * dm.G
    carry = down_ref[ro:ro + 32, :]
    pgx_ref[0:size, :] = pg[mid:mid + size]
    pgx_ref[size:size + 32, :] = carry
    if t > 0:
        back_conv(dm, t, pg, xf, x27, wt_ref, b_ref, msg_ref)
        end = dm.rows_of(t - 1)
        msg_ref[end:end + 32, :] = carry
        if t > dm.half:
            m = dm.sections - 1 - t
            first = (t - m) * dm.G
            skip_out[...] = dot_nt(pg[first:first + dm.rows_of(m)], b_ref[...]).astype(BF)


def turn_kernel(dm, *refs):
    q_ref = refs[0]
    blocks = refs[1:1 + dm.slabs]
    xt_ref, bt_ref = refs[1 + dm.slabs:]
    size = dm.own * dm.G
    for e in range(dm.micro):
        for r in range(dm.parts):
            block = blocks[e * dm.parts + r]
            place = lax.rem(q_ref[0] + (dm.parts - r), dm.parts) + e * dm.parts
            at = pl.multiple_of(place * size, size)
            xt_ref[:, pl.ds(at, size)] = jnp.transpose(block[0:size, :])
            bt_ref[:, pl.ds(at, size)] = jnp.transpose(block[size:2 * size, :])


def weight_kernel(dm, *refs):
    q_ref, xt_ref, bt_ref = refs[:3]
    blocks = refs[3:3 + dm.slabs]
    grad_ref, mix_ref, head_ref, loss_ref, full, part, sums = refs[3 + dm.slabs:]
    G, C, W = dm.G, dm.C, dm.W
    size = dm.own * G
    span = (W + 2) * G
    rows = dm.micro * span
    step = pl.program_id(0)

    @pl.when(step == 0)
    def _():
        total = jnp.zeros((8, C), F32)
        for e in range(dm.micro):
            start = PAD + e * span
            full[start:start + G, :] = jnp.zeros((G, C), F32)
            full[start + (W + 1) * G:start + span, :] = jnp.zeros((G, C), F32)
            for r in range(dm.parts):
                block = blocks[e * dm.parts + r]
                place = lax.rem(q_ref[0] + (dm.parts - r), dm.parts)
                at = pl.multiple_of(start + G + place * size, 8)
                full[pl.ds(at, size), :] = block[0:size, :].astype(F32)
                carry = block[size:size + 32, :].astype(F32)
                slot = lax.rem(q_ref[1] + (dm.micro - e), dm.micro) * dm.parts + place
                sums[slot] = (carry[0:8] + carry[8:16]) + carry[16:24]
        for slot in range(dm.slabs):
            total = total + sums[slot]
        head_ref[...] = total
        loss_ref[...] = total[dm.offs:dm.offs + 1, 0:1] / dm.count

    kz = step // 3 - 1
    ky = step % 3 - 1
    shift = kz * dm.R + ky
    value = pltpu.roll(full[PAD:PAD + rows, :], lax.rem(shift + rows, rows), 0)
    value = value.reshape(dm.micro * (W + 2), G, C)
    value = jnp.where(group_mask(dm, -kz, -ky), value, 0.0)
    part[...] = value.reshape(rows, C).astype(BF)
    xt = xt_ref[...]
    for kx in range(3):
        total = None
        for e in range(dm.micro):
            first = e * span + (2 - kx) * G
            one = dot(xt[:, e * W * G:(e + 1) * W * G], part[first:first + W * G, :])
            total = one if total is None else total + one
        grad_ref[kx] = total

    @pl.when(step == 4)
    def _():
        total = None
        for e in range(dm.micro):
            first = e * span + G
            one = dot(bt_ref[:, e * W * G:(e + 1) * W * G], part[first:first + W * G, :])
            total = one if total is None else total + one
        mix_ref[...] = total


def whole():
    return pl.BlockSpec(memory_space=pltpu.VMEM)


def scalar():
    return pl.BlockSpec(memory_space=pltpu.SMEM)


def shape(rows, cols, kind):
    return jax.ShapeDtypeStruct((rows, cols), kind)


def call(name, kernel, base, operands, outs, scratch, flops):
    moved = sum(a.size * a.dtype.itemsize for a in operands)
    moved += sum(o.shape[0] * o.shape[1] * jnp.dtype(o.dtype).itemsize for o in outs)
    return pl.pallas_call(
        kernel,
        name=name,
        out_shape=outs,
        in_specs=[scalar()] + [whole()] * len(operands),
        out_specs=[whole()] * len(outs),
        scratch_shapes=scratch,
        compiler_params=pltpu.CompilerParams(vmem_limit_bytes=VMEM_LIMIT),
        cost_estimate=pl.CostEstimate(flops=flops, bytes_accessed=moved, transcendentals=0),
    )(base, *operands)


def conv_scratch(dm, rin, ro):
    return [
        pltpu.VMEM((rin + 2 * PAD, dm.C), F32),
        pltpu.VMEM((ro, 27 * dm.C), BF),
    ]


def body(features_in, labels, offsets, conv_weight, branch_weight, head_weight):
    n = lax.axis_size("section")
    slabs = lax.axis_size("slab")
    micro, C, thick, R, W = features_in.shape
    dm = Dims(n, slabs, micro, C, thick * slabs, R, W, offsets.shape[0])
    G, D, own, parts, half = dm.G, dm.D, dm.own, dm.parts, dm.half
    section = lax.axis_index("section")
    slab = lax.axis_index("slab")
    c, q = slab % micro, slab // micro
    base = jnp.reshape(q * own, (1,)).astype(jnp.int32)
    q_arr = jnp.stack([q, c]).astype(jnp.int32)
    size = own * G

    def hop(x, source, target):
        return lax.ppermute(x, "section", [(source, target)])

    def rotate(x, r):
        pairs = [(p * micro + e, ((p + r) % parts) * micro + e) for p in range(parts) for e in range(micro)]
        return lax.ppermute(x, "slab", pairs)

    def swap(x, e):
        pairs = [(p * micro + i, p * micro + (i + e) % micro) for p in range(parts) for i in range(micro)]
        return lax.ppermute(x, "slab", pairs)

    def gather(block):
        found = [[block] + [rotate(block, r) for r in range(1, parts)]]
        for e in range(1, micro):
            found.append([swap(b, e) for b in found[0]])
        return sum(found, [])

    kernel = conv_weight[0].reshape(27 * C, C)
    kernel_t = jnp.swapaxes(conv_weight[0].reshape(27, C, C), 1, 2).reshape(27 * C, C)
    mixing = branch_weight[0]

    wing = dm.fwd(0) + 1
    wide = own + 2 * wing
    cells = jnp.transpose(features_in, (0, 4, 2, 3, 1)).reshape(micro, W, thick * R, C)
    marks = labels.astype(BF).reshape(micro, 1, thick * R, W)
    marks = jnp.pad(marks, ((0, 0), (0, 0), (0, 0), (0, C - W)))
    cells = jnp.concatenate([cells, marks], axis=1)
    pieces = {0: lax.dynamic_index_in_dim(cells, c, 0, keepdims=False)}
    for e in range(1, micro):
        pieces[e] = swap(lax.dynamic_index_in_dim(cells, (c + e) % micro, 0, keepdims=False), e)

    def by_place(found, me, count):
        placed = []
        for p in range(count):
            value = found[0]
            for r in range(1, count):
                value = jnp.where((me + (count - r)) % count == p, found[r], value)
            placed.append(value)
        return placed

    chip = jnp.concatenate(by_place(pieces, c, micro), axis=1)
    padded = jnp.pad(chip[:W], ((wing, wing), (0, 0), (0, 0)))

    def window(place):
        view = lax.dynamic_slice_in_dim(padded, place * own, wide, 0)
        return jnp.concatenate([view, chip[W:]], axis=0)

    found = {0: window(q)}
    for r in range(1, parts):
        found[r] = rotate(window((q + r) % parts), r)
    first = jnp.concatenate(by_place(found, q, parts), axis=1)
    current = first[:wide].reshape(wide * G, C)
    crop = first[wide, :, :W].reshape(D, R, W)

    crop_pad = jnp.pad(crop, 1)
    maps = []
    for channel in range(dm.offs):
        at = 1 + offsets[channel]
        neighbor = lax.dynamic_slice(crop_pad, (at[0], at[1], at[2]), crop.shape)
        maps.append(jnp.where((neighbor == crop) & (crop != 0), 1.0, 0.0).astype(F32))
    targets = jnp.stack(maps, axis=-1)
    targets = jnp.pad(targets, ((0, 0), (0, 0), (n - 1, n - 1), (0, 128 - dm.offs)))
    targets = lax.dynamic_slice_in_dim(targets, q * own, own + 2 * (n - 1), 2)
    targets = jnp.transpose(targets, (2, 0, 1, 3)).reshape(dm.rows_of(n - 1), 128)
    head = jnp.pad(head_weight, ((0, 0), (0, 128 - dm.offs)))
    head_t = jnp.transpose(head)

    own_x, own_b, pres, mirrors = [], [], [], {}
    for t in range(n - 1):
        k = dm.fwd(t)
        begin = (k + 1) * G
        own_x.append(current[begin:begin + size])
        has_skip, has_mirror = t > half, t < half - 1
        operands = [current, kernel, mixing]
        if has_skip:
            skip = mirrors[t]
            operands.append(skip)
            own_b.append(skip[k * G:k * G + size])
        else:
            own_b.append(own_x[-1])
        outs = [shape(dm.rows_of(k), C, BF), shape(dm.rows_of(t), C, F32)]
        if has_mirror:
            outs.append(shape(dm.rows_of(dm.fwd(n - 1 - t)), C, BF))
        results = call(
            f"forward_{t}",
            functools.partial(forward_kernel, dm, t, has_skip, has_mirror),
            base, operands, outs,
            conv_scratch(dm, dm.rows_of(k + 1), dm.rows_of(k)),
            2 * dm.rows_of(k) * 28 * C * C,
        )
        pres.append(results[1])
        current = hop(results[0], t, t + 1)
        if has_mirror:
            later, current = lax.optimization_barrier((results[2], current))
            mirrors[n - 1 - t] = hop(later, t, n - 1 - t)

    t = n - 1
    own_x.append(current[(t + 1) * G:(t + 1) * G + size])
    skip = mirrors.get(t, current[G:G + dm.rows_of(t)])
    own_b.append(skip[t * G:t * G + size])
    outs = [
        shape(dm.rows_of(t - 1) + 32, C, BF),
        shape(size + 32, C, BF),
        shape(dm.rows_of(0), C, BF),
    ]
    results = call(
        "forward_last",
        functools.partial(last_kernel, dm),
        base,
        [current, kernel, mixing, skip, kernel_t, head, head_t, targets],
        outs,
        conv_scratch(dm, dm.rows_of(t + 1), dm.rows_of(t)),
        4 * dm.rows_of(t) * 28 * C * C,
    )
    own_pg = {t: results[1]}
    skip_grads = {0: hop(results[2], t, 0)}
    down = hop(results[0], t, t - 1)

    def mine(values):
        value = values[0]
        for s in range(1, n):
            value = jnp.where(section == s, values[s], value)
        return value

    held = jnp.concatenate([mine(own_x), mine(own_b)], axis=0)
    held, down = lax.optimization_barrier((held, down))
    held = gather(held)
    cells_all = micro * W * G
    xt, bt = call(
        "turn",
        functools.partial(turn_kernel, dm),
        q_arr, held,
        [shape(C, cells_all, BF), shape(C, cells_all, BF)],
        [], 1000,
    )

    for t in range(n - 2, -1, -1):
        has_skip = t < half - 1
        operands = [down, pres[t]]
        if t > 0:
            operands += [kernel_t, mixing]
        if has_skip:
            operands.append(skip_grads[t])
        outs = [shape(size + 32, C, BF)]
        scratch = []
        if t > 0:
            outs.append(shape(dm.rows_of(t - 1) + 32, C, BF))
            if t > half:
                outs.append(shape(dm.rows_of(n - 1 - t), C, BF))
            scratch = conv_scratch(dm, dm.rows_of(t), dm.rows_of(t - 1))
        results = call(
            f"backward_{t}",
            functools.partial(backward_kernel, dm, t, has_skip),
            base, operands, outs, scratch,
            2 * dm.rows_of(max(t - 1, 0)) * 28 * C * C if t > 0 else 1000,
        )
        own_pg[t] = results[0]
        if t > 0:
            down = hop(results[1], t, t - 1)
            if t > half:
                skip_grads[n - 1 - t] = hop(results[2], t, n - 1 - t)

    blocks = gather(mine(own_pg))
    span = (W + 2) * G
    grad, mix, heads, loss = pl.pallas_call(
        functools.partial(weight_kernel, dm),
        name="weights",
        grid=(9,),
        out_shape=[
            jax.ShapeDtypeStruct((27, C, C), F32),
            shape(C, C, F32),
            shape(8, C, F32),
            shape(1, 1, F32),
        ],
        in_specs=[scalar()] + [whole()] * (2 + slabs),
        out_specs=[pl.BlockSpec((3, C, C), lambda i: (i, 0, 0)), whole(), whole(), whole()],
        scratch_shapes=[
            pltpu.VMEM((micro * span + 2 * PAD, C), F32),
            pltpu.VMEM((micro * span, C), BF),
            pltpu.VMEM((slabs, 8, C), F32),
        ],
        compiler_params=pltpu.CompilerParams(vmem_limit_bytes=VMEM_LIMIT),
        cost_estimate=pl.CostEstimate(
            flops=2 * cells_all * 28 * C * C, bytes_accessed=28 * C * C * 4, transcendentals=0
        ),
    )(q_arr, xt, bt, *blocks)
    grad_head = jnp.transpose(heads[:dm.offs])
    return (
        loss[0, 0],
        grad.reshape((1, 3, 3, 3, C, C)),
        mix[None],
        grad_head,
    )


def solution(mesh):
    placed = (
        P(None, None, "slab", None, None),
        P(None, "slab", None, None),
        P(),
        P("section", None, None, None, None, None),
        P("section", None, None),
        P(),
    )
    return jax.shard_map(
        body,
        mesh=mesh,
        in_specs=placed,
        out_specs=(P(), P("section", None, None, None, None, None), P("section", None, None), P()),
        check_vma=False,
    )
```

time: 500 us -> 179 us (0.36)
  waiting for transfers between devices: 153 us -> 38 us
  starting transfers between devices: 110 us -> 36.3 us
  matrix products: 71.7 us -> 0 us
  Pallas kernels: 0 us -> 62.2 us
  blocking collectives: 42.9 us -> 0 us
  local copies, waits for them, and re-layouts: 54.3 us -> 16.8 us
  other arithmetic: 32.7 us -> 6.15 us
  between operations: 28 us -> 18.3 us
    psum x1 -> x0, waiting for transfers between devices: 112 us -> none  [body(): grad_kernel, grad_mixing = lax.psum((loop_state[2], loop_state[3]), 'slab')]
    ppermute x52 -> x26, starting transfers between devices: 110 us -> 36.3 us  [the longest x9 14.5 us: swap(): return lax.ppermute(x, 'slab', pairs)]
    pallas_call x0 -> x9, Pallas kernels: none -> 62.2 us  [the longest x8 36.7 us: call(): pl.pallas_call(kernel, name=name, out_shape=outs, in_specs=[scalar()] + [...]
    psum x1 -> x0, blocking collectives: 42.9 us -> none  [body(): loss_sum, grad_head = lax.psum((loss_part, head_part), ('section', 'slab'))]
    transpose x5 -> x0, matrix products: 42 us -> none  [weight_grad(): return jnp.transpose(result, (2, 3, 4, 0, 1))]
    dot_general x18 -> x0, matrix products: 22.9 us -> none  [the longest x5 9.4 us: forward_step(): jnp.einsum('io,izyx->ozyx', mixing, branch, preferred_element_type=jnp.fl...]
    dynamic_slice x20 -> x3, local copies, waits for them, and re-layouts: 16.7 us -> 0.34 us  [the longest x1 0.26 us: window(): view = lax.dynamic_slice_in_dim(padded, place * own, wide, 0)]
    dynamic_update_slice x25 -> x0, other arithmetic: 13.5 us -> none  [put_slot(): lax.dynamic_update_index_in_dim(buffer, jnp.where(active, value, previous...]
  transfers between devices with their start and end apart: 53 -> 26, of which waited for: 26 -> 7; matrix products, arithmetic and copies ran while one was open for 17% -> 7% of each run, Pallas kernels for 0% -> 5%
where the time goes in v1:
time: 179 us; the launch traced here: 178 us
  Pallas kernels  62.2 us (35%)
  waiting for transfers between devices  38 us (21%)
  starting transfers between devices  36.3 us (20%)
  between operations  18.3 us (10%)
  local copies, waits for them, and re-layouts  16.8 us (9%)
  other arithmetic  6.15 us (3%)
    pallas_call x8, Pallas kernels, call(): pl.pallas_call(kernel, name=name, out_shape=outs, in_specs=[scalar()] + [...  36.7 us
    pallas_call x1, Pallas kernels, body(): pl.pallas_call(functools.partial(weight_kernel, dm), name='weights', grid...  25.5 us
    ppermute x9, waiting for transfers between devices, rotate(): return lax.ppermute(x, 'slab', pairs)  22.8 us
    ppermute x9, starting transfers between devices, swap(): return lax.ppermute(x, 'slab', pairs)  14.5 us
    ppermute x8, waiting for transfers between devices, hop(): return lax.ppermute(x, 'section', [(source, target)])  14.3 us
    ppermute x9, starting transfers between devices, rotate(): return lax.ppermute(x, 'slab', pairs)  11.9 us
    ppermute x8, starting transfers between devices, hop(): return lax.ppermute(x, 'section', [(source, target)])  9.96 us
    unnamed x82, local copies, waits for them, and re-layouts  6.47 us
  transfers between devices with their start and end apart: 26, of which 7 were waited for; matrix products, arithmetic and copies ran while one was open for 7% of the time, Pallas kernels for 5%

profile of v1, /device:TPU:3, one launch (start us, length us, event | category | flops | bytes accessed | tf_op | source)
XLA Modules:
  0.0 177.9 jit_solution(7441883593922478239)
XLA Ops:
  0.7 0.7 convert_element_type.13
  1.4 0.9 fusion.10
  2.4 0.7 collective-permute-start
  3.1 0.9 collective-permute-done
  4.6 1.3 collective-permute-start.3
  6.0 2.4 %collective-permute-start.2 = (bf16[31,4,256]{2,1,0:T(4,128)(2,1)S(1)}, bf16[31,4,256]{2,1,0:T(4,128)(2,1)S(1)}, u32[]{:S(2)}, u32[]{:S(2)}) collective-permute-start(bf16[31,4,256]{2,1,0:T(4,128)(2,1)S(1)} %get-tuple-element.69), channel_id=1, source_target_pairs={{0,4},{1,5},{2,6},{3,7},{4,0},{5,1},{6,2},{7,3},{8,12},{9,13},{10,... | collective-permute-start | bytes 190472 | tf_op jit(solution)/shard_map/ppermute | solution.py:347
  8.4 1.1 collective-permute-start.1
  9.6 3.5 %collective-permute-done.2 = bf16[31,4,256]{2,1,0:T(4,128)(2,1)S(1)} collective-permute-done((bf16[31,4,256]{2,1,0:T(4,128)(2,1)S(1)}, bf16[31,4,256]{2,1,0:T(4,128)(2,1)S(1)}, u32[]{:S(2)}, u32[]{:S(2)}) %collective-permute-start.2) | collective-permute-done | bytes 63520 | tf_op jit(solution)/shard_map/ppermute | solution.py:347
  13.7 0.7 copy-done.1
  14.4 0.7 slice.107
  15.1 4.7 %forward_0.1 = (bf16[448,256]{1,0:T(8,128)(2,1)}, f32[256,256]{1,0:T(8,128)}, bf16[352,256]{1,0:T(8,128)(2,1)}) custom-call(s32[1]{0:T(128)} %bitcast.2.refs_0_, bf16[480,256]{1,0:T(8,128)(2,1)} %bitcast.66, bf16[6912,256]{1,0:T(8,128)(2,1)} %bitcast.55, bf16[256,256]{1,0:T(8,128)(2,1)} %bitcast.60), custom_call_target="tpu_custom_call" | custom-call | flops 1644167168 | bytes 4587520 | tf_op jit(solution)/shard_map/forward_0/pallas_call | solution.py:310
  19.8 1.3 collective-permute-start.4
  24.3 0.7 fusion.16
  33.8 0.7 copy.36
  34.6 3.5 %copy.23 = bf16[27,256,256]{1,2,0:T(8,128)(2,1)} copy(bf16[27,256,256]{2,1,0:T(8,128)(2,1)S(1)} %bitcast.59) | data formatting | bytes 7077888 | tf_op jit(solution)/shard_map/reshape;squeeze | solution.py:360
  43.9 1.5 pad.22.clone.refs_6_
  45.3 4.5 %forward_1.1 = (bf16[416,256]{1,0:T(8,128)(2,1)}, f32[288,256]{1,0:T(8,128)}) custom-call(s32[1]{0:T(128)} %bitcast.2.refs_0_, bf16[448,256]{1,0:T(8,128)(2,1)} %collective-permute-done.4.refs_1_, bf16[6912,256]{1,0:T(8,128)(2,1)} %bitcast.56, bf16[256,256]{1,0:T(8,128)(2,1)} %bitcast.61), custom_call_target="tpu_custom_call" | custom-call | flops 1526726656 | bytes 4407296 | tf_op jit(solution)/shard_map/forward_1/pallas_call | solution.py:310
  49.9 3.1 %collective-permute-start.5 = (bf16[416,256]{1,0:T(8,128)(2,1)}, bf16[416,256]{1,0:T(8,128)(2,1)S(1)}, u32[]{:S(2)}, u32[]{:S(2)}) collective-permute-start(bf16[416,256]{1,0:T(8,128)(2,1)} %get-tuple-element.31), channel_id=1, source_target_pairs={{8,16},{9,17},{10,18},{11,19},{12,20},{13,21},{14,22},{15,23}} | collective-permute-start | bytes 638984 | tf_op jit(solution)/shard_map/ppermute | solution.py:343
  53.7 0.7 collective-permute-start.7
  54.4 2.6 %collective-permute-done.5.refs_1_ = bf16[416,256]{1,0:T(8,128)(2,1)S(1)} collective-permute-done((bf16[416,256]{1,0:T(8,128)(2,1)}, bf16[416,256]{1,0:T(8,128)(2,1)S(1)}, u32[]{:S(2)}, u32[]{:S(2)}) %collective-permute-start.5) | collective-permute-done | bytes 213024 | tf_op jit(solution)/shard_map/ppermute | solution.py:343
  57.0 0.7 copy-done.27
  57.7 4.4 %forward_2.1 = (bf16[384,256]{1,0:T(8,128)(2,1)}, f32[320,256]{1,0:T(8,128)}) custom-call(s32[1]{0:T(128)} %bitcast.2.refs_0_, bf16[416,256]{1,0:T(8,128)(2,1)} %copy-done.27, bf16[6912,256]{1,0:T(8,128)(2,1)} %bitcast.57, bf16[256,256]{1,0:T(8,128)(2,1)} %bitcast.62), custom_call_target="tpu_custom_call" | custom-call | flops 1409286144 | bytes 4407296 | tf_op jit(solution)/shard_map/forward_2/pallas_call | solution.py:310
  63.0 1.1 copy.30
  64.1 0.7 copy-done.25
  64.8 9.5 %forward_last.1 = (bf16[352,256]{1,0:T(8,128)(2,1)}, bf16[288,256]{1,0:T(8,128)(2,1)}, bf16[256,256]{1,0:T(8,128)(2,1)}) custom-call(s32[1]{0:T(128)} %bitcast.2.refs_0_, bf16[384,256]{1,0:T(8,128)(2,1)} %copy-done.26, bf16[6912,256]{1,0:T(8,128)(2,1)} %bitcast.58, bf16[256,256]{1,0:T(8,128)(2,1)} %bitcast.63, bf16[352,256]{1,0:T(8,128)(2,1)} %copy-done.25, ...), custom_call_target="tpu_custom_call" | custom-call | flops 2583691264 | bytes 8355840 | tf_op jit(solution)/shard_map/forward_last/pallas_call | solution.py:310
  74.4 0.8 collective-permute-start.8
  75.2 1.0 slice_select_fusion.2
  76.2 0.9 slice_select_fusion
  77.2 0.7 copy-done.18
  77.9 4.2 %backward_2.1 = (bf16[288,256]{1,0:T(8,128)(2,1)}, bf16[320,256]{1,0:T(8,128)(2,1)}) custom-call(s32[1]{0:T(128)} %bitcast.2.refs_0_, bf16[352,256]{1,0:T(8,128)(2,1)} %copy-done.18, f32[320,256]{1,0:T(8,128)} %get-tuple-element.40.refs_2_, bf16[6912,256]{1,0:T(8,128)(2,1)} %bitcast.53, bf16[256,256]{1,0:T(8,128)(2,1)} %bitcast.64), custom_call_target="tpu_custom_call" | custom-call | flops 1056964608 | bytes 4489216 | tf_op jit(solution)/shard_map/backward_2/pallas_call | solution.py:310
  82.2 1.4 collective-permute-start.16
  83.6 11.7 %collective-permute-done.16.refs_1_ = bf16[320,256]{1,0:T(8,128)(2,1)S(1)} collective-permute-done((bf16[320,256]{1,0:T(8,128)(2,1)}, bf16[320,256]{1,0:T(8,128)(2,1)S(1)}, u32[]{:S(2)}, u32[]{:S(2)}) %collective-permute-start.16) | collective-permute-done | bytes 163872 | tf_op jit(solution)/shard_map/ppermute | solution.py:343
  95.9 4.0 %backward_1.1 = (bf16[288,256]{1,0:T(8,128)(2,1)}, bf16[288,256]{1,0:T(8,128)(2,1)}) custom-call(s32[1]{0:T(128)} %bitcast.2.refs_0_, bf16[320,256]{1,0:T(8,128)(2,1)} %copy-done.19, f32[288,256]{1,0:T(8,128)} %get-tuple-element.43.refs_2_, bf16[6912,256]{1,0:T(8,128)(2,1)} %bitcast.54, bf16[256,256]{1,0:T(8,128)(2,1)} %bitcast.65), custom_call_target="tpu_custom_call" | custom-call | flops 939524096 | bytes 4423680 | tf_op jit(solution)/shard_map/backward_1/pallas_call | solution.py:310
  100.0 1.3 collective-permute-start.17
  102.0 1.2 collective-permute-start.11
  103.2 2.5 %collective-permute-start.10 = (bf16[512,256]{1,0:T(8,128)(2,1)S(1)}, bf16[512,256]{1,0:T(8,128)(2,1)S(1)}, u32[]{:S(2)}, u32[]{:S(2)}) collective-permute-start(bf16[512,256]{1,0:T(8,128)(2,1)S(1)} %pad_maximum_fusion.refs_1_), channel_id=1, source_target_pairs={{0,4},{1,5},{2,6},{3,7},{4,0},{5,1},{6,2},{7,3},{8,12},{9,13},{10,... | collective-permute-start | bytes 786440 | tf_op jit(solution)/shard_map/ppermute | solution.py:347
  105.7 4.5 %collective-permute-start.12 = (bf16[512,256]{1,0:T(8,128)(2,1)S(1)}, bf16[512,256]{1,0:T(8,128)(2,1)S(1)}, u32[]{:S(2)}, u32[]{:S(2)}) collective-permute-start(bf16[512,256]{1,0:T(8,128)(2,1)S(1)} %pad_maximum_fusion.refs_1_), channel_id=1, source_target_pairs={{0,1},{1,0},{2,3},{3,2},{4,5},{5,4},{6,7},{7,6},{8,9},{9,8},{10,11... | collective-permute-start | bytes 786440 | tf_op jit(solution)/shard_map/ppermute | solution.py:351
  110.9 1.9 %backward_0.1 = bf16[288,256]{1,0:T(8,128)(2,1)} custom-call(s32[1]{0:T(128)} %bitcast.2.refs_0_, bf16[288,256]{1,0:T(8,128)(2,1)} %copy-done.23, f32[256,256]{1,0:T(8,128)} %get-tuple-element.46.refs_2_, bf16[256,256]{1,0:T(8,128)(2,1)} %copy-done.24), custom_call_target="tpu_custom_call" | custom-call | flops 1000 | bytes 688128 | tf_op jit(solution)/shard_map/backward_0/pallas_call | solution.py:310
  112.8 0.9 select_select_fusion.refs_3_
  113.8 3.3 %collective-permute-start.21 = (bf16[288,256]{1,0:T(8,128)(2,1)S(1)}, bf16[288,256]{1,0:T(8,128)(2,1)S(1)}, u32[]{:S(2)}, u32[]{:S(2)}) collective-permute-start(bf16[288,256]{1,0:T(8,128)(2,1)S(1)} %select_select_fusion.refs_3_), channel_id=1, source_target_pairs={{0,6},{1,7},{2,0},{3,1},{4,2},{5,3},{6,4},{7,5},{8,14},{9,15},{10,... | collective-permute-start | bytes 442376 | tf_op jit(solution)/shard_map/ppermute | solution.py:347
  117.6 10.0 %collective-permute-done.10.refs_3_ = bf16[512,256]{1,0:T(8,128)(2,1)S(1)} collective-permute-done((bf16[512,256]{1,0:T(8,128)(2,1)S(1)}, bf16[512,256]{1,0:T(8,128)(2,1)S(1)}, u32[]{:S(2)}, u32[]{:S(2)}) %collective-permute-start.10) | collective-permute-done | bytes 262176 | tf_op jit(solution)/shard_map/ppermute | solution.py:347
  127.6 6.9 %collective-permute-start.14 = (bf16[512,256]{1,0:T(8,128)(2,1)S(1)}, bf16[512,256]{1,0:T(8,128)(2,1)S(1)}, u32[]{:S(2)}, u32[]{:S(2)}) collective-permute-start(bf16[512,256]{1,0:T(8,128)(2,1)S(1)} %collective-permute-done.10.refs_3_), channel_id=1, source_target_pairs={{0,1},{1,0},{2,3},{3,2},{4,5},{5,4},{6,7},{7,6},{8,9},{9,8},{10,11... | collective-permute-start | bytes 786440 | tf_op jit(solution)/shard_map/ppermute | solution.py:351
  134.8 9.1 %collective-permute-done.20.refs_5_ = bf16[288,256]{1,0:T(8,128)(2,1)S(1)} collective-permute-done((bf16[288,256]{1,0:T(8,128)(2,1)S(1)}, bf16[288,256]{1,0:T(8,128)(2,1)S(1)}, u32[]{:S(2)}, u32[]{:S(2)}) %collective-permute-start.20) | collective-permute-done | bytes 147488 | tf_op jit(solution)/shard_map/ppermute | solution.py:347
  143.9 0.9 collective-permute-start.22
  146.1 0.7 copy-done.17
  146.9 3.4 %turn.1 = (bf16[256,2048]{1,0:T(8,128)(2,1)}, bf16[256,2048]{1,0:T(8,128)(2,1)}) custom-call(s32[2]{0:T(128)} %pad_add_fusion.refs_0_, bf16[512,256]{1,0:T(8,128)(2,1)} %copy-done.2, bf16[512,256]{1,0:T(8,128)(2,1)} %copy-done.14, bf16[512,256]{1,0:T(8,128)(2,1)} %copy-done.12, bf16[512,256]{1,0:T(8,128)(2,1)} %copy-done.11, bf16[512,256]{1,0:T(8,128)(2,1)} %copy-done.13, ...), custom_call_target="tpu_custom_call" | custom-call | flops 1000 | bytes 4194304 | tf_op jit(solution)/shard_map/turn/pallas_call | solution.py:310
  151.1 25.5 %weights.1 = (f32[27,256,256]{2,1,0:T(8,128)}, f32[256,256]{1,0:T(8,128)}, f32[8,256]{1,0:T(8,128)}, f32[1,1]{1,0:T(1,128)}) custom-call(s32[2]{0:T(128)} %pad_add_fusion.refs_0_, bf16[256,2048]{1,0:T(8,128)(2,1)} %get-tuple-element.36.refs_1_, bf16[256,2048]{1,0:T(8,128)(2,1)} %get-tuple-element.37.refs_2_, bf16[288,256]{1,0:T(8,128)(2,1)} %copy-done.20, ...), custom_call_target="tpu_custom_call" | custom-call | flops 7516192768 | bytes 7340032 | tf_op jit(solution)/shard_map/weights/pallas_call | solution.py:506
  176.6 1.3 slice_bitcast_fusion
  (127 shorter events, 8.5 us)
Async XLA Ops:
  2.4 1.6 collective-permute-start
  4.6 5.0 %collective-permute-start.3 = (bf16[31,4,256]{2,1,0:T(4,128)(2,1)S(1)}, bf16[31,4,256]{2,1,0:T(4,128)(2,1)S(1)}, u32[]{:S(2)}, u32[]{:S(2)}) collective-permute-start(bf16[31,4,256]{2,1,0:T(4,128)(2,1)S(1)} %get-tuple-element.56), channel_id=1, source_target_pairs={{0,2},{1,3},{2,4},{3,5},{4,6},{5,7},{6,0},{7,1},{8,10},{9,11},{10,... | collective-permute-start | bytes 190472 | tf_op jit(solution)/shard_map/ppermute | solution.py:347
  6.0 7.1 %collective-permute-start.2 = (bf16[31,4,256]{2,1,0:T(4,128)(2,1)S(1)}, bf16[31,4,256]{2,1,0:T(4,128)(2,1)S(1)}, u32[]{:S(2)}, u32[]{:S(2)}) collective-permute-start(bf16[31,4,256]{2,1,0:T(4,128)(2,1)S(1)} %get-tuple-element.69), channel_id=1, source_target_pairs={{0,4},{1,5},{2,6},{3,7},{4,0},{5,1},{6,2},{7,3},{8,12},{9,13},{10,... | collective-permute-start | bytes 190472 | tf_op jit(solution)/shard_map/ppermute | solution.py:347
  8.4 4.7 %collective-permute-start.1 = (bf16[31,4,256]{2,1,0:T(4,128)(2,1)S(1)}, bf16[31,4,256]{2,1,0:T(4,128)(2,1)S(1)}, u32[]{:S(2)}, u32[]{:S(2)}) collective-permute-start(bf16[31,4,256]{2,1,0:T(4,128)(2,1)S(1)} %get-tuple-element.70), channel_id=1, source_target_pairs={{0,6},{1,7},{2,0},{3,1},{4,2},{5,3},{6,4},{7,5},{8,14},{9,15},{10,... | collective-permute-start | bytes 190472 | tf_op jit(solution)/shard_map/ppermute | solution.py:347
  13.4 7.6 %copy-start.30 = (s32[3,3]{1,0:T(4,128)S(1)}, s32[3,3]{1,0:T(4,128)}, u32[]{:S(2)}) copy-start(s32[3,3]{1,0:T(4,128)} %param.8) | copy-start | bytes 112
  13.4 20.4 %copy-start.29 = (bf16[256,3]{0,1:T(4,128)(2,1)S(1)}, bf16[256,3]{0,1:T(4,128)(2,1)}, u32[]{:S(2)}) copy-start(bf16[256,3]{0,1:T(4,128)(2,1)} %param.11) | copy-start | bytes 4612
  13.5 21.1 %copy-start = (bf16[1,3,3,3,256,256]{5,4,3,2,1,0:T(8,128)(2,1)S(1)}, bf16[1,3,3,3,256,256]{5,4,3,2,1,0:T(8,128)(2,1)}, u32[]{:S(2)}) copy-start(bf16[1,3,3,3,256,256]{5,4,3,2,1,0:T(8,128)(2,1)} %param.9) | copy-start | bytes 10616836
  19.8 25.5 %collective-permute-start.4 = (bf16[448,256]{1,0:T(8,128)(2,1)}, bf16[448,256]{1,0:T(8,128)(2,1)}, u32[]{:S(2)}, u32[]{:S(2)}) collective-permute-start(bf16[448,256]{1,0:T(8,128)(2,1)} %get-tuple-element.29), channel_id=1, source_target_pairs={{0,8},{1,9},{2,10},{3,11},{4,12},{5,13},{6,14},{7,15}} | collective-permute-start | bytes 688136 | tf_op jit(solution)/shard_map/ppermute | solution.py:343
  38.1 15.5 %copy-start.4 = (bf16[31,4,256]{2,1,0:T(4,128)(2,1)S(1)}, bf16[31,4,256]{2,1,0:T(4,128)(2,1)}, u32[]{:S(2)}) copy-start(bf16[31,4,256]{2,1,0:T(4,128)(2,1)} %copy-done.3) | copy-start | bytes 190468
  38.1 15.5 %copy-start.6 = (bf16[31,4,256]{2,1,0:T(4,128)(2,1)S(1)}, bf16[31,4,256]{2,1,0:T(4,128)(2,1)}, u32[]{:S(2)}) copy-start(bf16[31,4,256]{2,1,0:T(4,128)(2,1)} %copy-done.5) | copy-start | bytes 190468
  38.1 15.5 %copy-start.8 = (bf16[31,4,256]{2,1,0:T(4,128)(2,1)S(1)}, bf16[31,4,256]{2,1,0:T(4,128)(2,1)}, u32[]{:S(2)}) copy-start(bf16[31,4,256]{2,1,0:T(4,128)(2,1)} %copy-done.7) | copy-start | bytes 190468
  38.1 15.5 %copy-start.10 = (bf16[31,4,256]{2,1,0:T(4,128)(2,1)S(1)}, bf16[31,4,256]{2,1,0:T(4,128)(2,1)}, u32[]{:S(2)}) copy-start(bf16[31,4,256]{2,1,0:T(4,128)(2,1)} %copy-done.9) | copy-start | bytes 190468
  38.1 15.6 %copy-start.31 = (bf16[352,256]{1,0:T(8,128)(2,1)S(1)}, bf16[352,256]{1,0:T(8,128)(2,1)}, u32[]{:S(2)}) copy-start(bf16[352,256]{1,0:T(8,128)(2,1)} %get-tuple-element.33) | copy-start | bytes 540676
  49.9 7.1 %collective-permute-start.5 = (bf16[416,256]{1,0:T(8,128)(2,1)}, bf16[416,256]{1,0:T(8,128)(2,1)S(1)}, u32[]{:S(2)}, u32[]{:S(2)}) collective-permute-start(bf16[416,256]{1,0:T(8,128)(2,1)} %get-tuple-element.31), channel_id=1, source_target_pairs={{8,16},{9,17},{10,18},{11,19},{12,20},{13,21},{14,22},{15,23}} | collective-permute-start | bytes 638984 | tf_op jit(solution)/shard_map/ppermute | solution.py:343
  53.7 10.4 %collective-permute-start.7 = (bf16[352,256]{1,0:T(8,128)(2,1)S(1)}, bf16[352,256]{1,0:T(8,128)(2,1)S(1)}, u32[]{:S(2)}, u32[]{:S(2)}) collective-permute-start(bf16[352,256]{1,0:T(8,128)(2,1)S(1)} %copy-done.31), channel_id=1, source_target_pairs={{0,24},{1,25},{2,26},{3,27},{4,28},{5,29},{6,30},{7,31}} | collective-permute-start | bytes 540680 | tf_op jit(solution)/shard_map/ppermute | solution.py:343
  62.1 2.0 %collective-permute-start.6 = (bf16[384,256]{1,0:T(8,128)(2,1)}, bf16[384,256]{1,0:T(8,128)(2,1)S(1)}, u32[]{:S(2)}, u32[]{:S(2)}) collective-permute-start(bf16[384,256]{1,0:T(8,128)(2,1)} %get-tuple-element.32), channel_id=1, source_target_pairs={{16,24},{17,25},{18,26},{19,27},{20,28},{21,29},{22,30},{23,31}} | collective-permute-start | bytes 589832 | tf_op jit(solution)/shard_map/ppermute | solution.py:343
  64.8 10.4 %slice-start = ((bf16[31,16,256]{2,1,0:T(8,128)(2,1)}), bf16[16,16,256]{2,1,0:T(8,128)(2,1)S(1)}, s32[]{:S(2)}) async-start(bf16[31,16,256]{2,1,0:T(8,128)(2,1)} %copy-done.1), calls=%async_computation | async-start | bytes 262144 | tf_op jit(solution)/shard_map/slice | solution.py:413
  64.8 10.4 %copy-start.28 = (bf16[416,256]{1,0:T(8,128)(2,1)S(1)}, bf16[416,256]{1,0:T(8,128)(2,1)}, u32[]{:S(2)}) copy-start(bf16[416,256]{1,0:T(8,128)(2,1)} %copy-done.27) | copy-start | bytes 638980
  74.4 2.8 %collective-permute-start.8 = (bf16[352,256]{1,0:T(8,128)(2,1)}, bf16[352,256]{1,0:T(8,128)(2,1)S(1)}, u32[]{:S(2)}, u32[]{:S(2)}) collective-permute-start(bf16[352,256]{1,0:T(8,128)(2,1)} %get-tuple-element.34), channel_id=1, source_target_pairs={{24,16},{25,17},{26,18},{27,19},{28,20},{29,21},{30,22},{31,23}} | collective-permute-start | bytes 540680 | tf_op jit(solution)/shard_map/ppermute | solution.py:343
  77.2 33.0 %copy-start.2 = (bf16[512,256]{1,0:T(8,128)(2,1)}, bf16[512,256]{1,0:T(8,128)(2,1)S(1)}, u32[]{:S(2)}) copy-start(bf16[512,256]{1,0:T(8,128)(2,1)S(1)} %pad_maximum_fusion.refs_1_) | copy-start | bytes 786436
  77.9 23.4 %copy-start.39 = (bf16[256,256]{1,0:T(8,128)(2,1)S(1)}, bf16[256,256]{1,0:T(8,128)(2,1)}, u32[]{:S(2)}) copy-start(bf16[256,256]{1,0:T(8,128)(2,1)} %get-tuple-element.47) | copy-start | bytes 393220
  77.9 34.9 %copy-start.21 = (bf16[288,256]{1,0:T(8,128)(2,1)S(1)}, bf16[288,256]{1,0:T(8,128)(2,1)}, u32[]{:S(2)}) copy-start(bf16[288,256]{1,0:T(8,128)(2,1)} %get-tuple-element.38) | copy-start | bytes 442372
  82.2 30.6 %copy-start.22 = (bf16[288,256]{1,0:T(8,128)(2,1)S(1)}, bf16[288,256]{1,0:T(8,128)(2,1)}, u32[]{:S(2)}) copy-start(bf16[288,256]{1,0:T(8,128)(2,1)} %get-tuple-element.41) | copy-start | bytes 442372
  82.2 13.1 %collective-permute-start.16 = (bf16[320,256]{1,0:T(8,128)(2,1)}, bf16[320,256]{1,0:T(8,128)(2,1)S(1)}, u32[]{:S(2)}, u32[]{:S(2)}) collective-permute-start(bf16[320,256]{1,0:T(8,128)(2,1)} %get-tuple-element.42), channel_id=1, source_target_pairs={{16,8},{17,9},{18,10},{19,11},{20,12},{21,13},{22,14},{23,15}} | collective-permute-start | bytes 491528 | tf_op jit(solution)/shard_map/ppermute | solution.py:343
  100.0 10.3 %collective-permute-start.17 = (bf16[288,256]{1,0:T(8,128)(2,1)}, bf16[288,256]{1,0:T(8,128)(2,1)S(1)}, u32[]{:S(2)}, u32[]{:S(2)}) collective-permute-start(bf16[288,256]{1,0:T(8,128)(2,1)} %get-tuple-element.45), channel_id=1, source_target_pairs={{8,0},{9,1},{10,2},{11,3},{12,4},{13,5},{14,6},{15,7}} | collective-permute-start | bytes 442376 | tf_op jit(solution)/shard_map/ppermute | solution.py:343
  101.3 8.9 %collective-permute-start.18 = (bf16[256,256]{1,0:T(8,128)(2,1)S(1)}, bf16[256,256]{1,0:T(8,128)(2,1)S(1)}, u32[]{:S(2)}, u32[]{:S(2)}) collective-permute-start(bf16[256,256]{1,0:T(8,128)(2,1)S(1)} %copy-done.39), channel_id=1, source_target_pairs={{24,0},{25,1},{26,2},{27,3},{28,4},{29,5},{30,6},{31,7}} | collective-permute-start | bytes 393224 | tf_op jit(solution)/shard_map/ppermute | solution.py:343
  102.0 15.1 %collective-permute-start.11 = (bf16[512,256]{1,0:T(8,128)(2,1)S(1)}, bf16[512,256]{1,0:T(8,128)(2,1)S(1)}, u32[]{:S(2)}, u32[]{:S(2)}) collective-permute-start(bf16[512,256]{1,0:T(8,128)(2,1)S(1)} %pad_maximum_fusion.refs_1_), channel_id=1, source_target_pairs={{0,6},{1,7},{2,0},{3,1},{4,2},{5,3},{6,4},{7,5},{8,14},{9,15},{10,... | collective-permute-start | bytes 786440 | tf_op jit(solution)/shard_map/ppermute | solution.py:347
  103.2 24.4 %collective-permute-start.10 = (bf16[512,256]{1,0:T(8,128)(2,1)S(1)}, bf16[512,256]{1,0:T(8,128)(2,1)S(1)}, u32[]{:S(2)}, u32[]{:S(2)}) collective-permute-start(bf16[512,256]{1,0:T(8,128)(2,1)S(1)} %pad_maximum_fusion.refs_1_), channel_id=1, source_target_pairs={{0,4},{1,5},{2,6},{3,7},{4,0},{5,1},{6,2},{7,3},{8,12},{9,13},{10,... | collective-permute-start | bytes 786440 | tf_op jit(solution)/shard_map/ppermute | solution.py:347
  105.7 28.9 %collective-permute-start.12 = (bf16[512,256]{1,0:T(8,128)(2,1)S(1)}, bf16[512,256]{1,0:T(8,128)(2,1)S(1)}, u32[]{:S(2)}, u32[]{:S(2)}) collective-permute-start(bf16[512,256]{1,0:T(8,128)(2,1)S(1)} %pad_maximum_fusion.refs_1_), channel_id=1, source_target_pairs={{0,1},{1,0},{2,3},{3,2},{4,5},{5,4},{6,7},{7,6},{8,9},{9,8},{10,11... | collective-permute-start | bytes 786440 | tf_op jit(solution)/shard_map/ppermute | solution.py:351
  110.2 24.4 %collective-permute-start.9 = (bf16[512,256]{1,0:T(8,128)(2,1)S(1)}, bf16[512,256]{1,0:T(8,128)(2,1)S(1)}, u32[]{:S(2)}, u32[]{:S(2)}) collective-permute-start(bf16[512,256]{1,0:T(8,128)(2,1)S(1)} %pad_maximum_fusion.refs_1_), channel_id=1, source_target_pairs={{0,2},{1,3},{2,4},{3,5},{4,6},{5,7},{6,0},{7,1},{8,10},{9,11},{10,... | collective-permute-start | bytes 786440 | tf_op jit(solution)/shard_map/ppermute | solution.py:347
  113.7 36.6 %copy-start.20 = (bf16[288,256]{1,0:T(8,128)(2,1)}, bf16[288,256]{1,0:T(8,128)(2,1)S(1)}, u32[]{:S(2)}) copy-start(bf16[288,256]{1,0:T(8,128)(2,1)S(1)} %select_select_fusion.refs_3_) | copy-start | bytes 442372
  113.8 20.9 %collective-permute-start.21 = (bf16[288,256]{1,0:T(8,128)(2,1)S(1)}, bf16[288,256]{1,0:T(8,128)(2,1)S(1)}, u32[]{:S(2)}, u32[]{:S(2)}) collective-permute-start(bf16[288,256]{1,0:T(8,128)(2,1)S(1)} %select_select_fusion.refs_3_), channel_id=1, source_target_pairs={{0,6},{1,7},{2,0},{3,1},{4,2},{5,3},{6,4},{7,5},{8,14},{9,15},{10,... | collective-permute-start | bytes 442376 | tf_op jit(solution)/shard_map/ppermute | solution.py:347
  117.0 29.0 %copy-start.11 = (bf16[512,256]{1,0:T(8,128)(2,1)}, bf16[512,256]{1,0:T(8,128)(2,1)S(1)}, u32[]{:S(2)}) copy-start(bf16[512,256]{1,0:T(8,128)(2,1)S(1)} %collective-permute-done.11.refs_4_) | copy-start | bytes 786436
  117.1 27.9 %collective-permute-start.15 = (bf16[512,256]{1,0:T(8,128)(2,1)S(1)}, bf16[512,256]{1,0:T(8,128)(2,1)S(1)}, u32[]{:S(2)}, u32[]{:S(2)}) collective-permute-start(bf16[512,256]{1,0:T(8,128)(2,1)S(1)} %collective-permute-done.11.refs_4_), channel_id=1, source_target_pairs={{0,1},{1,0},{2,3},{3,2},{4,5},{5,4},{6,7},{7,6},{8,9},{9,8},{10,11... | collective-permute-start | bytes 786440 | tf_op jit(solution)/shard_map/ppermute | solution.py:351
  127.6 18.5 %copy-start.12 = (bf16[512,256]{1,0:T(8,128)(2,1)}, bf16[512,256]{1,0:T(8,128)(2,1)S(1)}, u32[]{:S(2)}) copy-start(bf16[512,256]{1,0:T(8,128)(2,1)S(1)} %collective-permute-done.10.refs_3_) | copy-start | bytes 786436
  127.6 17.8 %collective-permute-start.14 = (bf16[512,256]{1,0:T(8,128)(2,1)S(1)}, bf16[512,256]{1,0:T(8,128)(2,1)S(1)}, u32[]{:S(2)}, u32[]{:S(2)}) collective-permute-start(bf16[512,256]{1,0:T(8,128)(2,1)S(1)} %collective-permute-done.10.refs_3_), channel_id=1, source_target_pairs={{0,1},{1,0},{2,3},{3,2},{4,5},{5,4},{6,7},{7,6},{8,9},{9,8},{10,11... | collective-permute-start | bytes 786440 | tf_op jit(solution)/shard_map/ppermute | solution.py:351
  134.5 11.6 %copy-start.13 = (bf16[512,256]{1,0:T(8,128)(2,1)}, bf16[512,256]{1,0:T(8,128)(2,1)S(1)}, u32[]{:S(2)}) copy-start(bf16[512,256]{1,0:T(8,128)(2,1)S(1)} %collective-permute-done.12.refs_5_) | copy-start | bytes 786436
  134.6 9.4 %collective-permute-start.20 = (bf16[288,256]{1,0:T(8,128)(2,1)S(1)}, bf16[288,256]{1,0:T(8,128)(2,1)S(1)}, u32[]{:S(2)}, u32[]{:S(2)}) collective-permute-start(bf16[288,256]{1,0:T(8,128)(2,1)S(1)} %select_select_fusion.refs_3_), channel_id=1, source_target_pairs={{0,4},{1,5},{2,6},{3,7},{4,0},{5,1},{6,2},{7,3},{8,12},{9,13},{10,... | collective-permute-start | bytes 442376 | tf_op jit(solution)/shard_map/ppermute | solution.py:347
  134.6 11.5 %copy-start.14 = (bf16[512,256]{1,0:T(8,128)(2,1)}, bf16[512,256]{1,0:T(8,128)(2,1)S(1)}, u32[]{:S(2)}) copy-start(bf16[512,256]{1,0:T(8,128)(2,1)S(1)} %collective-permute-done.9.refs_2_) | copy-start | bytes 786436
  134.6 10.3 %collective-permute-start.19 = (bf16[288,256]{1,0:T(8,128)(2,1)S(1)}, bf16[288,256]{1,0:T(8,128)(2,1)S(1)}, u32[]{:S(2)}, u32[]{:S(2)}) collective-permute-start(bf16[288,256]{1,0:T(8,128)(2,1)S(1)} %select_select_fusion.refs_3_), channel_id=1, source_target_pairs={{0,2},{1,3},{2,4},{3,5},{4,6},{5,7},{6,0},{7,1},{8,10},{9,11},{10,... | collective-permute-start | bytes 442376 | tf_op jit(solution)/shard_map/ppermute | solution.py:347
  134.7 15.7 %copy-start.32 = (bf16[288,256]{1,0:T(8,128)(2,1)}, bf16[288,256]{1,0:T(8,128)(2,1)S(1)}, u32[]{:S(2)}) copy-start(bf16[288,256]{1,0:T(8,128)(2,1)S(1)} %collective-permute-done.21.refs_6_) | copy-start | bytes 442372
  134.7 11.4 %collective-permute-start.13 = (bf16[512,256]{1,0:T(8,128)(2,1)S(1)}, bf16[512,256]{1,0:T(8,128)(2,1)S(1)}, u32[]{:S(2)}, u32[]{:S(2)}) collective-permute-start(bf16[512,256]{1,0:T(8,128)(2,1)S(1)} %collective-permute-done.9.refs_2_), channel_id=1, source_target_pairs={{0,1},{1,0},{2,3},{3,2},{4,5},{5,4},{6,7},{7,6},{8,9},{9,8},{10,11... | collective-permute-start | bytes 786440 | tf_op jit(solution)/shard_map/ppermute | solution.py:351
  143.9 6.4 %copy-start.33 = (bf16[288,256]{1,0:T(8,128)(2,1)}, bf16[288,256]{1,0:T(8,128)(2,1)S(1)}, u32[]{:S(2)}) copy-start(bf16[288,256]{1,0:T(8,128)(2,1)S(1)} %collective-permute-done.20.refs_5_) | copy-start | bytes 442372
  143.9 6.3 %collective-permute-start.22 = (bf16[288,256]{1,0:T(8,128)(2,1)S(1)}, bf16[288,256]{1,0:T(8,128)(2,1)S(1)}, u32[]{:S(2)}, u32[]{:S(2)}) collective-permute-start(bf16[288,256]{1,0:T(8,128)(2,1)S(1)} %select_select_fusion.refs_3_), channel_id=1, source_target_pairs={{0,1},{1,0},{2,3},{3,2},{4,5},{5,4},{6,7},{7,6},{8,9},{9,8},{10,11... | collective-permute-start | bytes 442376 | tf_op jit(solution)/shard_map/ppermute | solution.py:351
  144.9 5.5 %copy-start.34 = (bf16[288,256]{1,0:T(8,128)(2,1)}, bf16[288,256]{1,0:T(8,128)(2,1)S(1)}, u32[]{:S(2)}) copy-start(bf16[288,256]{1,0:T(8,128)(2,1)S(1)} %collective-permute-done.19.refs_4_) | copy-start | bytes 442372
  144.9 5.4 %collective-permute-start.25 = (bf16[288,256]{1,0:T(8,128)(2,1)S(1)}, bf16[288,256]{1,0:T(8,128)(2,1)S(1)}, u32[]{:S(2)}, u32[]{:S(2)}) collective-permute-start(bf16[288,256]{1,0:T(8,128)(2,1)S(1)} %collective-permute-done.21.refs_6_), channel_id=1, source_target_pairs={{0,1},{1,0},{2,3},{3,2},{4,5},{5,4},{6,7},{7,6},{8,9},{9,8},{10,11... | collective-permute-start | bytes 442376 | tf_op jit(solution)/shard_map/ppermute | solution.py:351
  145.0 5.3 %collective-permute-start.24 = (bf16[288,256]{1,0:T(8,128)(2,1)S(1)}, bf16[288,256]{1,0:T(8,128)(2,1)S(1)}, u32[]{:S(2)}, u32[]{:S(2)}) collective-permute-start(bf16[288,256]{1,0:T(8,128)(2,1)S(1)} %collective-permute-done.20.refs_5_), channel_id=1, source_target_pairs={{0,1},{1,0},{2,3},{3,2},{4,5},{5,4},{6,7},{7,6},{8,9},{9,8},{10,11... | collective-permute-start | bytes 442376 | tf_op jit(solution)/shard_map/ppermute | solution.py:351
  145.4 4.9 %collective-permute-start.23 = (bf16[288,256]{1,0:T(8,128)(2,1)S(1)}, bf16[288,256]{1,0:T(8,128)(2,1)S(1)}, u32[]{:S(2)}, u32[]{:S(2)}) collective-permute-start(bf16[288,256]{1,0:T(8,128)(2,1)S(1)} %collective-permute-done.19.refs_4_), channel_id=1, source_target_pairs={{0,1},{1,0},{2,3},{3,2},{4,5},{5,4},{6,7},{7,6},{8,9},{9,8},{10,11... | collective-permute-start | bytes 442376 | tf_op jit(solution)/shard_map/ppermute | solution.py:351
  (19 other events, 17.8 us)

commit v2 on v1

v2 whole, which is shorter than its diff:
```python
import functools
import math

import jax
import jax.numpy as jnp
from jax import lax
from jax.experimental import pallas as pl
from jax.experimental.pallas import tpu as pltpu
from jax.sharding import PartitionSpec as P


loss_scale = 1024.0
BF = jnp.bfloat16
F32 = jnp.float32
PAD = 8
SPARE = 6 * 1024 * 1024


class Dims:
    def __init__(self, sections, slabs, micro, channels, depth, rows, cols, offs):
        self.sections, self.half = sections, sections // 2
        self.slabs, self.micro = slabs, micro
        self.C, self.D, self.R, self.W, self.offs = channels, depth, rows, cols, offs
        self.G = depth * rows
        self.parts = slabs // micro
        self.own = cols // self.parts
        self.count = micro * offs * depth * rows * cols

    def fwd(self, t):
        return 2 * (self.sections - 1) - t

    def rows_of(self, k):
        return (self.own + 2 * k) * self.G


def group_mask(dm, kz, ky):
    g = lax.broadcasted_iota(jnp.int32, (1, dm.G, dm.C), 1)
    d = g // dm.R + kz
    r = g % dm.R + ky
    return (d >= 0) & (d < dm.D) & (r >= 0) & (r < dm.R)


def column_mask(dm, base, k, width):
    col = lax.broadcasted_iota(jnp.int32, (width, dm.G, dm.C), 0) + (base - k)
    return (col >= 0) & (col < dm.W)


def spread(dm, xf, x27, width, sign):
    G, C = dm.G, dm.C
    rin = (width + 2) * G
    for kz in range(3):
        for ky in range(3):
            dz, dy = sign * (kz - 1), sign * (ky - 1)
            delta = dz * dm.R + dy
            part = xf[PAD + delta:PAD + delta + rin, :]
            if kz != 1 or ky != 1:
                part = part.reshape(width + 2, G, C)
                part = jnp.where(group_mask(dm, dz, dy), part, 0.0).reshape(rin, C)
            part = part.astype(BF)
            for kx in range(3):
                first = (1 + sign * (kx - 1)) * G
                tap = (kz * 3 + ky) * 3 + kx
                x27[0:width * G, tap * C:(tap + 1) * C] = part[first:first + width * G]


def dot(a, b):
    return lax.dot_general(a, b, (((1,), (0,)), ((), ())), preferred_element_type=F32)


def dot_nt(a, b):
    return lax.dot_general(a, b, (((1,), (1,)), ((), ())), preferred_element_type=F32)


def dot_tn(a, b):
    return lax.dot_general(a, b, (((0,), (0,)), ((), ())), preferred_element_type=F32)


def stage(xf, x, rin):
    xf[PAD:PAD + rin, :] = x.astype(F32)


def preact(dm, t, xf, x27, skip_ref, w_ref, b_ref):
    width = dm.own + 2 * dm.fwd(t)
    ro = width * dm.G
    spread(dm, xf, x27, width, 1)
    if t <= dm.half:
        branch = x27[0:ro, 13 * dm.C:14 * dm.C]
    else:
        branch = skip_ref[0:ro, :]
    return dot(x27[0:ro, :], w_ref[...]) + dot(branch, b_ref[...])


def silu_masked(dm, base, k, pre):
    width = dm.own + 2 * k
    value = pre * (1.0 / (1.0 + jnp.exp(-pre)))
    value = value.reshape(width, dm.G, dm.C)
    value = jnp.where(column_mask(dm, base, k, width), value, 0.0)
    return value.reshape(width * dm.G, dm.C).astype(BF)


def pre_gradient(dm, base, k, upstream, pre):
    width = dm.own + 2 * k
    sig = 1.0 / (1.0 + jnp.exp(-pre))
    value = upstream * (sig * (1.0 + pre * (1.0 - sig)))
    value = value.reshape(width, dm.G, dm.C)
    value = jnp.where(column_mask(dm, base, k, width), value, 0.0)
    return value.reshape(width * dm.G, dm.C).astype(BF)


def forward_kernel(dm, t, has_skip_in, has_mirror, *refs):
    refs = list(refs)
    me_ref, x_ref, w_ref, b_ref = refs[:4]
    at = 4
    skip_ref = kept_ref = None
    if has_skip_in:
        skip_ref = refs[at]
        at += 1
    if t > 0:
        kept_ref = refs[at]
        at += 1
    y_ref, pre_ref, own_ref = refs[at:at + 3]
    at += 3
    if has_mirror:
        mirror_ref = refs[at]
        at += 1
    if t == 0:
        lab_ref = refs[at]
        at += 1
        wide = dm.own + 2 * (dm.fwd(0) + 1)
        lab_ref[...] = x_ref[...].astype(F32)[:, wide, :]
    xf, x27 = refs[at:at + 2]

    @pl.when(me_ref[2] == t)
    def _():
        base = me_ref[0] * dm.own
        k = dm.fwd(t)
        if t == 0:
            gather_cells(dm, x_ref, xf)
        else:
            stage(xf, x_ref[...], dm.rows_of(k + 1))
        size, mid = dm.own * dm.G, (k + 1) * dm.G
        own_ref[...] = xf[PAD + mid:PAD + mid + size, :].astype(BF)
        pre = preact(dm, t, xf, x27, skip_ref, w_ref, b_ref)
        first = (k - t) * dm.G
        pre_ref[...] = pre[first:first + dm.rows_of(t)]
        y = silu_masked(dm, base, k, pre)
        y_ref[...] = y
        if has_mirror:
            keep = dm.fwd(dm.sections - 1 - t)
            first = (k - keep) * dm.G
            mirror_ref[...] = y[first:first + dm.rows_of(keep)]

    if t > 0:
        @pl.when(me_ref[2] != t)
        def _():
            own_ref[...] = kept_ref[...]


def pack_kernel(dm, wing, cols, me_ref, f_ref, l_ref, out_ref, xs, marks):
    C, W, own = dm.C, dm.W, dm.own
    layers = f_ref.shape[0] // dm.micro
    front = -(-wing // 8) * 8
    marks[...] = jnp.zeros(marks.shape, F32)
    marks[0:dm.micro * layers, 0:W] = l_ref[...].astype(F32)
    xs[0:front, :] = jnp.zeros((front, C), F32)
    xs[front + W:, :] = jnp.zeros((xs.shape[0] - front - W, C), F32)
    row = lax.broadcasted_iota(jnp.int32, (cols, C), 0)
    for e in range(dm.micro):
        for layer in range(layers):
            at = e * layers + layer
            xs[front:front + W, :] = f_ref[at].astype(F32)
            mark = marks[at:at + 1, :]
            for p in range(dm.parts):
                start = front + p * own - wing
                value = jnp.where(row == own + 2 * wing, mark, xs[start:start + cols, :])
                first = ((p * dm.micro + e) * layers + layer) * cols
                out_ref[first:first + cols, :] = value.astype(BF)


def gather_cells(dm, x_ref, xf):
    rows = (dm.own + 2 * (dm.fwd(0) + 1)) * dm.G
    cells = jnp.transpose(x_ref[...].astype(F32), (1, 0, 2))
    cells = cells.reshape(cells.shape[0] * dm.G, dm.C)
    xf[PAD:PAD + rows, :] = cells[0:rows]


def load_kernel(chunks, w_ref, b_ref, out_ref, out_b_ref, sems):
    rows = w_ref.shape[0] // chunks
    copies = []
    for i in range(chunks):
        part = pl.ds(i * rows, rows)
        copies.append(pltpu.make_async_copy(w_ref.at[part], out_ref.at[part], sems.at[i]))
        copies[i].start()
    copies.append(pltpu.make_async_copy(b_ref, out_b_ref, sems.at[chunks]))
    copies[chunks].start()
    for copy in copies:
        copy.wait()


def flip_kernel(C, w_ref, out_ref):
    for tap in range(27):
        out_ref[tap * C:(tap + 1) * C, :] = jnp.transpose(w_ref[tap * C:(tap + 1) * C, :])


def back_conv(dm, t, pg, xf, x27, wt_ref, b_ref, msg_ref):
    width = dm.own + 2 * (t - 1)
    stage(xf, pg, dm.rows_of(t))
    spread(dm, xf, x27, width, -1)
    grad = dot(x27[0:width * dm.G, :], wt_ref[...])
    if t <= dm.half:
        grad = grad + dot_nt(pg[dm.G:dm.G + width * dm.G], b_ref[...])
    msg_ref[0:width * dm.G, :] = grad.astype(BF)


def flat_labels(dm, base, width, lab_ref):
    G, cells = dm.G, width * dm.G
    lanes = dm.C
    cell = lax.broadcasted_iota(jnp.int32, (lanes, cells), 1)
    row = lax.broadcasted_iota(jnp.int32, (lanes, cells), 0)
    pick = jnp.where((cell // G + base == row) & (row < dm.W), 1.0, 0.0).astype(BF)
    found = dot(lab_ref[...].astype(BF), pick)
    g = lax.broadcasted_iota(jnp.int32, (G, cells), 1) % G
    row = lax.broadcasted_iota(jnp.int32, (G, cells), 0)
    line = jnp.sum(jnp.where(g == row, found, 0.0), axis=0, keepdims=True)
    return jnp.broadcast_to(line, (8, cells))


def affinity(dm, width, lab, off_ref):
    G, cells = dm.G, width * dm.G
    total = lab.shape[1]
    mid = lab[:, G:G + cells]
    row = lax.broadcasted_iota(jnp.int32, (8, cells), 0)
    g = lax.broadcasted_iota(jnp.int32, (8, cells), 1) % G
    d, r = g // dm.R, g % dm.R
    target = jnp.zeros((8, cells), F32)
    for j in range(dm.offs):
        dz, dy, dx = off_ref[j, 0], off_ref[j, 1], off_ref[j, 2]
        shift = G + dx * G + dz * dm.R + dy
        near = pltpu.roll(lab, lax.rem(2 * total - shift, total), 1)[:, 0:cells]
        inside = (d + dz >= 0) & (d + dz < dm.D) & (r + dy >= 0) & (r + dy < dm.R)
        same = inside & (near == mid) & (mid != 0.0) & (row == j)
        target = jnp.where(same, 1.0, target)
    return target


def last_kernel(dm, *refs):
    (me_ref, off_ref, x_ref, w_ref, b_ref, skip_ref, kept_ref, wt_ref, head_ref, lab_ref) = refs[:10]
    msg_ref, pgx_ref, skip_out, own_ref, xf, x27 = refs[10:]
    t = dm.sections - 1

    @pl.when(me_ref[2] == t)
    def _():
        base = me_ref[0] * dm.own
        G, C, own = dm.G, dm.C, dm.own
        mid, size = t * G, own * G
        own_ref[...] = x_ref[mid + G:mid + G + size, :]
        stage(xf, x_ref[...], dm.rows_of(t + 1))
        pre = preact(dm, t, xf, x27, skip_ref, w_ref, b_ref)
        y = silu_masked(dm, base, t, pre)
        logits = dot_nt(head_ref[...], y)
        lab = flat_labels(dm, base - t - 1, own + 2 * t + 2, lab_ref)
        target = affinity(dm, own + 2 * t, lab, off_ref)
        live = lax.broadcasted_iota(jnp.int32, logits.shape, 0) < dm.offs
        sig = 1.0 / (1.0 + jnp.exp(-logits))
        lg = jnp.where(live, loss_scale * (sig - target) / dm.count, 0.0).astype(BF)
        term = jnp.maximum(logits, 0.0) + jnp.log(1.0 + jnp.exp(-jnp.abs(logits))) - target * logits
        term = jnp.where(live, term, 0.0)[:, mid:mid + size]
        loss = jnp.sum(jnp.sum(term, axis=1, keepdims=True), axis=0, keepdims=True)
        head_part = dot(lg[:, mid:mid + size], y[mid:mid + size])
        row = lax.broadcasted_iota(jnp.int32, (8, C), 0)
        carry = jnp.where(row < dm.offs, head_part, jnp.where(row == dm.offs, loss, 0.0))
        pieces = []
        for _ in range(3):
            piece = carry.astype(BF).astype(F32)
            pieces.append(piece)
            carry = carry - piece
        carry = jnp.concatenate(pieces + [jnp.zeros((8, C), F32)], axis=0).astype(BF)
        upstream = dot_tn(lg, head_ref[...])
        pg = pre_gradient(dm, base, t, upstream, pre)
        pgx_ref[0:size, :] = pg[mid:mid + size]
        pgx_ref[size:size + 32, :] = carry
        back_conv(dm, t, pg, xf, x27, wt_ref, b_ref, msg_ref)
        end = dm.rows_of(t - 1)
        msg_ref[end:end + 32, :] = carry
        m = dm.sections - 1 - t
        first = (t - m) * G
        skip_out[...] = dot_nt(pg[first:first + dm.rows_of(m)], b_ref[...]).astype(BF)

    @pl.when(me_ref[2] != t)
    def _():
        own_ref[...] = kept_ref[...]


def backward_kernel(dm, t, has_skip_in, *refs):
    refs = list(refs)
    me_ref, down_ref, pre_ref, kept_ref = refs[:4]
    at = 4
    if t > 0:
        wt_ref, b_ref = refs[at:at + 2]
        at += 2
    if has_skip_in:
        skip_ref = refs[at]
        at += 1
    pgx_ref = refs[at]
    at += 1
    if t > 0:
        msg_ref = refs[at]
        at += 1
        if t > dm.half:
            skip_out = refs[at]
            at += 1
        xf, x27 = refs[at:at + 2]

    @pl.when(me_ref[2] == t)
    def _():
        base = me_ref[0] * dm.own
        ro = dm.rows_of(t)
        upstream = down_ref[0:ro, :].astype(F32)
        if has_skip_in:
            upstream = upstream + skip_ref[0:ro, :].astype(F32)
        pg = pre_gradient(dm, base, t, upstream, pre_ref[...])
        mid, size = t * dm.G, dm.own * dm.G
        carry = down_ref[ro:ro + 32, :]
        pgx_ref[0:size, :] = pg[mid:mid + size]
        pgx_ref[size:size + 32, :] = carry
        if t > 0:
            back_conv(dm, t, pg, xf, x27, wt_ref, b_ref, msg_ref)
            end = dm.rows_of(t - 1)
            msg_ref[end:end + 32, :] = carry
            if t > dm.half:
                m = dm.sections - 1 - t
                first = (t - m) * dm.G
                skip_out[...] = dot_nt(pg[first:first + dm.rows_of(m)], b_ref[...]).astype(BF)

    @pl.when(me_ref[2] != t)
    def _():
        pgx_ref[...] = kept_ref[...]


def turn_kernel(dm, *refs):
    q_ref = refs[0]
    x_refs = refs[1:1 + dm.slabs]
    b_refs = refs[1 + dm.slabs:1 + 2 * dm.slabs]
    xt_ref, bt_ref, xf = refs[1 + 2 * dm.slabs:]
    C, size = dm.C, dm.own * dm.G
    cells = dm.slabs * size
    for e in range(dm.micro):
        for r in range(dm.parts):
            block = e * dm.parts + r
            place = lax.rem(q_ref[0] + (dm.parts - r), dm.parts) + e * dm.parts
            at = pl.multiple_of(place * size, size)
            xf[pl.ds(PAD + at, size), :] = x_refs[block][...].astype(F32)

            @pl.when(q_ref[2] > dm.half)
            def _():
                bt_ref[:, pl.ds(at, size)] = jnp.transpose(b_refs[block][...])

    for kz in range(3):
        for ky in range(3):
            delta = (kz - 1) * dm.R + ky - 1
            part = xf[PAD + delta:PAD + delta + cells, :]
            if kz != 1 or ky != 1:
                part = part.reshape(cells // dm.G, dm.G, C)
                part = jnp.where(group_mask(dm, kz - 1, ky - 1), part, 0.0).reshape(cells, C)
            tap = kz * 3 + ky
            xt_ref[tap * C:(tap + 1) * C, :] = jnp.transpose(part.astype(BF))


def weight_kernel(dm, *refs):
    q_ref, xt_ref, bt_ref = refs[:3]
    blocks = refs[3:3 + dm.slabs]
    grad_ref, mix_ref, head_ref, loss_ref, full, held, sums, sems = refs[3 + dm.slabs:]
    G, C, W = dm.G, dm.C, dm.W
    size = dm.own * G
    span = (W + 2) * G
    cells = W * G
    for e in range(dm.micro):
        start = e * span
        full[start:start + G, :] = jnp.zeros((G, C), BF)
        full[start + (W + 1) * G:start + span, :] = jnp.zeros((G, C), BF)
        for r in range(dm.parts):
            block = blocks[e * dm.parts + r]
            place = lax.rem(q_ref[0] + (dm.parts - r), dm.parts)
            at = pl.multiple_of(start + G + place * size, 16)
            full[pl.ds(at, size), :] = block[0:size, :]
            carry = block[size:size + 32, :].astype(F32)
            slot = lax.rem(q_ref[1] + (dm.micro - e), dm.micro) * dm.parts + place
            sums[slot] = (carry[0:8] + carry[8:16]) + carry[16:24]

    def product(lhs_ref, row, count, kx):
        total = None
        for e in range(dm.micro):
            first = e * span + (2 - kx) * G
            one = dot(lhs_ref[row:row + count, e * cells:(e + 1) * cells], full[first:first + cells, :])
            total = one if total is None else total + one
        return total

    copies = []
    for step in range(27):
        kx, tap = step // 9, step % 9
        held[step] = product(xt_ref, tap * C, C, kx)
        copies.append(pltpu.make_async_copy(held.at[step], grad_ref.at[tap, kx], sems.at[step]))
        copies[step].start()

    @pl.when(q_ref[2] > dm.half)
    def _():
        mix_ref[...] = product(bt_ref, 0, C, 1)

    @pl.when(q_ref[2] <= dm.half)
    def _():
        mix_ref[...] = held[13]

    total = jnp.zeros((8, C), F32)
    for slot in range(dm.slabs):
        total = total + sums[slot]
    head_ref[...] = total[0:dm.offs]
    loss_ref[...] = total[dm.offs:dm.offs + 1, 0:1] / dm.count
    for copy in copies:
        copy.wait()


def whole():
    return pl.BlockSpec(memory_space=pltpu.VMEM)


def scalar():
    return pl.BlockSpec(memory_space=pltpu.SMEM)


def shape(rows, cols, kind):
    return jax.ShapeDtypeStruct((rows, cols), kind)


def nbytes(arrays):
    return sum(math.prod(a.shape) * jnp.dtype(a.dtype).itemsize for a in arrays)


def call(kernel, scalars, operands, outs, scratch, flops, places=None):
    moved = nbytes(operands) + nbytes(outs)
    room = moved + nbytes([a for a in scratch if a.dtype in (BF, F32)]) + SPARE
    return pl.pallas_call(
        kernel,
        out_shape=outs,
        in_specs=[scalar()] * len(scalars) + [whole()] * len(operands),
        out_specs=places or [whole()] * len(outs),
        scratch_shapes=scratch,
        compiler_params=pltpu.CompilerParams(vmem_limit_bytes=room),
        cost_estimate=pl.CostEstimate(flops=flops, bytes_accessed=moved, transcendentals=0),
    )(*scalars, *operands)


def conv_scratch(dm, rin, ro):
    return [
        pltpu.VMEM((rin + 2 * PAD, dm.C), F32),
        pltpu.VMEM((ro, 27 * dm.C), BF),
    ]


def body(features_in, labels, offsets, conv_weight, branch_weight, head_weight):
    n = lax.axis_size("section")
    slabs = lax.axis_size("slab")
    micro, C, thick, R, W = features_in.shape
    dm = Dims(n, slabs, micro, C, thick * slabs, R, W, offsets.shape[0])
    G, own, parts, half = dm.G, dm.own, dm.parts, dm.half
    section = lax.axis_index("section")
    slab = lax.axis_index("slab")
    c, q = lax.rem(slab, micro), lax.div(slab, micro)
    me = jnp.stack([q, c, section]).astype(jnp.int32)
    size = own * G

    def hop(x, source, target):
        return lax.ppermute(x, "section", [(source, target)])

    def rotate(x, r):
        pairs = [(p * micro + e, ((p + r) % parts) * micro + e) for p in range(parts) for e in range(micro)]
        return lax.ppermute(x, "slab", pairs)

    def swap(x, e):
        pairs = [(p * micro + i, p * micro + (i + e) % micro) for p in range(parts) for i in range(micro)]
        return lax.ppermute(x, "slab", pairs)

    def gather(block, lowest):
        found = [block]
        for r in range(1, parts):
            pairs = [(p * micro + e, (p + r) % parts * micro + e) for p in range(parts) for e in range(micro)]
            found.append(along(block, pairs, lowest))
        blocks = list(found)
        for e in range(1, micro):
            pairs = [(p * micro + i, p * micro + (i + e) % micro) for p in range(parts) for i in range(micro)]
            blocks += [along(b, pairs, lowest) for b in found]
        return blocks

    def along(x, pairs, lowest):
        joint = [(s * slabs + i, s * slabs + j) for s in range(lowest, n) for i, j in pairs]
        return lax.ppermute(x, ("section", "slab"), joint)

    source = conv_weight[0].reshape(27 * C, C)
    held_hbm = pl.BlockSpec(memory_space=pltpu.HBM)
    kernel, mixing = pl.pallas_call(
        functools.partial(load_kernel, 9),
        name="load",
        out_shape=[shape(27 * C, C, BF), shape(C, C, BF)],
        in_specs=[held_hbm, held_hbm],
        out_specs=[whole(), whole()],
        scratch_shapes=[pltpu.SemaphoreType.DMA((10,))],
        compiler_params=pltpu.CompilerParams(vmem_limit_bytes=27 * C * C * 2 + SPARE),
        cost_estimate=pl.CostEstimate(flops=0, bytes_accessed=27 * C * C * 4, transcendentals=0),
    )(source, branch_weight[0])

    wing = dm.fwd(0) + 1
    wide = own + 2 * wing
    cols = -(-(wide + 1) // 16) * 16
    cells = jnp.transpose(features_in, (0, 2, 3, 4, 1)).reshape(micro * thick * R, W, C)
    front = -(-wing // 8) * 8
    packs = call(
        functools.partial(pack_kernel, dm, wing, cols),
        [me], [cells, labels.reshape(micro * thick * R, W)],
        [shape(slabs * thick * R * cols, C, BF)],
        [
            pltpu.VMEM((front + W + cols, C), F32),
            pltpu.VMEM((-(-micro * thick * R // 8) * 8, C), F32),
        ],
        1000,
    )[0].reshape(slabs, thick * R, cols, C)
    first = lax.all_to_all(packs, "slab", 0, 0, tiled=True).reshape(G, cols, C)
    current = first

    head = jnp.pad(jnp.transpose(head_weight), ((0, 8 - dm.offs), (0, 0)))

    pres, mirrors = [], {}
    kept = kernel_t = None
    for t in range(n - 1):
        k = dm.fwd(t)
        has_skip, has_mirror = t > half, t < half - 1
        operands = [current, kernel, mixing]
        if has_skip:
            operands.append(mirrors[t])
        if t > 0:
            operands.append(kept)
        outs = [shape(dm.rows_of(k), C, BF), shape(dm.rows_of(t), C, F32), shape(size, C, BF)]
        scratch = conv_scratch(dm, dm.rows_of(k + 1), dm.rows_of(k))
        if has_mirror:
            outs.append(shape(dm.rows_of(dm.fwd(n - 1 - t)), C, BF))
        if t == 0:
            outs.append(shape(G, C, F32))
        results = call(
            functools.partial(forward_kernel, dm, t, has_skip, has_mirror),
            [me], operands, outs, scratch,
            2 * dm.rows_of(k) * 28 * C * C,
        )
        pres.append(results[1])
        kept = results[2]
        current = hop(results[0], t, t + 1)
        if t == 0:
            marks = results[-1]
            raw, _ = lax.optimization_barrier((kernel, results[0]))
            kernel_t = call(
                functools.partial(flip_kernel, C), [], [raw],
                [shape(27 * C, C, BF)], [], 2 * 27 * C * C * 100,
            )[0]
        if has_mirror:
            later, current = lax.optimization_barrier((results[3], current))
            mirrors[n - 1 - t] = hop(later, t, n - 1 - t)

    t = n - 1
    skip = mirrors[t]
    branch = skip[t * G:t * G + size]
    for s in range(half + 1, n - 1):
        first = dm.fwd(s) * G
        branch = jnp.where(section == s, mirrors[s][first:first + size], branch)
    branch, _ = lax.optimization_barrier((branch, results[0]))
    branches = gather(branch, half + 1)
    outs = [
        shape(dm.rows_of(t - 1) + 32, C, BF),
        shape(size + 32, C, BF),
        shape(dm.rows_of(0), C, BF),
        shape(size, C, BF),
    ]
    results = call(
        functools.partial(last_kernel, dm),
        [me, offsets],
        [current, kernel, mixing, skip, kept, kernel_t, head, marks],
        outs,
        conv_scratch(dm, dm.rows_of(t + 1), dm.rows_of(t)),
        4 * dm.rows_of(t) * 28 * C * C,
    )
    down = hop(results[0], t, t - 1)
    block, held = results[1], results[3]
    skip_grads = {0: hop(results[2], t, 0)}
    held = gather(held, 0)
    cells_all = micro * W * G

    for t in range(n - 2, -1, -1):
        has_skip = t < half - 1
        operands = [down, pres[t], block]
        if t > 0:
            operands += [kernel_t, mixing]
        if has_skip:
            operands.append(skip_grads[t])
        outs = [shape(size + 32, C, BF)]
        scratch = []
        if t > 0:
            outs.append(shape(dm.rows_of(t - 1) + 32, C, BF))
            if t > half:
                outs.append(shape(dm.rows_of(n - 1 - t), C, BF))
            scratch = conv_scratch(dm, dm.rows_of(t), dm.rows_of(t - 1))
        results = call(
            functools.partial(backward_kernel, dm, t, has_skip),
            [me], operands, outs, scratch,
            2 * dm.rows_of(max(t - 1, 0)) * 28 * C * C if t > 0 else 1000,
        )
        block = results[0]
        if t > 0:
            down = hop(results[1], t, t - 1)
            if t > half:
                skip_grads[n - 1 - t] = hop(results[2], t, n - 1 - t)

    held[0], _ = lax.optimization_barrier((held[0], block))
    xt, bt = call(
        functools.partial(turn_kernel, dm),
        [me], held + branches,
        [shape(9 * C, cells_all, BF), shape(C, cells_all, BF)],
        [pltpu.VMEM((cells_all + 2 * PAD, C), F32)],
        2 * 10 * cells_all * C * 100,
    )
    near = [block] + [rotate(block, r) for r in range(1, parts)]
    *far, xt = lax.optimization_barrier((*near[1:], xt))
    near = [block] + far
    blocks = list(near)
    for e in range(1, micro):
        blocks += [swap(b, e) for b in near]
    operands = [xt, bt, *blocks]
    scratch = [
        pltpu.VMEM((micro * (W + 2) * G, C), BF),
        pltpu.VMEM((27, C, C), F32),
        pltpu.VMEM((slabs, 8, C), F32),
        pltpu.SemaphoreType.DMA((27,)),
    ]
    outs = [
        jax.ShapeDtypeStruct((9, 3, C, C), F32),
        shape(C, C, F32),
        shape(dm.offs, C, F32),
        shape(1, 1, F32),
    ]
    moved = nbytes(operands) + nbytes(outs)
    grad, mix, heads, loss = pl.pallas_call(
        functools.partial(weight_kernel, dm),
        name="weights",
        out_shape=outs,
        in_specs=[scalar()] + [whole()] * len(operands),
        out_specs=[pl.BlockSpec(memory_space=pl.ANY), whole(), whole(), whole()],
        scratch_shapes=scratch,
        compiler_params=pltpu.CompilerParams(
            vmem_limit_bytes=nbytes(operands) + nbytes(scratch[:3]) + SPARE
        ),
        cost_estimate=pl.CostEstimate(
            flops=2 * cells_all * 28 * C * C, bytes_accessed=moved, transcendentals=0
        ),
    )(me, *operands)
    return (
        loss[0, 0],
        grad.reshape((1, 3, 3, 3, C, C)),
        mix[None],
        jnp.transpose(heads),
    )


def solution(mesh):
    placed = (
        P(None, None, "slab", None, None),
        P(None, "slab", None, None),
        P(),
        P("section", None, None, None, None, None),
        P("section", None, None),
        P(),
    )
    return jax.shard_map(
        body,
        mesh=mesh,
        in_specs=placed,
        out_specs=(P(), P("section", None, None, None, None, None), P("section", None, None), P()),
        check_vma=False,
    )
```

time: 179 us -> 116 us (0.65)
  the two profiles are of different devices: /device:TPU:3 before, /device:TPU:7 now
where the time goes in v2:
time: 116 us; the launch traced here: 115 us
  starting transfers between devices  45.7 us (39%)
  waiting for transfers between devices  33.4 us (29%)
  Pallas kernels  28.5 us (25%)
  local copies, waits for them, and re-layouts  6.08 us (5%)
  between operations  1.18 us (1%)
    ppermute x14, starting transfers between devices, along(): return lax.ppermute(x, ('section', 'slab'), joint)  27.1 us
    ppermute x8, waiting for transfers between devices, hop(): return lax.ppermute(x, 'section', [(source, target)])  18 us
    pallas_call x10, Pallas kernels, call(): pl.pallas_call(kernel, out_shape=outs, in_specs=[scalar()] * len(scalars)...  16.5 us
    pallas_call x1, Pallas kernels, body(): pl.pallas_call(functools.partial(weight_kernel, dm), name='weights', out_...  10 us
    ppermute x8, starting transfers between devices, hop(): return lax.ppermute(x, 'section', [(source, target)])  7.86 us
    ppermute x3, waiting for transfers between devices, rotate(): return lax.ppermute(x, 'slab', pairs)  6.28 us
    unnamed x18, local copies, waits for them, and re-layouts  6.06 us
    all_to_all x1, starting transfers between devices, body(): first = lax.all_to_all(packs, 'slab', 0, 0, tiled=True).reshape(G, cols, C)  5.55 us
  transfers between devices with their start and end apart: 30, of which 9 were waited for; matrix products, arithmetic and copies ran while one was open for 0% of the time, Pallas kernels for 8%

profile of v2, /device:TPU:7, one launch (start us, length us, event | category | flops | bytes accessed | tf_op | source)
XLA Modules:
  0.0 114.9 jit_solution(7960449918757534667)
XLA Ops:
  0.7 0.9 copy-done.5
  1.6 0.7 copy-done.6
  2.3 1.3 %shard_map.93 = bf16[512,256]{1,0:T(8,128)(2,1)} custom-call(s32[3]{0:T(128)S(1)} %pad_add_fusion.me_ref.refs_0_, bf16[4,64,256]{2,1,0:T(8,128)(2,1)S(1)} %bitcast.18, s32[4,64]{1,0:T(4,128)S(1)} %bitcast.19), custom_call_target="tpu_custom_call" | custom-call | flops 1000 | bytes 394240 | tf_op jit(solution)/shard_map/pallas_call | solution.py:441
  3.6 5.5 %all-to-all-start = ((bf16[8,2,32,256]{3,2,1,0:T(8,128)(2,1)}), bf16[8,2,32,256]{3,2,1,0:T(8,128)(2,1)}, u32[]{:S(2)}, u32[]{:S(2)}) async-start(bf16[8,2,32,256]{3,2,1,0:T(8,128)(2,1)} %bitcast.6), calls=%async_computation | async-start | bytes 524288 | tf_op jit(solution)/shard_map/all_to_all | solution.py:525
  9.2 2.0 %copy-done = bf16[1,3,3,3,256,256]{5,4,3,2,1,0:T(8,128)(2,1)S(1)} copy-done((bf16[1,3,3,3,256,256]{5,4,3,2,1,0:T(8,128)(2,1)S(1)}, bf16[1,3,3,3,256,256]{5,4,3,2,1,0:T(8,128)(2,1)}, u32[]{:S(2)}) %copy-start) | copy-done | bytes 3538968
  11.2 0.9 copy-done.4
  12.1 1.9 %load.1 = (bf16[6912,256]{1,0:T(8,128)(2,1)S(1)}, bf16[256,256]{1,0:T(8,128)(2,1)S(1)}) custom-call(bf16[6912,256]{1,0:T(8,128)(2,1)S(1)} %bitcast.16, bf16[256,256]{1,0:T(8,128)(2,1)S(1)} %bitcast.17), custom_call_target="tpu_custom_call" | custom-call | bytes 7077888 | tf_op jit(solution)/shard_map/load/pallas_call | solution.py:499
  14.0 0.6 copy-done.1
  14.7 3.3 %all-to-all-done = bf16[8,2,32,256]{3,2,1,0:T(8,128)(2,1)} async-done(((bf16[8,2,32,256]{3,2,1,0:T(8,128)(2,1)}), bf16[8,2,32,256]{3,2,1,0:T(8,128)(2,1)}, u32[]{:S(2)}, u32[]{:S(2)}) %all-to-all-start) | async-done | bytes 262176 | tf_op jit(solution)/shard_map/all_to_all | solution.py:525
  17.9 0.9 copy-done.2
  18.8 1.0 shard_map.94
  19.8 0.7 collective-permute-start
  20.5 0.6 shard_map.95
  21.1 0.7 collective-permute-start.1
  21.8 0.6 shard_map.96
  22.4 1.3 %collective-permute-start.2 = (bf16[384,256]{1,0:T(8,128)(2,1)S(1)}, bf16[384,256]{1,0:T(8,128)(2,1)S(1)}, u32[]{:S(2)}, u32[]{:S(2)}) collective-permute-start(bf16[384,256]{1,0:T(8,128)(2,1)S(1)} %get-tuple-element.48), channel_id=1, source_target_pairs={{16,24},{17,25},{18,26},{19,27},{20,28},{21,29},{22,30},{23,31}} | collective-permute-start | bytes 589832 | tf_op jit(solution)/shard_map/ppermute | solution.py:472
  23.7 1.3 %collective-permute-start.3 = (bf16[352,256]{1,0:T(8,128)(2,1)S(1)}, bf16[352,256]{1,0:T(8,128)(2,1)S(1)}, u32[]{:S(2)}, u32[]{:S(2)}) collective-permute-start(bf16[352,256]{1,0:T(8,128)(2,1)S(1)} %get-tuple-element.49), channel_id=1, source_target_pairs={{0,24},{1,25},{2,26},{3,27},{4,28},{5,29},{6,30},{7,31}} | collective-permute-start | bytes 540680 | tf_op jit(solution)/shard_map/ppermute | solution.py:472
  25.0 1.0 shard_map.97.refs_7_.refs_4_
  26.0 7.9 %collective-permute-done.3.refs_5_ = bf16[352,256]{1,0:T(8,128)(2,1)S(1)} collective-permute-done((bf16[352,256]{1,0:T(8,128)(2,1)S(1)}, bf16[352,256]{1,0:T(8,128)(2,1)S(1)}, u32[]{:S(2)}, u32[]{:S(2)}) %collective-permute-start.3) | collective-permute-done | bytes 180256 | tf_op jit(solution)/shard_map/ppermute | solution.py:472
  33.9 9.4 %collective-permute-done.2.refs_2_ = bf16[384,256]{1,0:T(8,128)(2,1)S(1)} collective-permute-done((bf16[384,256]{1,0:T(8,128)(2,1)S(1)}, bf16[384,256]{1,0:T(8,128)(2,1)S(1)}, u32[]{:S(2)}, u32[]{:S(2)}) %collective-permute-start.2) | collective-permute-done | bytes 196640 | tf_op jit(solution)/shard_map/ppermute | solution.py:472
  43.3 6.2 %shard_map.98 = (bf16[352,256]{1,0:T(8,128)(2,1)S(1)}, bf16[288,256]{1,0:T(8,128)(2,1)S(1)}, bf16[256,256]{1,0:T(8,128)(2,1)S(1)}, bf16[256,256]{1,0:T(8,128)(2,1)S(1)}) custom-call(s32[3]{0:T(128)S(1)} %pad_add_fusion.me_ref.refs_0_, s32[3,3]{1,0:T(4,128)S(1)} %copy-done.7, bf16[384,256]{1,0:T(8,128)(2,1)S(1)} %collective-permute-done.2.refs_2_, ...), custom_call_target="tpu_custom_call" | custom-call | flops 2583691264 | bytes 8327168 | tf_op jit(solution)/shard_map/pallas_call | solution.py:441
  49.5 1.3 %collective-permute-start.4 = (bf16[352,256]{1,0:T(8,128)(2,1)S(1)}, bf16[352,256]{1,0:T(8,128)(2,1)S(1)}, u32[]{:S(2)}, u32[]{:S(2)}) collective-permute-start(bf16[352,256]{1,0:T(8,128)(2,1)S(1)} %get-tuple-element.53), channel_id=1, source_target_pairs={{24,16},{25,17},{26,18},{27,19},{28,20},{29,21},{30,22},{31,23}} | collective-permute-start | bytes 540680 | tf_op jit(solution)/shard_map/ppermute | solution.py:472
  50.8 5.1 %collective-permute-start.20 = (bf16[256,256]{1,0:T(8,128)(2,1)S(1)}, bf16[256,256]{1,0:T(8,128)(2,1)S(1)}, u32[]{:S(2)}, u32[]{:S(2)}) collective-permute-start(bf16[256,256]{1,0:T(8,128)(2,1)S(1)} %slice.4.refs_9_), channel_id=1, source_target_pairs={{24,30},{25,31},{26,24},{27,25},{28,26},{29,27},{30,28},{31,29}} | collective-permute-start | bytes 393224 | tf_op jit(solution)/shard_map/ppermute | solution.py:495
  55.9 0.6 shard_map.99
  56.5 0.7 collective-permute-start.5
  57.2 1.9 %collective-permute-start.19 = (bf16[256,256]{1,0:T(8,128)(2,1)S(1)}, bf16[256,256]{1,0:T(8,128)(2,1)S(1)}, u32[]{:S(2)}, u32[]{:S(2)}) collective-permute-start(bf16[256,256]{1,0:T(8,128)(2,1)S(1)} %slice.4.refs_9_), channel_id=1, source_target_pairs={{24,28},{25,29},{26,30},{27,31},{28,24},{29,25},{30,26},{31,27}} | collective-permute-start | bytes 393224 | tf_op jit(solution)/shard_map/ppermute | solution.py:495
  59.1 4.6 %collective-permute-start.21 = (bf16[256,256]{1,0:T(8,128)(2,1)S(1)}, bf16[256,256]{1,0:T(8,128)(2,1)S(1)}, u32[]{:S(2)}, u32[]{:S(2)}) collective-permute-start(bf16[256,256]{1,0:T(8,128)(2,1)S(1)} %slice.4.refs_9_), channel_id=1, source_target_pairs={{24,25},{25,24},{26,27},{27,26},{28,29},{29,28},{30,31},{31,30}} | collective-permute-start | bytes 393224 | tf_op jit(solution)/shard_map/ppermute | solution.py:495
  63.7 3.2 %collective-permute-start.18 = (bf16[256,256]{1,0:T(8,128)(2,1)S(1)}, bf16[256,256]{1,0:T(8,128)(2,1)S(1)}, u32[]{:S(2)}, u32[]{:S(2)}) collective-permute-start(bf16[256,256]{1,0:T(8,128)(2,1)S(1)} %slice.4.refs_9_), channel_id=1, source_target_pairs={{24,26},{25,27},{26,28},{27,29},{28,30},{29,31},{30,24},{31,25}} | collective-permute-start | bytes 393224 | tf_op jit(solution)/shard_map/ppermute | solution.py:495
  66.9 2.2 %collective-permute-start.24 = (bf16[256,256]{1,0:T(8,128)(2,1)S(1)}, bf16[256,256]{1,0:T(8,128)(2,1)S(1)}, u32[]{:S(2)}, u32[]{:S(2)}) collective-permute-start(bf16[256,256]{1,0:T(8,128)(2,1)S(1)} %collective-permute-done.20.refs_12_), channel_id=1, source_target_pairs={{24,25},{25,24},{26,27},{27,26},{28,29},{29,28},{30,31},{31,30}} | collective-permute-start | bytes 393224 | tf_op jit(solution)/shard_map/ppermute | solution.py:495
  69.2 2.1 %collective-permute-start.23 = (bf16[256,256]{1,0:T(8,128)(2,1)S(1)}, bf16[256,256]{1,0:T(8,128)(2,1)S(1)}, u32[]{:S(2)}, u32[]{:S(2)}) collective-permute-start(bf16[256,256]{1,0:T(8,128)(2,1)S(1)} %collective-permute-done.19.refs_11_), channel_id=1, source_target_pairs={{24,25},{25,24},{26,27},{27,26},{28,29},{29,28},{30,31},{31,30}} | collective-permute-start | bytes 393224 | tf_op jit(solution)/shard_map/ppermute | solution.py:495
  71.3 2.0 %collective-permute-start.13 = (bf16[256,256]{1,0:T(8,128)(2,1)S(1)}, bf16[256,256]{1,0:T(8,128)(2,1)S(1)}, u32[]{:S(2)}, u32[]{:S(2)}) collective-permute-start(bf16[256,256]{1,0:T(8,128)(2,1)S(1)} %get-tuple-element.64.refs_1_), channel_id=1, source_target_pairs={{0,6},{1,7},{2,0},{3,1},{4,2},{5,3},{6,4},{7,5},{8,14},{9,15},{10,... | collective-permute-start | bytes 393224 | tf_op jit(solution)/shard_map/ppermute | solution.py:495
  73.3 0.8 collective-permute-start.12
  74.2 1.3 %collective-permute-start.7 = (bf16[256,256]{1,0:T(8,128)(2,1)S(1)}, bf16[256,256]{1,0:T(8,128)(2,1)S(1)}, u32[]{:S(2)}, u32[]{:S(2)}) collective-permute-start(bf16[256,256]{1,0:T(8,128)(2,1)S(1)} %get-tuple-element.62), channel_id=1, source_target_pairs={{24,0},{25,1},{26,2},{27,3},{28,4},{29,5},{30,6},{31,7}} | collective-permute-start | bytes 393224 | tf_op jit(solution)/shard_map/ppermute | solution.py:472
  75.4 0.7 shard_map.100
  76.2 0.7 collective-permute-start.6
  77.0 0.7 collective-permute-done.7.refs_4_
  77.7 3.3 %collective-permute-start.22 = (bf16[256,256]{1,0:T(8,128)(2,1)S(1)}, bf16[256,256]{1,0:T(8,128)(2,1)S(1)}, u32[]{:S(2)}, u32[]{:S(2)}) collective-permute-start(bf16[256,256]{1,0:T(8,128)(2,1)S(1)} %collective-permute-done.18.refs_10_), channel_id=1, source_target_pairs={{24,25},{25,24},{26,27},{27,26},{28,29},{29,28},{30,31},{31,30}} | collective-permute-start | bytes 393224 | tf_op jit(solution)/shard_map/ppermute | solution.py:495
  81.1 4.7 %collective-permute-done.12.refs_3_ = bf16[256,256]{1,0:T(8,128)(2,1)S(1)} collective-permute-done((bf16[256,256]{1,0:T(8,128)(2,1)S(1)}, bf16[256,256]{1,0:T(8,128)(2,1)S(1)}, u32[]{:S(2)}, u32[]{:S(2)}) %collective-permute-start.12) | collective-permute-done | bytes 131104 | tf_op jit(solution)/shard_map/ppermute | solution.py:495
  85.9 1.2 %collective-permute-start.17 = (bf16[256,256]{1,0:T(8,128)(2,1)S(1)}, bf16[256,256]{1,0:T(8,128)(2,1)S(1)}, u32[]{:S(2)}, u32[]{:S(2)}) collective-permute-start(bf16[256,256]{1,0:T(8,128)(2,1)S(1)} %collective-permute-done.13.refs_4_), channel_id=1, source_target_pairs={{0,1},{1,0},{2,3},{3,2},{4,5},{5,4},{6,7},{7,6},{8,9},{9,8},{10,11... | collective-permute-start | bytes 393224 | tf_op jit(solution)/shard_map/ppermute | solution.py:495
  87.5 0.6 shard_map.101.refs_3_
  88.2 0.8 collective-permute-start.9
  89.0 1.4 %collective-permute-start.8 = (bf16[288,256]{1,0:T(8,128)(2,1)S(1)}, bf16[288,256]{1,0:T(8,128)(2,1)S(1)}, u32[]{:S(2)}, u32[]{:S(2)}) collective-permute-start(bf16[288,256]{1,0:T(8,128)(2,1)S(1)} %shard_map.101.refs_3_), channel_id=1, source_target_pairs={{0,2},{1,3},{2,4},{3,5},{4,6},{5,7},{6,0},{7,1},{8,10},{9,11},{10,... | collective-permute-start | bytes 442376 | tf_op jit(solution)/shard_map/ppermute | solution.py:476
  90.4 1.3 %collective-permute-start.25 = (bf16[288,256]{1,0:T(8,128)(2,1)S(1)}, bf16[288,256]{1,0:T(8,128)(2,1)S(1)}, u32[]{:S(2)}, u32[]{:S(2)}) collective-permute-start(bf16[288,256]{1,0:T(8,128)(2,1)S(1)} %shard_map.101.refs_3_), channel_id=1, source_target_pairs={{0,1},{1,0},{2,3},{3,2},{4,5},{5,4},{6,7},{7,6},{8,9},{9,8},{10,11... | collective-permute-start | bytes 442376 | tf_op jit(solution)/shard_map/ppermute | solution.py:480
  91.7 4.1 %shard_map.102 = (bf16[2304,2048]{1,0:T(8,128)(2,1)S(1)}, bf16[256,2048]{1,0:T(8,128)(2,1)S(1)}) custom-call(s32[3]{0:T(128)S(1)} %pad_add_fusion.me_ref.refs_0_, bf16[256,256]{1,0:T(8,128)(2,1)S(1)} %get-tuple-element.64.refs_1_, bf16[256,256]{1,0:T(8,128)(2,1)S(1)} %collective-permute-done.11.refs_2_, ...), custom_call_target="tpu_custom_call" | custom-call | flops 1048576000 | bytes 12582912 | tf_op jit(solution)/shard_map/pallas_call | solution.py:441
  95.8 6.3 %collective-permute-done.9.refs_5_ = bf16[288,256]{1,0:T(8,128)(2,1)S(1)} collective-permute-done((bf16[288,256]{1,0:T(8,128)(2,1)S(1)}, bf16[288,256]{1,0:T(8,128)(2,1)S(1)}, u32[]{:S(2)}, u32[]{:S(2)}) %collective-permute-start.9) | collective-permute-done | bytes 147488 | tf_op jit(solution)/shard_map/ppermute | solution.py:476
  102.1 1.1 collective-permute-start.26
  103.2 0.5 collective-permute-start.28
  104.8 10.0 %weights.1 = (f32[9,3,256,256]{3,2,1,0:T(8,128)}, f32[256,256]{1,0:T(8,128)}, f32[3,256]{1,0:T(4,128)}, f32[1,1]{1,0:T(1,128)}) custom-call(s32[3]{0:T(128)S(1)} %pad_add_fusion.me_ref.refs_0_, bf16[2304,2048]{1,0:T(8,128)(2,1)S(1)} %get-tuple-element.67.refs_1_, bf16[256,2048]{1,0:T(8,128)(2,1)S(1)} %get-tuple-element.68.refs_2_, ...), custom_call_target="tpu_custom_call" | custom-call | flops 7516192768 | bytes 19008516 | tf_op jit(solution)/shard_map/weights/pallas_call | solution.py:646
  (45 shorter events, 2.0 us)
Async XLA Ops:
  0.7 0.9 copy-start.5
  1.6 0.7 copy-start.6
  3.6 14.3 %all-to-all-start = ((bf16[8,2,32,256]{3,2,1,0:T(8,128)(2,1)}), bf16[8,2,32,256]{3,2,1,0:T(8,128)(2,1)}, u32[]{:S(2)}, u32[]{:S(2)}) async-start(bf16[8,2,32,256]{3,2,1,0:T(8,128)(2,1)} %bitcast.6), calls=%async_computation | async-start | bytes 524288 | tf_op jit(solution)/shard_map/all_to_all | solution.py:525
  9.2 2.0 %copy-start = (bf16[1,3,3,3,256,256]{5,4,3,2,1,0:T(8,128)(2,1)S(1)}, bf16[1,3,3,3,256,256]{5,4,3,2,1,0:T(8,128)(2,1)}, u32[]{:S(2)}) copy-start(bf16[1,3,3,3,256,256]{5,4,3,2,1,0:T(8,128)(2,1)} %param.9) | copy-start | bytes 10616836
  11.2 0.9 copy-start.4
  14.0 0.7 copy-start.1
  17.9 0.9 copy-start.2
  19.8 0.7 collective-permute-start
  21.1 3.9 %copy-start.8 = (bf16[256,3]{0,1:T(4,128)(2,1)S(1)}, bf16[256,3]{0,1:T(4,128)(2,1)}, u32[]{:S(2)}) copy-start(bf16[256,3]{0,1:T(4,128)(2,1)} %param.11) | copy-start | bytes 4612
  21.1 0.7 collective-permute-start.1
  22.4 20.9 %collective-permute-start.2 = (bf16[384,256]{1,0:T(8,128)(2,1)S(1)}, bf16[384,256]{1,0:T(8,128)(2,1)S(1)}, u32[]{:S(2)}, u32[]{:S(2)}) collective-permute-start(bf16[384,256]{1,0:T(8,128)(2,1)S(1)} %get-tuple-element.48), channel_id=1, source_target_pairs={{16,24},{17,25},{18,26},{19,27},{20,28},{21,29},{22,30},{23,31}} | collective-permute-start | bytes 589832 | tf_op jit(solution)/shard_map/ppermute | solution.py:472
  23.7 10.2 %collective-permute-start.3 = (bf16[352,256]{1,0:T(8,128)(2,1)S(1)}, bf16[352,256]{1,0:T(8,128)(2,1)S(1)}, u32[]{:S(2)}, u32[]{:S(2)}) collective-permute-start(bf16[352,256]{1,0:T(8,128)(2,1)S(1)} %get-tuple-element.49), channel_id=1, source_target_pairs={{0,24},{1,25},{2,26},{3,27},{4,28},{5,29},{6,30},{7,31}} | collective-permute-start | bytes 540680 | tf_op jit(solution)/shard_map/ppermute | solution.py:472
  25.0 18.3 %copy-start.3 = (bf16[256,256]{1,0:T(8,128)(2,1)S(1)}, bf16[256,256]{1,0:T(8,128)(2,1)}, u32[]{:S(2)}) copy-start(bf16[256,256]{1,0:T(8,128)(2,1)} %copy-done.1) | copy-start | bytes 393220
  25.0 18.3 %copy-start.7 = (s32[3,3]{1,0:T(4,128)S(1)}, s32[3,3]{1,0:T(4,128)}, u32[]{:S(2)}) copy-start(s32[3,3]{1,0:T(4,128)} %refs_1_.1) | copy-start | bytes 112
  49.5 6.4 %collective-permute-start.4 = (bf16[352,256]{1,0:T(8,128)(2,1)S(1)}, bf16[352,256]{1,0:T(8,128)(2,1)S(1)}, u32[]{:S(2)}, u32[]{:S(2)}) collective-permute-start(bf16[352,256]{1,0:T(8,128)(2,1)S(1)} %get-tuple-element.53), channel_id=1, source_target_pairs={{24,16},{25,17},{26,18},{27,19},{28,20},{29,21},{30,22},{31,23}} | collective-permute-start | bytes 540680 | tf_op jit(solution)/shard_map/ppermute | solution.py:472
  50.8 16.1 %collective-permute-start.20 = (bf16[256,256]{1,0:T(8,128)(2,1)S(1)}, bf16[256,256]{1,0:T(8,128)(2,1)S(1)}, u32[]{:S(2)}, u32[]{:S(2)}) collective-permute-start(bf16[256,256]{1,0:T(8,128)(2,1)S(1)} %slice.4.refs_9_), channel_id=1, source_target_pairs={{24,30},{25,31},{26,24},{27,25},{28,26},{29,27},{30,28},{31,29}} | collective-permute-start | bytes 393224 | tf_op jit(solution)/shard_map/ppermute | solution.py:495
  56.5 17.6 %collective-permute-start.5 = (bf16[320,256]{1,0:T(8,128)(2,1)S(1)}, bf16[320,256]{1,0:T(8,128)(2,1)S(1)}, u32[]{:S(2)}, u32[]{:S(2)}) collective-permute-start(bf16[320,256]{1,0:T(8,128)(2,1)S(1)} %get-tuple-element.56), channel_id=1, source_target_pairs={{16,8},{17,9},{18,10},{19,11},{20,12},{21,13},{22,14},{23,15}} | collective-permute-start | bytes 491528 | tf_op jit(solution)/shard_map/ppermute | solution.py:472
  57.2 12.0 %collective-permute-start.19 = (bf16[256,256]{1,0:T(8,128)(2,1)S(1)}, bf16[256,256]{1,0:T(8,128)(2,1)S(1)}, u32[]{:S(2)}, u32[]{:S(2)}) collective-permute-start(bf16[256,256]{1,0:T(8,128)(2,1)S(1)} %slice.4.refs_9_), channel_id=1, source_target_pairs={{24,28},{25,29},{26,30},{27,31},{28,24},{29,25},{30,26},{31,27}} | collective-permute-start | bytes 393224 | tf_op jit(solution)/shard_map/ppermute | solution.py:495
  59.1 12.2 %collective-permute-start.21 = (bf16[256,256]{1,0:T(8,128)(2,1)S(1)}, bf16[256,256]{1,0:T(8,128)(2,1)S(1)}, u32[]{:S(2)}, u32[]{:S(2)}) collective-permute-start(bf16[256,256]{1,0:T(8,128)(2,1)S(1)} %slice.4.refs_9_), channel_id=1, source_target_pairs={{24,25},{25,24},{26,27},{27,26},{28,29},{29,28},{30,31},{31,30}} | collective-permute-start | bytes 393224 | tf_op jit(solution)/shard_map/ppermute | solution.py:495
  63.7 9.6 %collective-permute-start.18 = (bf16[256,256]{1,0:T(8,128)(2,1)S(1)}, bf16[256,256]{1,0:T(8,128)(2,1)S(1)}, u32[]{:S(2)}, u32[]{:S(2)}) collective-permute-start(bf16[256,256]{1,0:T(8,128)(2,1)S(1)} %slice.4.refs_9_), channel_id=1, source_target_pairs={{24,26},{25,27},{26,28},{27,29},{28,30},{29,31},{30,24},{31,25}} | collective-permute-start | bytes 393224 | tf_op jit(solution)/shard_map/ppermute | solution.py:495
  66.9 9.3 %collective-permute-start.24 = (bf16[256,256]{1,0:T(8,128)(2,1)S(1)}, bf16[256,256]{1,0:T(8,128)(2,1)S(1)}, u32[]{:S(2)}, u32[]{:S(2)}) collective-permute-start(bf16[256,256]{1,0:T(8,128)(2,1)S(1)} %collective-permute-done.20.refs_12_), channel_id=1, source_target_pairs={{24,25},{25,24},{26,27},{27,26},{28,29},{29,28},{30,31},{31,30}} | collective-permute-start | bytes 393224 | tf_op jit(solution)/shard_map/ppermute | solution.py:495
  69.2 7.7 %collective-permute-start.23 = (bf16[256,256]{1,0:T(8,128)(2,1)S(1)}, bf16[256,256]{1,0:T(8,128)(2,1)S(1)}, u32[]{:S(2)}, u32[]{:S(2)}) collective-permute-start(bf16[256,256]{1,0:T(8,128)(2,1)S(1)} %collective-permute-done.19.refs_11_), channel_id=1, source_target_pairs={{24,25},{25,24},{26,27},{27,26},{28,29},{29,28},{30,31},{31,30}} | collective-permute-start | bytes 393224 | tf_op jit(solution)/shard_map/ppermute | solution.py:495
  71.3 9.7 %collective-permute-start.13 = (bf16[256,256]{1,0:T(8,128)(2,1)S(1)}, bf16[256,256]{1,0:T(8,128)(2,1)S(1)}, u32[]{:S(2)}, u32[]{:S(2)}) collective-permute-start(bf16[256,256]{1,0:T(8,128)(2,1)S(1)} %get-tuple-element.64.refs_1_), channel_id=1, source_target_pairs={{0,6},{1,7},{2,0},{3,1},{4,2},{5,3},{6,4},{7,5},{8,14},{9,15},{10,... | collective-permute-start | bytes 393224 | tf_op jit(solution)/shard_map/ppermute | solution.py:495
  73.3 12.6 %collective-permute-start.12 = (bf16[256,256]{1,0:T(8,128)(2,1)S(1)}, bf16[256,256]{1,0:T(8,128)(2,1)S(1)}, u32[]{:S(2)}, u32[]{:S(2)}) collective-permute-start(bf16[256,256]{1,0:T(8,128)(2,1)S(1)} %get-tuple-element.64.refs_1_), channel_id=1, source_target_pairs={{0,4},{1,5},{2,6},{3,7},{4,0},{5,1},{6,2},{7,3},{8,12},{9,13},{10,... | collective-permute-start | bytes 393224 | tf_op jit(solution)/shard_map/ppermute | solution.py:495
  74.2 3.5 %collective-permute-start.7 = (bf16[256,256]{1,0:T(8,128)(2,1)S(1)}, bf16[256,256]{1,0:T(8,128)(2,1)S(1)}, u32[]{:S(2)}, u32[]{:S(2)}) collective-permute-start(bf16[256,256]{1,0:T(8,128)(2,1)S(1)} %get-tuple-element.62), channel_id=1, source_target_pairs={{24,0},{25,1},{26,2},{27,3},{28,4},{29,5},{30,6},{31,7}} | collective-permute-start | bytes 393224 | tf_op jit(solution)/shard_map/ppermute | solution.py:472
  76.2 10.8 %collective-permute-start.6 = (bf16[288,256]{1,0:T(8,128)(2,1)S(1)}, bf16[288,256]{1,0:T(8,128)(2,1)S(1)}, u32[]{:S(2)}, u32[]{:S(2)}) collective-permute-start(bf16[288,256]{1,0:T(8,128)(2,1)S(1)} %get-tuple-element.59), channel_id=1, source_target_pairs={{8,0},{9,1},{10,2},{11,3},{12,4},{13,5},{14,6},{15,7}} | collective-permute-start | bytes 442376 | tf_op jit(solution)/shard_map/ppermute | solution.py:472
  76.9 10.1 %collective-permute-start.11 = (bf16[256,256]{1,0:T(8,128)(2,1)S(1)}, bf16[256,256]{1,0:T(8,128)(2,1)S(1)}, u32[]{:S(2)}, u32[]{:S(2)}) collective-permute-start(bf16[256,256]{1,0:T(8,128)(2,1)S(1)} %get-tuple-element.64.refs_1_), channel_id=1, source_target_pairs={{0,2},{1,3},{2,4},{3,5},{4,6},{5,7},{6,0},{7,1},{8,10},{9,11},{10,... | collective-permute-start | bytes 393224 | tf_op jit(solution)/shard_map/ppermute | solution.py:495
  77.7 10.4 %collective-permute-start.22 = (bf16[256,256]{1,0:T(8,128)(2,1)S(1)}, bf16[256,256]{1,0:T(8,128)(2,1)S(1)}, u32[]{:S(2)}, u32[]{:S(2)}) collective-permute-start(bf16[256,256]{1,0:T(8,128)(2,1)S(1)} %collective-permute-done.18.refs_10_), channel_id=1, source_target_pairs={{24,25},{25,24},{26,27},{27,26},{28,29},{29,28},{30,31},{31,30}} | collective-permute-start | bytes 393224 | tf_op jit(solution)/shard_map/ppermute | solution.py:495
  81.0 7.1 %collective-permute-start.14 = (bf16[256,256]{1,0:T(8,128)(2,1)S(1)}, bf16[256,256]{1,0:T(8,128)(2,1)S(1)}, u32[]{:S(2)}, u32[]{:S(2)}) collective-permute-start(bf16[256,256]{1,0:T(8,128)(2,1)S(1)} %get-tuple-element.64.refs_1_), channel_id=1, source_target_pairs={{0,1},{1,0},{2,3},{3,2},{4,5},{5,4},{6,7},{7,6},{8,9},{9,8},{10,11... | collective-permute-start | bytes 393224 | tf_op jit(solution)/shard_map/ppermute | solution.py:495
  85.9 3.1 %collective-permute-start.17 = (bf16[256,256]{1,0:T(8,128)(2,1)S(1)}, bf16[256,256]{1,0:T(8,128)(2,1)S(1)}, u32[]{:S(2)}, u32[]{:S(2)}) collective-permute-start(bf16[256,256]{1,0:T(8,128)(2,1)S(1)} %collective-permute-done.13.refs_4_), channel_id=1, source_target_pairs={{0,1},{1,0},{2,3},{3,2},{4,5},{5,4},{6,7},{7,6},{8,9},{9,8},{10,11... | collective-permute-start | bytes 393224 | tf_op jit(solution)/shard_map/ppermute | solution.py:495
  87.0 3.4 %collective-permute-start.16 = (bf16[256,256]{1,0:T(8,128)(2,1)S(1)}, bf16[256,256]{1,0:T(8,128)(2,1)S(1)}, u32[]{:S(2)}, u32[]{:S(2)}) collective-permute-start(bf16[256,256]{1,0:T(8,128)(2,1)S(1)} %collective-permute-done.12.refs_3_), channel_id=1, source_target_pairs={{0,1},{1,0},{2,3},{3,2},{4,5},{5,4},{6,7},{7,6},{8,9},{9,8},{10,11... | collective-permute-start | bytes 393224 | tf_op jit(solution)/shard_map/ppermute | solution.py:495
  87.0 4.7 %collective-permute-start.15 = (bf16[256,256]{1,0:T(8,128)(2,1)S(1)}, bf16[256,256]{1,0:T(8,128)(2,1)S(1)}, u32[]{:S(2)}, u32[]{:S(2)}) collective-permute-start(bf16[256,256]{1,0:T(8,128)(2,1)S(1)} %collective-permute-done.11.refs_2_), channel_id=1, source_target_pairs={{0,1},{1,0},{2,3},{3,2},{4,5},{5,4},{6,7},{7,6},{8,9},{9,8},{10,11... | collective-permute-start | bytes 393224 | tf_op jit(solution)/shard_map/ppermute | solution.py:495
  88.1 7.7 %collective-permute-start.10 = (bf16[288,256]{1,0:T(8,128)(2,1)S(1)}, bf16[288,256]{1,0:T(8,128)(2,1)S(1)}, u32[]{:S(2)}, u32[]{:S(2)}) collective-permute-start(bf16[288,256]{1,0:T(8,128)(2,1)S(1)} %shard_map.101.refs_3_), channel_id=1, source_target_pairs={{0,6},{1,7},{2,0},{3,1},{4,2},{5,3},{6,4},{7,5},{8,14},{9,15},{10,... | collective-permute-start | bytes 442376 | tf_op jit(solution)/shard_map/ppermute | solution.py:476
  88.2 13.9 %collective-permute-start.9 = (bf16[288,256]{1,0:T(8,128)(2,1)S(1)}, bf16[288,256]{1,0:T(8,128)(2,1)S(1)}, u32[]{:S(2)}, u32[]{:S(2)}) collective-permute-start(bf16[288,256]{1,0:T(8,128)(2,1)S(1)} %shard_map.101.refs_3_), channel_id=1, source_target_pairs={{0,4},{1,5},{2,6},{3,7},{4,0},{5,1},{6,2},{7,3},{8,12},{9,13},{10,... | collective-permute-start | bytes 442376 | tf_op jit(solution)/shard_map/ppermute | solution.py:476
  89.0 13.1 %collective-permute-start.8 = (bf16[288,256]{1,0:T(8,128)(2,1)S(1)}, bf16[288,256]{1,0:T(8,128)(2,1)S(1)}, u32[]{:S(2)}, u32[]{:S(2)}) collective-permute-start(bf16[288,256]{1,0:T(8,128)(2,1)S(1)} %shard_map.101.refs_3_), channel_id=1, source_target_pairs={{0,2},{1,3},{2,4},{3,5},{4,6},{5,7},{6,0},{7,1},{8,10},{9,11},{10,... | collective-permute-start | bytes 442376 | tf_op jit(solution)/shard_map/ppermute | solution.py:476
  90.4 13.3 %collective-permute-start.25 = (bf16[288,256]{1,0:T(8,128)(2,1)S(1)}, bf16[288,256]{1,0:T(8,128)(2,1)S(1)}, u32[]{:S(2)}, u32[]{:S(2)}) collective-permute-start(bf16[288,256]{1,0:T(8,128)(2,1)S(1)} %shard_map.101.refs_3_), channel_id=1, source_target_pairs={{0,1},{1,0},{2,3},{3,2},{4,5},{5,4},{6,7},{7,6},{8,9},{9,8},{10,11... | collective-permute-start | bytes 442376 | tf_op jit(solution)/shard_map/ppermute | solution.py:480
  102.1 2.1 %collective-permute-start.26 = (bf16[288,256]{1,0:T(8,128)(2,1)S(1)}, bf16[288,256]{1,0:T(8,128)(2,1)S(1)}, u32[]{:S(2)}, u32[]{:S(2)}) collective-permute-start(bf16[288,256]{1,0:T(8,128)(2,1)S(1)} %collective-permute-done.8.refs_4_), channel_id=1, source_target_pairs={{0,1},{1,0},{2,3},{3,2},{4,5},{5,4},{6,7},{7,6},{8,9},{9,8},{10,11... | collective-permute-start | bytes 442376 | tf_op jit(solution)/shard_map/ppermute | solution.py:480
  103.2 1.4 %collective-permute-start.27 = (bf16[288,256]{1,0:T(8,128)(2,1)S(1)}, bf16[288,256]{1,0:T(8,128)(2,1)S(1)}, u32[]{:S(2)}, u32[]{:S(2)}) collective-permute-start(bf16[288,256]{1,0:T(8,128)(2,1)S(1)} %collective-permute-done.9.refs_5_), channel_id=1, source_target_pairs={{0,1},{1,0},{2,3},{3,2},{4,5},{5,4},{6,7},{7,6},{8,9},{9,8},{10,11... | collective-permute-start | bytes 442376 | tf_op jit(solution)/shard_map/ppermute | solution.py:480
  103.2 1.6 %collective-permute-start.28 = (bf16[288,256]{1,0:T(8,128)(2,1)S(1)}, bf16[288,256]{1,0:T(8,128)(2,1)S(1)}, u32[]{:S(2)}, u32[]{:S(2)}) collective-permute-start(bf16[288,256]{1,0:T(8,128)(2,1)S(1)} %collective-permute-done.10.refs_6_), channel_id=1, source_target_pairs={{0,1},{1,0},{2,3},{3,2},{4,5},{5,4},{6,7},{7,6},{8,9},{9,8},{10,11... | collective-permute-start | bytes 442376 | tf_op jit(solution)/shard_map/ppermute | solution.py:480

commit v3 on v2

--- a/solution.py
+++ b/solution.py
@@ -14,6 +14,7 @@
 F32 = jnp.float32
 PAD = 8
 SPARE = 6 * 1024 * 1024
+CARRY = 16
 
 
 class Dims:
@@ -109,8 +110,11 @@
 
 def forward_kernel(dm, t, has_skip_in, has_mirror, *refs):
     refs = list(refs)
-    me_ref, x_ref, w_ref, b_ref = refs[:4]
-    at = 4
+    count = dm.parts if t == 0 else 1
+    me_ref, x_refs = refs[0], refs[1:1 + count]
+    w_ref, b_ref = refs[1 + count:3 + count]
+    at = 3 + count
+    x_ref = x_refs[0]
     skip_ref = kept_ref = None
     if has_skip_in:
         skip_ref = refs[at]
@@ -124,10 +128,14 @@
         mirror_ref = refs[at]
         at += 1
     if t == 0:
-        lab_ref = refs[at]
+        lab_ref, xg = refs[at], refs[-1]
         at += 1
         wide = dm.own + 2 * (dm.fwd(0) + 1)
-        lab_ref[...] = x_ref[...].astype(F32)[:, wide, :]
+        layers = dm.G // dm.parts
+        for r in range(dm.parts):
+            place = lax.rem(me_ref[0] + (dm.parts - r), dm.parts)
+            xg[pl.ds(place * layers, layers)] = x_refs[r][...].astype(F32)
+        lab_ref[...] = xg[:, wide, :]
     xf, x27 = refs[at:at + 2]
 
     @pl.when(me_ref[2] == t)
@@ -135,7 +143,7 @@
         base = me_ref[0] * dm.own
         k = dm.fwd(t)
         if t == 0:
-            gather_cells(dm, x_ref, xf)
+            gather_cells(dm, xg, xf)
         else:
             stage(xf, x_ref[...], dm.rows_of(k + 1))
         size, mid = dm.own * dm.G, (k + 1) * dm.G
@@ -156,30 +164,43 @@
             own_ref[...] = kept_ref[...]
 
 
-def pack_kernel(dm, wing, cols, me_ref, f_ref, l_ref, out_ref, xs, marks):
+def split_kernel(dm, me_ref, f_ref, l_ref, *refs):
+    outs, marks = refs[:dm.micro], refs[dm.micro]
+    W = dm.W
+    layers = f_ref.shape[0] // dm.micro
+    for e in range(dm.micro):
+        crop = lax.rem(me_ref[1] + e, dm.micro)
+        marks[...] = jnp.zeros(marks.shape, F32)
+        for layer in range(layers):
+            at = crop * layers + layer
+            outs[e][layer * W:(layer + 1) * W, :] = f_ref[at]
+            marks[layer:layer + 1, 0:W] = l_ref[at].astype(F32)
+        outs[e][layers * W:, :] = marks[...].astype(BF)
+
+
+def window_kernel(dm, wing, cols, me_ref, *refs):
+    crops, outs, xs = refs[:dm.micro], refs[dm.micro:-1], refs[-1]
     C, W, own = dm.C, dm.W, dm.own
-    layers = f_ref.shape[0] // dm.micro
-    front = -(-wing // 8) * 8
-    marks[...] = jnp.zeros(marks.shape, F32)
-    marks[0:dm.micro * layers, 0:W] = l_ref[...].astype(F32)
-    xs[0:front, :] = jnp.zeros((front, C), F32)
-    xs[front + W:, :] = jnp.zeros((xs.shape[0] - front - W, C), F32)
+    layers = dm.G // dm.slabs
+    xs[0:16, :] = jnp.zeros((16, C), F32)
+    xs[wing + W:, :] = jnp.zeros((xs.shape[0] - wing - W, C), F32)
     row = lax.broadcasted_iota(jnp.int32, (cols, C), 0)
     for e in range(dm.micro):
+        crop = crops[e][...].astype(F32)
+        core = lax.rem(me_ref[1] + (dm.micro - e), dm.micro)
         for layer in range(layers):
-            at = e * layers + layer
-            xs[front:front + W, :] = f_ref[at].astype(F32)
-            mark = marks[at:at + 1, :]
-            for p in range(dm.parts):
-                start = front + p * own - wing
-                value = jnp.where(row == own + 2 * wing, mark, xs[start:start + cols, :])
-                first = ((p * dm.micro + e) * layers + layer) * cols
-                out_ref[first:first + cols, :] = value.astype(BF)
-
-
-def gather_cells(dm, x_ref, xf):
+            xs[wing:wing + W, :] = crop[layer * W:(layer + 1) * W]
+            mark = crop[layers * W + layer:layers * W + layer + 1]
+            for r in range(dm.parts):
+                place = lax.rem(me_ref[0] + r, dm.parts)
+                start = pl.multiple_of(place * own, 8)
+                value = jnp.where(row == own + 2 * wing, mark, xs[pl.ds(start, cols), :])
+                outs[r][core * layers + layer] = value.astype(BF)
+
+
+def gather_cells(dm, xg, xf):
     rows = (dm.own + 2 * (dm.fwd(0) + 1)) * dm.G
-    cells = jnp.transpose(x_ref[...].astype(F32), (1, 0, 2))
+    cells = jnp.transpose(xg[...], (1, 0, 2))
     cells = cells.reshape(cells.shape[0] * dm.G, dm.C)
     xf[PAD:PAD + rows, :] = cells[0:rows]
 
@@ -243,9 +264,15 @@
     return target
 
 
+def target_kernel(dm, me_ref, off_ref, lab_ref, out_ref):
+    t = dm.sections - 1
+    lab = flat_labels(dm, me_ref[0] * dm.own - t - 1, dm.own + 2 * t + 2, lab_ref)
+    out_ref[...] = affinity(dm, dm.own + 2 * t, lab, off_ref)
+
+
 def last_kernel(dm, *refs):
-    (me_ref, off_ref, x_ref, w_ref, b_ref, skip_ref, kept_ref, wt_ref, head_ref, lab_ref) = refs[:10]
-    msg_ref, pgx_ref, skip_out, own_ref, xf, x27 = refs[10:]
+    (me_ref, x_ref, w_ref, b_ref, skip_ref, kept_ref, wt_ref, head_ref, target_ref) = refs[:9]
+    msg_ref, pgx_ref, skip_out, own_ref, xf, x27, lines = refs[9:]
     t = dm.sections - 1
 
     @pl.when(me_ref[2] == t)
@@ -258,8 +285,7 @@
         pre = preact(dm, t, xf, x27, skip_ref, w_ref, b_ref)
         y = silu_masked(dm, base, t, pre)
         logits = dot_nt(head_ref[...], y)
-        lab = flat_labels(dm, base - t - 1, own + 2 * t + 2, lab_ref)
-        target = affinity(dm, own + 2 * t, lab, off_ref)
+        target = target_ref[...]
         live = lax.broadcasted_iota(jnp.int32, logits.shape, 0) < dm.offs
         sig = 1.0 / (1.0 + jnp.exp(-logits))
         lg = jnp.where(live, loss_scale * (sig - target) / dm.count, 0.0).astype(BF)
@@ -267,21 +293,23 @@
         term = jnp.where(live, term, 0.0)[:, mid:mid + size]
         loss = jnp.sum(jnp.sum(term, axis=1, keepdims=True), axis=0, keepdims=True)
         head_part = dot(lg[:, mid:mid + size], y[mid:mid + size])
-        row = lax.broadcasted_iota(jnp.int32, (8, C), 0)
-        carry = jnp.where(row < dm.offs, head_part, jnp.where(row == dm.offs, loss, 0.0))
-        pieces = []
-        for _ in range(3):
-            piece = carry.astype(BF).astype(F32)
-            pieces.append(piece)
-            carry = carry - piece
-        carry = jnp.concatenate(pieces + [jnp.zeros((8, C), F32)], axis=0).astype(BF)
+        used = dm.offs + 1
+        lines[...] = jnp.zeros(lines.shape, F32)
+        lines[0:dm.offs, :] = head_part[0:dm.offs]
+        lines[dm.offs:used, :] = jnp.broadcast_to(loss, (1, C))
+        rest = lines[0:8, :]
+        for i in range(3):
+            piece = rest.astype(BF).astype(F32)
+            lines[i * used:(i + 1) * used, :] = piece[0:used]
+            rest = rest - piece
+        carry = lines[...].astype(BF)
         upstream = dot_tn(lg, head_ref[...])
         pg = pre_gradient(dm, base, t, upstream, pre)
         pgx_ref[0:size, :] = pg[mid:mid + size]
-        pgx_ref[size:size + 32, :] = carry
+        pgx_ref[size:size + CARRY, :] = carry
         back_conv(dm, t, pg, xf, x27, wt_ref, b_ref, msg_ref)
         end = dm.rows_of(t - 1)
-        msg_ref[end:end + 32, :] = carry
+        msg_ref[end:end + CARRY, :] = carry
         m = dm.sections - 1 - t
         first = (t - m) * G
         skip_out[...] = dot_nt(pg[first:first + dm.rows_of(m)], b_ref[...]).astype(BF)
@@ -320,13 +348,13 @@
             upstream = upstream + skip_ref[0:ro, :].astype(F32)
         pg = pre_gradient(dm, base, t, upstream, pre_ref[...])
         mid, size = t * dm.G, dm.own * dm.G
-        carry = down_ref[ro:ro + 32, :]
+        carry = down_ref[ro:ro + CARRY, :]
         pgx_ref[0:size, :] = pg[mid:mid + size]
-        pgx_ref[size:size + 32, :] = carry
+        pgx_ref[size:size + CARRY, :] = carry
         if t > 0:
             back_conv(dm, t, pg, xf, x27, wt_ref, b_ref, msg_ref)
             end = dm.rows_of(t - 1)
-            msg_ref[end:end + 32, :] = carry
+            msg_ref[end:end + CARRY, :] = carry
             if t > dm.half:
                 m = dm.sections - 1 - t
                 first = (t - m) * dm.G
@@ -383,9 +411,10 @@
             place = lax.rem(q_ref[0] + (dm.parts - r), dm.parts)
             at = pl.multiple_of(start + G + place * size, 16)
             full[pl.ds(at, size), :] = block[0:size, :]
-            carry = block[size:size + 32, :].astype(F32)
+            carry = block[size:size + CARRY, :].astype(F32)
             slot = lax.rem(q_ref[1] + (dm.micro - e), dm.micro) * dm.parts + place
-            sums[slot] = (carry[0:8] + carry[8:16]) + carry[16:24]
+            used = dm.offs + 1
+            sums[slot, 0:used] = (carry[0:used] + carry[used:2 * used]) + carry[2 * used:3 * used]
 
     def product(lhs_ref, row, count, kx):
         total = None
@@ -510,20 +539,28 @@
     wing = dm.fwd(0) + 1
     wide = own + 2 * wing
     cols = -(-(wide + 1) // 16) * 16
-    cells = jnp.transpose(features_in, (0, 2, 3, 4, 1)).reshape(micro * thick * R, W, C)
-    front = -(-wing // 8) * 8
-    packs = call(
-        functools.partial(pack_kernel, dm, wing, cols),
-        [me], [cells, labels.reshape(micro * thick * R, W)],
-        [shape(slabs * thick * R * cols, C, BF)],
-        [
-            pltpu.VMEM((front + W + cols, C), F32),
-            pltpu.VMEM((-(-micro * thick * R // 8) * 8, C), F32),
-        ],
+    layers = thick * R
+    cells = jnp.transpose(features_in, (0, 2, 3, 4, 1)).reshape(micro * layers, W, C)
+    lines = -(-layers // 16) * 16
+    crops = list(call(
+        functools.partial(split_kernel, dm),
+        [me], [cells, labels.reshape(micro * layers, 1, W)],
+        [shape(layers * W + lines, C, BF)] * micro,
+        [pltpu.VMEM((lines, C), F32)],
         1000,
-    )[0].reshape(slabs, thick * R, cols, C)
-    first = lax.all_to_all(packs, "slab", 0, 0, tiled=True).reshape(G, cols, C)
-    current = first
+    ))
+    for e in range(1, micro):
+        crops[e] = swap(crops[e], e)
+    windows = call(
+        functools.partial(window_kernel, dm, wing, cols),
+        [me], crops,
+        [jax.ShapeDtypeStruct((micro * layers, cols, C), BF)] * parts,
+        [pltpu.VMEM((-(-(wing + W + cols) // 8) * 8, C), F32)],
+        1000,
+    )
+    current = [windows[0]]
+    for r in range(1, parts):
+        current.append(rotate(windows[r], r))
 
     head = jnp.pad(jnp.transpose(head_weight), ((0, 8 - dm.offs), (0, 0)))
 
@@ -532,7 +569,7 @@
     for t in range(n - 1):
         k = dm.fwd(t)
         has_skip, has_mirror = t > half, t < half - 1
-        operands = [current, kernel, mixing]
+        operands = [*(current if t == 0 else [current]), kernel, mixing]
         if has_skip:
             operands.append(mirrors[t])
         if t > 0:
@@ -543,6 +580,7 @@
             outs.append(shape(dm.rows_of(dm.fwd(n - 1 - t)), C, BF))
         if t == 0:
             outs.append(shape(G, C, F32))
+            scratch.append(pltpu.VMEM((G, cols, C), F32))
         results = call(
             functools.partial(forward_kernel, dm, t, has_skip, has_mirror),
             [me], operands, outs, scratch,
@@ -553,7 +591,11 @@
         current = hop(results[0], t, t + 1)
         if t == 0:
             marks = results[-1]
-            raw, _ = lax.optimization_barrier((kernel, results[0]))
+            raw, marks, _ = lax.optimization_barrier((kernel, marks, results[0]))
+            targets = call(
+                functools.partial(target_kernel, dm), [me, offsets], [marks],
+                [shape(8, dm.rows_of(n - 1), F32)], [], 1000,
+            )[0]
             kernel_t = call(
                 functools.partial(flip_kernel, C), [], [raw],
                 [shape(27 * C, C, BF)], [], 2 * 27 * C * C * 100,
@@ -571,17 +613,17 @@
     branch, _ = lax.optimization_barrier((branch, results[0]))
     branches = gather(branch, half + 1)
     outs = [
-        shape(dm.rows_of(t - 1) + 32, C, BF),
-        shape(size + 32, C, BF),
+        shape(dm.rows_of(t - 1) + CARRY, C, BF),
+        shape(size + CARRY, C, BF),
         shape(dm.rows_of(0), C, BF),
         shape(size, C, BF),
     ]
     results = call(
         functools.partial(last_kernel, dm),
-        [me, offsets],
-        [current, kernel, mixing, skip, kept, kernel_t, head, marks],
+        [me],
+        [current, kernel, mixing, skip, kept, kernel_t, head, targets],
         outs,
-        conv_scratch(dm, dm.rows_of(t + 1), dm.rows_of(t)),
+        conv_scratch(dm, dm.rows_of(t + 1), dm.rows_of(t)) + [pltpu.VMEM((CARRY, C), F32)],
         4 * dm.rows_of(t) * 28 * C * C,
     )
     down = hop(results[0], t, t - 1)
@@ -597,10 +639,10 @@
             operands += [kernel_t, mixing]
         if has_skip:
             operands.append(skip_grads[t])
-        outs = [shape(size + 32, C, BF)]
+        outs = [shape(size + CARRY, C, BF)]
         scratch = []
         if t > 0:
-            outs.append(shape(dm.rows_of(t - 1) + 32, C, BF))
+            outs.append(shape(dm.rows_of(t - 1) + CARRY, C, BF))
             if t > half:
                 outs.append(shape(dm.rows_of(n - 1 - t), C, BF))
             scratch = conv_scratch(dm, dm.rows_of(t), dm.rows_of(t - 1))

time: 116 us -> 110 us (0.948)
  waiting for transfers between devices: 33.4 us -> 29.1 us
  local copies, waits for them, and re-layouts: 6.08 us -> 4.52 us
    all_to_all x1 -> x0, starting transfers between devices: 5.55 us -> none  [body(): first = lax.all_to_all(packs, 'slab', 0, 0, tiled=True).reshape(G, cols, C)]
    ppermute x3 -> x6, starting transfers between devices: 2.24 us -> 7.75 us  [rotate(): return lax.ppermute(x, 'slab', pairs)]
    all_to_all x1 -> x0, waiting for transfers between devices: 3.26 us -> none  [body(): first = lax.all_to_all(packs, 'slab', 0, 0, tiled=True).reshape(G, cols, C)]
    unnamed x18 -> x12, local copies, waits for them, and re-layouts: 6.06 us -> 4.5 us
    ppermute x4 -> x5, starting transfers between devices: 2.94 us -> 3.68 us  [swap(): return lax.ppermute(x, 'slab', pairs)]
    ppermute x3 -> x6, waiting for transfers between devices: 6.28 us -> 5.59 us  [rotate(): return lax.ppermute(x, 'slab', pairs)]
    pallas_call x10 -> x12, Pallas kernels: 16.5 us -> 16.7 us  [call(): pl.pallas_call(kernel, out_shape=outs, in_specs=[scalar()] * len(scalars)...]
  transfers between devices with their start and end apart: 30 -> 33, of which waited for: 9 -> 9; matrix products, arithmetic and copies ran while one was open for 0% -> 0% of each run, Pallas kernels for 8% -> 9%
where the time goes in v3:
time: 110 us; the launch traced here: 109 us
  starting transfers between devices  45.9 us (42%)
  waiting for transfers between devices  29.1 us (26%)
  Pallas kernels  28.6 us (26%)
  local copies, waits for them, and re-layouts  4.52 us (4%)
  between operations  1.19 us (1%)
    ppermute x14, starting transfers between devices, along(): return lax.ppermute(x, ('section', 'slab'), joint)  26.6 us
    ppermute x8, waiting for transfers between devices, hop(): return lax.ppermute(x, 'section', [(source, target)])  17 us
    pallas_call x12, Pallas kernels, call(): pl.pallas_call(kernel, out_shape=outs, in_specs=[scalar()] * len(scalars)...  16.7 us
    pallas_call x1, Pallas kernels, body(): pl.pallas_call(functools.partial(weight_kernel, dm), name='weights', out_...  10 us
    ppermute x8, starting transfers between devices, hop(): return lax.ppermute(x, 'section', [(source, target)])  7.87 us
    ppermute x6, starting transfers between devices, rotate(): return lax.ppermute(x, 'slab', pairs)  7.75 us
    ppermute x6, waiting for transfers between devices, rotate(): return lax.ppermute(x, 'slab', pairs)  5.59 us
    unnamed x12, local copies, waits for them, and re-layouts  4.5 us
  transfers between devices with their start and end apart: 33, of which 9 were waited for; matrix products, arithmetic and copies ran while one was open for 0% of the time, Pallas kernels for 9%

profile of v3, /device:TPU:7, one launch (start us, length us, event | category | flops | bytes accessed | tf_op | source)
XLA Modules:
  0.0 109.4 jit_solution(4632610252061303932)
XLA Ops:
  0.7 0.9 copy-done.2
  1.6 0.7 copy-done.3
  2.3 0.6 shard_map.93
  2.9 0.7 collective-permute-start
  3.6 0.9 collective-permute-done.refs_1_
  4.5 0.6 shard_map.94
  5.1 1.3 %collective-permute-start.1 = (bf16[4,32,256]{2,1,0:T(8,128)(2,1)S(1)}, bf16[4,32,256]{2,1,0:T(8,128)(2,1)S(1)}, u32[]{:S(2)}, u32[]{:S(2)}) collective-permute-start(bf16[4,32,256]{2,1,0:T(8,128)(2,1)S(1)} %get-tuple-element.50), channel_id=1, source_target_pairs={{0,2},{1,3},{2,4},{3,5},{4,6},{5,7},{6,0},{7,1},{8,10},{9,11},{10,... | collective-permute-start | bytes 196616 | tf_op jit(solution)/shard_map/ppermute | solution.py:505
  6.5 2.3 %collective-permute-start.2 = (bf16[4,32,256]{2,1,0:T(8,128)(2,1)S(1)}, bf16[4,32,256]{2,1,0:T(8,128)(2,1)S(1)}, u32[]{:S(2)}, u32[]{:S(2)}) collective-permute-start(bf16[4,32,256]{2,1,0:T(8,128)(2,1)S(1)} %get-tuple-element.51), channel_id=1, source_target_pairs={{0,4},{1,5},{2,6},{3,7},{4,0},{5,1},{6,2},{7,3},{8,12},{9,13},{10,... | collective-permute-start | bytes 196616 | tf_op jit(solution)/shard_map/ppermute | solution.py:505
  8.8 1.1 collective-permute-start.3
  9.9 2.0 %copy-done = bf16[1,3,3,3,256,256]{5,4,3,2,1,0:T(8,128)(2,1)S(1)} copy-done((bf16[1,3,3,3,256,256]{5,4,3,2,1,0:T(8,128)(2,1)S(1)}, bf16[1,3,3,3,256,256]{5,4,3,2,1,0:T(8,128)(2,1)}, u32[]{:S(2)}) %copy-start) | copy-done | bytes 3538968
  11.9 0.9 copy-done.1
  12.8 1.9 %load.1 = (bf16[6912,256]{1,0:T(8,128)(2,1)S(1)}, bf16[256,256]{1,0:T(8,128)(2,1)S(1)}) custom-call(bf16[6912,256]{1,0:T(8,128)(2,1)S(1)} %bitcast.14, bf16[256,256]{1,0:T(8,128)(2,1)S(1)} %bitcast.15), custom_call_target="tpu_custom_call" | custom-call | bytes 7077888 | tf_op jit(solution)/shard_map/load/pallas_call | solution.py:528
  14.8 0.6 shard_map.95
  15.4 0.7 collective-permute-start.4
  16.1 0.6 shard_map.96
  16.6 0.7 collective-permute-start.5
  17.9 1.3 %collective-permute-start.6 = (bf16[384,256]{1,0:T(8,128)(2,1)S(1)}, bf16[384,256]{1,0:T(8,128)(2,1)S(1)}, u32[]{:S(2)}, u32[]{:S(2)}) collective-permute-start(bf16[384,256]{1,0:T(8,128)(2,1)S(1)} %get-tuple-element.61), channel_id=1, source_target_pairs={{16,24},{17,25},{18,26},{19,27},{20,28},{21,29},{22,30},{23,31}} | collective-permute-start | bytes 589832 | tf_op jit(solution)/shard_map/ppermute | solution.py:501
  19.2 1.3 %collective-permute-start.7 = (bf16[352,256]{1,0:T(8,128)(2,1)S(1)}, bf16[352,256]{1,0:T(8,128)(2,1)S(1)}, u32[]{:S(2)}, u32[]{:S(2)}) collective-permute-start(bf16[352,256]{1,0:T(8,128)(2,1)S(1)} %get-tuple-element.62), channel_id=1, source_target_pairs={{0,24},{1,25},{2,26},{3,27},{4,28},{5,29},{6,30},{7,31}} | collective-permute-start | bytes 540680 | tf_op jit(solution)/shard_map/ppermute | solution.py:501
  20.5 0.8 shard_map.99.refs_8_
  21.3 1.0 shard_map.98.refs_6_.refs_4_
  22.3 7.0 %collective-permute-done.7.refs_4_ = bf16[352,256]{1,0:T(8,128)(2,1)S(1)} collective-permute-done((bf16[352,256]{1,0:T(8,128)(2,1)S(1)}, bf16[352,256]{1,0:T(8,128)(2,1)S(1)}, u32[]{:S(2)}, u32[]{:S(2)}) %collective-permute-start.7) | collective-permute-done | bytes 180256 | tf_op jit(solution)/shard_map/ppermute | solution.py:501
  29.3 9.3 %collective-permute-done.6.refs_1_ = bf16[384,256]{1,0:T(8,128)(2,1)S(1)} collective-permute-done((bf16[384,256]{1,0:T(8,128)(2,1)S(1)}, bf16[384,256]{1,0:T(8,128)(2,1)S(1)}, u32[]{:S(2)}, u32[]{:S(2)}) %collective-permute-start.6) | collective-permute-done | bytes 196640 | tf_op jit(solution)/shard_map/ppermute | solution.py:501
  38.6 6.1 %shard_map.100 = (bf16[336,256]{1,0:T(8,128)(2,1)S(1)}, bf16[272,256]{1,0:T(8,128)(2,1)S(1)}, bf16[256,256]{1,0:T(8,128)(2,1)S(1)}, bf16[256,256]{1,0:T(8,128)(2,1)S(1)}) custom-call(s32[3]{0:T(128)S(1)} %pad_add_fusion.me_ref.refs_0_, bf16[384,256]{1,0:T(8,128)(2,1)S(1)} %collective-permute-done.6.refs_1_, ...), custom_call_target="tpu_custom_call" | custom-call | flops 2583691264 | bytes 8305664 | tf_op jit(solution)/shard_map/pallas_call | solution.py:470
  44.8 1.3 %collective-permute-start.8 = (bf16[336,256]{1,0:T(8,128)(2,1)S(1)}, bf16[336,256]{1,0:T(8,128)(2,1)S(1)}, u32[]{:S(2)}, u32[]{:S(2)}) collective-permute-start(bf16[336,256]{1,0:T(8,128)(2,1)S(1)} %get-tuple-element.67), channel_id=1, source_target_pairs={{24,16},{25,17},{26,18},{27,19},{28,20},{29,21},{30,22},{31,23}} | collective-permute-start | bytes 516104 | tf_op jit(solution)/shard_map/ppermute | solution.py:501
  46.1 1.9 %collective-permute-start.24 = (bf16[256,256]{1,0:T(8,128)(2,1)S(1)}, bf16[256,256]{1,0:T(8,128)(2,1)S(1)}, u32[]{:S(2)}, u32[]{:S(2)}) collective-permute-start(bf16[256,256]{1,0:T(8,128)(2,1)S(1)} %slice.4.refs_9_), channel_id=1, source_target_pairs={{24,30},{25,31},{26,24},{27,25},{28,26},{29,27},{30,28},{31,29}} | collective-permute-start | bytes 393224 | tf_op jit(solution)/shard_map/ppermute | solution.py:524
  48.0 4.7 %collective-permute-start.23 = (bf16[256,256]{1,0:T(8,128)(2,1)S(1)}, bf16[256,256]{1,0:T(8,128)(2,1)S(1)}, u32[]{:S(2)}, u32[]{:S(2)}) collective-permute-start(bf16[256,256]{1,0:T(8,128)(2,1)S(1)} %slice.4.refs_9_), channel_id=1, source_target_pairs={{24,28},{25,29},{26,30},{27,31},{28,24},{29,25},{30,26},{31,27}} | collective-permute-start | bytes 393224 | tf_op jit(solution)/shard_map/ppermute | solution.py:524
  52.7 0.6 shard_map.101
  53.3 0.7 collective-permute-start.9
  54.0 5.5 %collective-permute-start.25 = (bf16[256,256]{1,0:T(8,128)(2,1)S(1)}, bf16[256,256]{1,0:T(8,128)(2,1)S(1)}, u32[]{:S(2)}, u32[]{:S(2)}) collective-permute-start(bf16[256,256]{1,0:T(8,128)(2,1)S(1)} %slice.4.refs_9_), channel_id=1, source_target_pairs={{24,25},{25,24},{26,27},{27,26},{28,29},{29,28},{30,31},{31,30}} | collective-permute-start | bytes 393224 | tf_op jit(solution)/shard_map/ppermute | solution.py:524
  59.5 1.9 %collective-permute-start.22 = (bf16[256,256]{1,0:T(8,128)(2,1)S(1)}, bf16[256,256]{1,0:T(8,128)(2,1)S(1)}, u32[]{:S(2)}, u32[]{:S(2)}) collective-permute-start(bf16[256,256]{1,0:T(8,128)(2,1)S(1)} %slice.4.refs_9_), channel_id=1, source_target_pairs={{24,26},{25,27},{26,28},{27,29},{28,30},{29,31},{30,24},{31,25}} | collective-permute-start | bytes 393224 | tf_op jit(solution)/shard_map/ppermute | solution.py:524
  61.4 1.9 %collective-permute-start.28 = (bf16[256,256]{1,0:T(8,128)(2,1)S(1)}, bf16[256,256]{1,0:T(8,128)(2,1)S(1)}, u32[]{:S(2)}, u32[]{:S(2)}) collective-permute-start(bf16[256,256]{1,0:T(8,128)(2,1)S(1)} %collective-permute-done.24.refs_12_), channel_id=1, source_target_pairs={{24,25},{25,24},{26,27},{27,26},{28,29},{29,28},{30,31},{31,30}} | collective-permute-start | bytes 393224 | tf_op jit(solution)/shard_map/ppermute | solution.py:524
  63.3 2.4 %collective-permute-start.27 = (bf16[256,256]{1,0:T(8,128)(2,1)S(1)}, bf16[256,256]{1,0:T(8,128)(2,1)S(1)}, u32[]{:S(2)}, u32[]{:S(2)}) collective-permute-start(bf16[256,256]{1,0:T(8,128)(2,1)S(1)} %collective-permute-done.23.refs_11_), channel_id=1, source_target_pairs={{24,25},{25,24},{26,27},{27,26},{28,29},{29,28},{30,31},{31,30}} | collective-permute-start | bytes 393224 | tf_op jit(solution)/shard_map/ppermute | solution.py:524
  65.8 3.3 %collective-permute-start.17 = (bf16[256,256]{1,0:T(8,128)(2,1)S(1)}, bf16[256,256]{1,0:T(8,128)(2,1)S(1)}, u32[]{:S(2)}, u32[]{:S(2)}) collective-permute-start(bf16[256,256]{1,0:T(8,128)(2,1)S(1)} %get-tuple-element.78.refs_1_), channel_id=1, source_target_pairs={{0,6},{1,7},{2,0},{3,1},{4,2},{5,3},{6,4},{7,5},{8,14},{9,15},{10,... | collective-permute-start | bytes 393224 | tf_op jit(solution)/shard_map/ppermute | solution.py:524
  69.1 1.3 %collective-permute-start.11 = (bf16[256,256]{1,0:T(8,128)(2,1)S(1)}, bf16[256,256]{1,0:T(8,128)(2,1)S(1)}, u32[]{:S(2)}, u32[]{:S(2)}) collective-permute-start(bf16[256,256]{1,0:T(8,128)(2,1)S(1)} %get-tuple-element.76), channel_id=1, source_target_pairs={{24,0},{25,1},{26,2},{27,3},{28,4},{29,5},{30,6},{31,7}} | collective-permute-start | bytes 393224 | tf_op jit(solution)/shard_map/ppermute | solution.py:501
  70.4 0.7 shard_map.102
  71.1 0.7 collective-permute-start.10
  72.2 0.7 collective-permute-done.11.refs_4_
  72.9 3.0 %collective-permute-start.26 = (bf16[256,256]{1,0:T(8,128)(2,1)S(1)}, bf16[256,256]{1,0:T(8,128)(2,1)S(1)}, u32[]{:S(2)}, u32[]{:S(2)}) collective-permute-start(bf16[256,256]{1,0:T(8,128)(2,1)S(1)} %collective-permute-done.22.refs_10_), channel_id=1, source_target_pairs={{24,25},{25,24},{26,27},{27,26},{28,29},{29,28},{30,31},{31,30}} | collective-permute-start | bytes 393224 | tf_op jit(solution)/shard_map/ppermute | solution.py:524
  76.1 4.5 %collective-permute-done.16.refs_3_ = bf16[256,256]{1,0:T(8,128)(2,1)S(1)} collective-permute-done((bf16[256,256]{1,0:T(8,128)(2,1)S(1)}, bf16[256,256]{1,0:T(8,128)(2,1)S(1)}, u32[]{:S(2)}, u32[]{:S(2)}) %collective-permute-start.16) | collective-permute-done | bytes 131104 | tf_op jit(solution)/shard_map/ppermute | solution.py:524
  80.5 1.0 collective-permute-start.21
  82.6 0.9 collective-permute-start.14
  83.5 0.7 collective-permute-start.13
  84.2 1.4 %collective-permute-start.12 = (bf16[272,256]{1,0:T(8,128)(2,1)S(1)}, bf16[272,256]{1,0:T(8,128)(2,1)S(1)}, u32[]{:S(2)}, u32[]{:S(2)}) collective-permute-start(bf16[272,256]{1,0:T(8,128)(2,1)S(1)} %shard_map.103.refs_3_), channel_id=1, source_target_pairs={{0,2},{1,3},{2,4},{3,5},{4,6},{5,7},{6,0},{7,1},{8,10},{9,11},{10,... | collective-permute-start | bytes 417800 | tf_op jit(solution)/shard_map/ppermute | solution.py:505
  85.6 1.3 %collective-permute-start.29 = (bf16[272,256]{1,0:T(8,128)(2,1)S(1)}, bf16[272,256]{1,0:T(8,128)(2,1)S(1)}, u32[]{:S(2)}, u32[]{:S(2)}) collective-permute-start(bf16[272,256]{1,0:T(8,128)(2,1)S(1)} %shard_map.103.refs_3_), channel_id=1, source_target_pairs={{0,1},{1,0},{2,3},{3,2},{4,5},{5,4},{6,7},{7,6},{8,9},{9,8},{10,11... | collective-permute-start | bytes 417800 | tf_op jit(solution)/shard_map/ppermute | solution.py:509
  87.0 4.1 %shard_map.104 = (bf16[2304,2048]{1,0:T(8,128)(2,1)S(1)}, bf16[256,2048]{1,0:T(8,128)(2,1)S(1)}) custom-call(s32[3]{0:T(128)S(1)} %pad_add_fusion.me_ref.refs_0_, bf16[256,256]{1,0:T(8,128)(2,1)S(1)} %get-tuple-element.78.refs_1_, bf16[256,256]{1,0:T(8,128)(2,1)S(1)} %collective-permute-done.15.refs_2_, ...), custom_call_target="tpu_custom_call" | custom-call | flops 1048576000 | bytes 12582912 | tf_op jit(solution)/shard_map/pallas_call | solution.py:470
  91.1 5.6 %collective-permute-done.13.refs_5_ = bf16[272,256]{1,0:T(8,128)(2,1)S(1)} collective-permute-done((bf16[272,256]{1,0:T(8,128)(2,1)S(1)}, bf16[272,256]{1,0:T(8,128)(2,1)S(1)}, u32[]{:S(2)}, u32[]{:S(2)}) %collective-permute-start.13) | collective-permute-done | bytes 139296 | tf_op jit(solution)/shard_map/ppermute | solution.py:505
  96.6 1.1 collective-permute-start.30
  99.3 10.0 %weights.1 = (f32[9,3,256,256]{3,2,1,0:T(8,128)}, f32[256,256]{1,0:T(8,128)}, f32[3,256]{1,0:T(4,128)}, f32[1,1]{1,0:T(1,128)}) custom-call(s32[3]{0:T(128)S(1)} %pad_add_fusion.me_ref.refs_0_, bf16[2304,2048]{1,0:T(8,128)(2,1)S(1)} %get-tuple-element.81.refs_1_, bf16[256,2048]{1,0:T(8,128)(2,1)S(1)} %get-tuple-element.82.refs_2_, ...), custom_call_target="tpu_custom_call" | custom-call | flops 7516192768 | bytes 18942980 | tf_op jit(solution)/shard_map/weights/pallas_call | solution.py:688
  (47 shorter events, 3.8 us)
Async XLA Ops:
  0.7 0.9 copy-start.2
  1.6 0.7 copy-start.3
  2.9 1.7 %collective-permute-start = (bf16[144,256]{1,0:T(8,128)(2,1)S(1)}, bf16[144,256]{1,0:T(8,128)(2,1)S(1)}, u32[]{:S(2)}, u32[]{:S(2)}) collective-permute-start(bf16[144,256]{1,0:T(8,128)(2,1)S(1)} %get-tuple-element.48), channel_id=1, source_target_pairs={{0,1},{1,0},{2,3},{3,2},{4,5},{5,4},{6,7},{7,6},{8,9},{9,8},{10,11... | collective-permute-start | bytes 221192 | tf_op jit(solution)/shard_map/ppermute | solution.py:509
  5.1 9.6 %collective-permute-start.1 = (bf16[4,32,256]{2,1,0:T(8,128)(2,1)S(1)}, bf16[4,32,256]{2,1,0:T(8,128)(2,1)S(1)}, u32[]{:S(2)}, u32[]{:S(2)}) collective-permute-start(bf16[4,32,256]{2,1,0:T(8,128)(2,1)S(1)} %get-tuple-element.50), channel_id=1, source_target_pairs={{0,2},{1,3},{2,4},{3,5},{4,6},{5,7},{6,0},{7,1},{8,10},{9,11},{10,... | collective-permute-start | bytes 196616 | tf_op jit(solution)/shard_map/ppermute | solution.py:505
  6.5 8.3 %collective-permute-start.2 = (bf16[4,32,256]{2,1,0:T(8,128)(2,1)S(1)}, bf16[4,32,256]{2,1,0:T(8,128)(2,1)S(1)}, u32[]{:S(2)}, u32[]{:S(2)}) collective-permute-start(bf16[4,32,256]{2,1,0:T(8,128)(2,1)S(1)} %get-tuple-element.51), channel_id=1, source_target_pairs={{0,4},{1,5},{2,6},{3,7},{4,0},{5,1},{6,2},{7,3},{8,12},{9,13},{10,... | collective-permute-start | bytes 196616 | tf_op jit(solution)/shard_map/ppermute | solution.py:505
  8.8 6.0 %collective-permute-start.3 = (bf16[4,32,256]{2,1,0:T(8,128)(2,1)S(1)}, bf16[4,32,256]{2,1,0:T(8,128)(2,1)S(1)}, u32[]{:S(2)}, u32[]{:S(2)}) collective-permute-start(bf16[4,32,256]{2,1,0:T(8,128)(2,1)S(1)} %get-tuple-element.52), channel_id=1, source_target_pairs={{0,6},{1,7},{2,0},{3,1},{4,2},{5,3},{6,4},{7,5},{8,14},{9,15},{10,... | collective-permute-start | bytes 196616 | tf_op jit(solution)/shard_map/ppermute | solution.py:505
  9.9 2.0 %copy-start = (bf16[1,3,3,3,256,256]{5,4,3,2,1,0:T(8,128)(2,1)S(1)}, bf16[1,3,3,3,256,256]{5,4,3,2,1,0:T(8,128)(2,1)}, u32[]{:S(2)}) copy-start(bf16[1,3,3,3,256,256]{5,4,3,2,1,0:T(8,128)(2,1)} %param.9) | copy-start | bytes 10616836
  11.9 0.9 copy-start.1
  15.4 0.7 collective-permute-start.4
  16.6 3.9 %copy-start.5 = (bf16[256,3]{0,1:T(4,128)(2,1)S(1)}, bf16[256,3]{0,1:T(4,128)(2,1)}, u32[]{:S(2)}) copy-start(bf16[256,3]{0,1:T(4,128)(2,1)} %param.11) | copy-start | bytes 4612
  16.6 3.9 %copy-start.4 = (s32[3,3]{1,0:T(4,128)S(1)}, s32[3,3]{1,0:T(4,128)}, u32[]{:S(2)}) copy-start(s32[3,3]{1,0:T(4,128)} %off_ref.1) | copy-start | bytes 112
  16.6 0.7 collective-permute-start.5
  17.9 20.7 %collective-permute-start.6 = (bf16[384,256]{1,0:T(8,128)(2,1)S(1)}, bf16[384,256]{1,0:T(8,128)(2,1)S(1)}, u32[]{:S(2)}, u32[]{:S(2)}) collective-permute-start(bf16[384,256]{1,0:T(8,128)(2,1)S(1)} %get-tuple-element.61), channel_id=1, source_target_pairs={{16,24},{17,25},{18,26},{19,27},{20,28},{21,29},{22,30},{23,31}} | collective-permute-start | bytes 589832 | tf_op jit(solution)/shard_map/ppermute | solution.py:501
  19.2 10.1 %collective-permute-start.7 = (bf16[352,256]{1,0:T(8,128)(2,1)S(1)}, bf16[352,256]{1,0:T(8,128)(2,1)S(1)}, u32[]{:S(2)}, u32[]{:S(2)}) collective-permute-start(bf16[352,256]{1,0:T(8,128)(2,1)S(1)} %get-tuple-element.62), channel_id=1, source_target_pairs={{0,24},{1,25},{2,26},{3,27},{4,28},{5,29},{6,30},{7,31}} | collective-permute-start | bytes 540680 | tf_op jit(solution)/shard_map/ppermute | solution.py:501
  44.8 8.0 %collective-permute-start.8 = (bf16[336,256]{1,0:T(8,128)(2,1)S(1)}, bf16[336,256]{1,0:T(8,128)(2,1)S(1)}, u32[]{:S(2)}, u32[]{:S(2)}) collective-permute-start(bf16[336,256]{1,0:T(8,128)(2,1)S(1)} %get-tuple-element.67), channel_id=1, source_target_pairs={{24,16},{25,17},{26,18},{27,19},{28,20},{29,21},{30,22},{31,23}} | collective-permute-start | bytes 516104 | tf_op jit(solution)/shard_map/ppermute | solution.py:501
  46.1 15.3 %collective-permute-start.24 = (bf16[256,256]{1,0:T(8,128)(2,1)S(1)}, bf16[256,256]{1,0:T(8,128)(2,1)S(1)}, u32[]{:S(2)}, u32[]{:S(2)}) collective-permute-start(bf16[256,256]{1,0:T(8,128)(2,1)S(1)} %slice.4.refs_9_), channel_id=1, source_target_pairs={{24,30},{25,31},{26,24},{27,25},{28,26},{29,27},{30,28},{31,29}} | collective-permute-start | bytes 393224 | tf_op jit(solution)/shard_map/ppermute | solution.py:524
  48.0 15.3 %collective-permute-start.23 = (bf16[256,256]{1,0:T(8,128)(2,1)S(1)}, bf16[256,256]{1,0:T(8,128)(2,1)S(1)}, u32[]{:S(2)}, u32[]{:S(2)}) collective-permute-start(bf16[256,256]{1,0:T(8,128)(2,1)S(1)} %slice.4.refs_9_), channel_id=1, source_target_pairs={{24,28},{25,29},{26,30},{27,31},{28,24},{29,25},{30,26},{31,27}} | collective-permute-start | bytes 393224 | tf_op jit(solution)/shard_map/ppermute | solution.py:524
  53.3 15.8 %collective-permute-start.9 = (bf16[304,256]{1,0:T(8,128)(2,1)S(1)}, bf16[304,256]{1,0:T(8,128)(2,1)S(1)}, u32[]{:S(2)}, u32[]{:S(2)}) collective-permute-start(bf16[304,256]{1,0:T(8,128)(2,1)S(1)} %get-tuple-element.70), channel_id=1, source_target_pairs={{16,8},{17,9},{18,10},{19,11},{20,12},{21,13},{22,14},{23,15}} | collective-permute-start | bytes 466952 | tf_op jit(solution)/shard_map/ppermute | solution.py:501
  54.0 11.8 %collective-permute-start.25 = (bf16[256,256]{1,0:T(8,128)(2,1)S(1)}, bf16[256,256]{1,0:T(8,128)(2,1)S(1)}, u32[]{:S(2)}, u32[]{:S(2)}) collective-permute-start(bf16[256,256]{1,0:T(8,128)(2,1)S(1)} %slice.4.refs_9_), channel_id=1, source_target_pairs={{24,25},{25,24},{26,27},{27,26},{28,29},{29,28},{30,31},{31,30}} | collective-permute-start | bytes 393224 | tf_op jit(solution)/shard_map/ppermute | solution.py:524
  59.5 9.6 %collective-permute-start.22 = (bf16[256,256]{1,0:T(8,128)(2,1)S(1)}, bf16[256,256]{1,0:T(8,128)(2,1)S(1)}, u32[]{:S(2)}, u32[]{:S(2)}) collective-permute-start(bf16[256,256]{1,0:T(8,128)(2,1)S(1)} %slice.4.refs_9_), channel_id=1, source_target_pairs={{24,26},{25,27},{26,28},{27,29},{28,30},{29,31},{30,24},{31,25}} | collective-permute-start | bytes 393224 | tf_op jit(solution)/shard_map/ppermute | solution.py:524
  61.4 9.7 %collective-permute-start.28 = (bf16[256,256]{1,0:T(8,128)(2,1)S(1)}, bf16[256,256]{1,0:T(8,128)(2,1)S(1)}, u32[]{:S(2)}, u32[]{:S(2)}) collective-permute-start(bf16[256,256]{1,0:T(8,128)(2,1)S(1)} %collective-permute-done.24.refs_12_), channel_id=1, source_target_pairs={{24,25},{25,24},{26,27},{27,26},{28,29},{29,28},{30,31},{31,30}} | collective-permute-start | bytes 393224 | tf_op jit(solution)/shard_map/ppermute | solution.py:524
  63.3 8.5 %collective-permute-start.27 = (bf16[256,256]{1,0:T(8,128)(2,1)S(1)}, bf16[256,256]{1,0:T(8,128)(2,1)S(1)}, u32[]{:S(2)}, u32[]{:S(2)}) collective-permute-start(bf16[256,256]{1,0:T(8,128)(2,1)S(1)} %collective-permute-done.23.refs_11_), channel_id=1, source_target_pairs={{24,25},{25,24},{26,27},{27,26},{28,29},{29,28},{30,31},{31,30}} | collective-permute-start | bytes 393224 | tf_op jit(solution)/shard_map/ppermute | solution.py:524
  65.8 10.2 %collective-permute-start.17 = (bf16[256,256]{1,0:T(8,128)(2,1)S(1)}, bf16[256,256]{1,0:T(8,128)(2,1)S(1)}, u32[]{:S(2)}, u32[]{:S(2)}) collective-permute-start(bf16[256,256]{1,0:T(8,128)(2,1)S(1)} %get-tuple-element.78.refs_1_), channel_id=1, source_target_pairs={{0,6},{1,7},{2,0},{3,1},{4,2},{5,3},{6,4},{7,5},{8,14},{9,15},{10,... | collective-permute-start | bytes 393224 | tf_op jit(solution)/shard_map/ppermute | solution.py:524
  69.1 11.5 %collective-permute-start.16 = (bf16[256,256]{1,0:T(8,128)(2,1)S(1)}, bf16[256,256]{1,0:T(8,128)(2,1)S(1)}, u32[]{:S(2)}, u32[]{:S(2)}) collective-permute-start(bf16[256,256]{1,0:T(8,128)(2,1)S(1)} %get-tuple-element.78.refs_1_), channel_id=1, source_target_pairs={{0,4},{1,5},{2,6},{3,7},{4,0},{5,1},{6,2},{7,3},{8,12},{9,13},{10,... | collective-permute-start | bytes 393224 | tf_op jit(solution)/shard_map/ppermute | solution.py:524
  69.1 3.8 %collective-permute-start.11 = (bf16[256,256]{1,0:T(8,128)(2,1)S(1)}, bf16[256,256]{1,0:T(8,128)(2,1)S(1)}, u32[]{:S(2)}, u32[]{:S(2)}) collective-permute-start(bf16[256,256]{1,0:T(8,128)(2,1)S(1)} %get-tuple-element.76), channel_id=1, source_target_pairs={{24,0},{25,1},{26,2},{27,3},{28,4},{29,5},{30,6},{31,7}} | collective-permute-start | bytes 393224 | tf_op jit(solution)/shard_map/ppermute | solution.py:501
  71.1 10.3 %collective-permute-start.10 = (bf16[272,256]{1,0:T(8,128)(2,1)S(1)}, bf16[272,256]{1,0:T(8,128)(2,1)S(1)}, u32[]{:S(2)}, u32[]{:S(2)}) collective-permute-start(bf16[272,256]{1,0:T(8,128)(2,1)S(1)} %get-tuple-element.73), channel_id=1, source_target_pairs={{8,0},{9,1},{10,2},{11,3},{12,4},{13,5},{14,6},{15,7}} | collective-permute-start | bytes 417800 | tf_op jit(solution)/shard_map/ppermute | solution.py:501
  71.8 9.7 %collective-permute-start.15 = (bf16[256,256]{1,0:T(8,128)(2,1)S(1)}, bf16[256,256]{1,0:T(8,128)(2,1)S(1)}, u32[]{:S(2)}, u32[]{:S(2)}) collective-permute-start(bf16[256,256]{1,0:T(8,128)(2,1)S(1)} %get-tuple-element.78.refs_1_), channel_id=1, source_target_pairs={{0,2},{1,3},{2,4},{3,5},{4,6},{5,7},{6,0},{7,1},{8,10},{9,11},{10,... | collective-permute-start | bytes 393224 | tf_op jit(solution)/shard_map/ppermute | solution.py:524
  72.9 9.7 %collective-permute-start.26 = (bf16[256,256]{1,0:T(8,128)(2,1)S(1)}, bf16[256,256]{1,0:T(8,128)(2,1)S(1)}, u32[]{:S(2)}, u32[]{:S(2)}) collective-permute-start(bf16[256,256]{1,0:T(8,128)(2,1)S(1)} %collective-permute-done.22.refs_10_), channel_id=1, source_target_pairs={{24,25},{25,24},{26,27},{27,26},{28,29},{29,28},{30,31},{31,30}} | collective-permute-start | bytes 393224 | tf_op jit(solution)/shard_map/ppermute | solution.py:524
  76.0 7.5 %collective-permute-start.18 = (bf16[256,256]{1,0:T(8,128)(2,1)S(1)}, bf16[256,256]{1,0:T(8,128)(2,1)S(1)}, u32[]{:S(2)}, u32[]{:S(2)}) collective-permute-start(bf16[256,256]{1,0:T(8,128)(2,1)S(1)} %get-tuple-element.78.refs_1_), channel_id=1, source_target_pairs={{0,1},{1,0},{2,3},{3,2},{4,5},{5,4},{6,7},{7,6},{8,9},{9,8},{10,11... | collective-permute-start | bytes 393224 | tf_op jit(solution)/shard_map/ppermute | solution.py:524
  80.5 3.7 %collective-permute-start.21 = (bf16[256,256]{1,0:T(8,128)(2,1)S(1)}, bf16[256,256]{1,0:T(8,128)(2,1)S(1)}, u32[]{:S(2)}, u32[]{:S(2)}) collective-permute-start(bf16[256,256]{1,0:T(8,128)(2,1)S(1)} %collective-permute-done.17.refs_4_), channel_id=1, source_target_pairs={{0,1},{1,0},{2,3},{3,2},{4,5},{5,4},{6,7},{7,6},{8,9},{9,8},{10,11... | collective-permute-start | bytes 393224 | tf_op jit(solution)/shard_map/ppermute | solution.py:524
  81.5 4.1 %collective-permute-start.20 = (bf16[256,256]{1,0:T(8,128)(2,1)S(1)}, bf16[256,256]{1,0:T(8,128)(2,1)S(1)}, u32[]{:S(2)}, u32[]{:S(2)}) collective-permute-start(bf16[256,256]{1,0:T(8,128)(2,1)S(1)} %collective-permute-done.16.refs_3_), channel_id=1, source_target_pairs={{0,1},{1,0},{2,3},{3,2},{4,5},{5,4},{6,7},{7,6},{8,9},{9,8},{10,11... | collective-permute-start | bytes 393224 | tf_op jit(solution)/shard_map/ppermute | solution.py:524
  81.5 5.5 %collective-permute-start.19 = (bf16[256,256]{1,0:T(8,128)(2,1)S(1)}, bf16[256,256]{1,0:T(8,128)(2,1)S(1)}, u32[]{:S(2)}, u32[]{:S(2)}) collective-permute-start(bf16[256,256]{1,0:T(8,128)(2,1)S(1)} %collective-permute-done.15.refs_2_), channel_id=1, source_target_pairs={{0,1},{1,0},{2,3},{3,2},{4,5},{5,4},{6,7},{7,6},{8,9},{9,8},{10,11... | collective-permute-start | bytes 393224 | tf_op jit(solution)/shard_map/ppermute | solution.py:524
  82.6 8.5 %collective-permute-start.14 = (bf16[272,256]{1,0:T(8,128)(2,1)S(1)}, bf16[272,256]{1,0:T(8,128)(2,1)S(1)}, u32[]{:S(2)}, u32[]{:S(2)}) collective-permute-start(bf16[272,256]{1,0:T(8,128)(2,1)S(1)} %shard_map.103.refs_3_), channel_id=1, source_target_pairs={{0,6},{1,7},{2,0},{3,1},{4,2},{5,3},{6,4},{7,5},{8,14},{9,15},{10,... | collective-permute-start | bytes 417800 | tf_op jit(solution)/shard_map/ppermute | solution.py:505
  83.5 13.1 %collective-permute-start.13 = (bf16[272,256]{1,0:T(8,128)(2,1)S(1)}, bf16[272,256]{1,0:T(8,128)(2,1)S(1)}, u32[]{:S(2)}, u32[]{:S(2)}) collective-permute-start(bf16[272,256]{1,0:T(8,128)(2,1)S(1)} %shard_map.103.refs_3_), channel_id=1, source_target_pairs={{0,4},{1,5},{2,6},{3,7},{4,0},{5,1},{6,2},{7,3},{8,12},{9,13},{10,... | collective-permute-start | bytes 417800 | tf_op jit(solution)/shard_map/ppermute | solution.py:505
  84.2 12.4 %collective-permute-start.12 = (bf16[272,256]{1,0:T(8,128)(2,1)S(1)}, bf16[272,256]{1,0:T(8,128)(2,1)S(1)}, u32[]{:S(2)}, u32[]{:S(2)}) collective-permute-start(bf16[272,256]{1,0:T(8,128)(2,1)S(1)} %shard_map.103.refs_3_), channel_id=1, source_target_pairs={{0,2},{1,3},{2,4},{3,5},{4,6},{5,7},{6,0},{7,1},{8,10},{9,11},{10,... | collective-permute-start | bytes 417800 | tf_op jit(solution)/shard_map/ppermute | solution.py:505
  85.6 12.6 %collective-permute-start.29 = (bf16[272,256]{1,0:T(8,128)(2,1)S(1)}, bf16[272,256]{1,0:T(8,128)(2,1)S(1)}, u32[]{:S(2)}, u32[]{:S(2)}) collective-permute-start(bf16[272,256]{1,0:T(8,128)(2,1)S(1)} %shard_map.103.refs_3_), channel_id=1, source_target_pairs={{0,1},{1,0},{2,3},{3,2},{4,5},{5,4},{6,7},{7,6},{8,9},{9,8},{10,11... | collective-permute-start | bytes 417800 | tf_op jit(solution)/shard_map/ppermute | solution.py:509
  96.6 2.1 %collective-permute-start.30 = (bf16[272,256]{1,0:T(8,128)(2,1)S(1)}, bf16[272,256]{1,0:T(8,128)(2,1)S(1)}, u32[]{:S(2)}, u32[]{:S(2)}) collective-permute-start(bf16[272,256]{1,0:T(8,128)(2,1)S(1)} %collective-permute-done.12.refs_4_), channel_id=1, source_target_pairs={{0,1},{1,0},{2,3},{3,2},{4,5},{5,4},{6,7},{7,6},{8,9},{9,8},{10,11... | collective-permute-start | bytes 417800 | tf_op jit(solution)/shard_map/ppermute | solution.py:509
  97.7 1.4 %collective-permute-start.31 = (bf16[272,256]{1,0:T(8,128)(2,1)S(1)}, bf16[272,256]{1,0:T(8,128)(2,1)S(1)}, u32[]{:S(2)}, u32[]{:S(2)}) collective-permute-start(bf16[272,256]{1,0:T(8,128)(2,1)S(1)} %collective-permute-done.13.refs_5_), channel_id=1, source_target_pairs={{0,1},{1,0},{2,3},{3,2},{4,5},{5,4},{6,7},{7,6},{8,9},{9,8},{10,11... | collective-permute-start | bytes 417800 | tf_op jit(solution)/shard_map/ppermute | solution.py:509
  97.7 1.6 %collective-permute-start.32 = (bf16[272,256]{1,0:T(8,128)(2,1)S(1)}, bf16[272,256]{1,0:T(8,128)(2,1)S(1)}, u32[]{:S(2)}, u32[]{:S(2)}) collective-permute-start(bf16[272,256]{1,0:T(8,128)(2,1)S(1)} %collective-permute-done.14.refs_6_), channel_id=1, source_target_pairs={{0,1},{1,0},{2,3},{3,2},{4,5},{5,4},{6,7},{7,6},{8,9},{9,8},{10,11... | collective-permute-start | bytes 417800 | tf_op jit(solution)/shard_map/ppermute | solution.py:509

commit v4 on v3

--- a/solution.py
+++ b/solution.py
@@ -216,6 +216,12 @@
     copies[chunks].start()
     for copy in copies:
         copy.wait()
+
+
+def stack_kernel(*refs):
+    rows = refs[0].shape[0]
+    for i, ref in enumerate(refs[:-1]):
+        refs[-1][i * rows:(i + 1) * rows, :] = ref[...]
 
 
 def flip_kernel(C, w_ref, out_ref):
@@ -368,8 +374,8 @@
 def turn_kernel(dm, *refs):
     q_ref = refs[0]
     x_refs = refs[1:1 + dm.slabs]
-    b_refs = refs[1 + dm.slabs:1 + 2 * dm.slabs]
-    xt_ref, bt_ref, xf = refs[1 + 2 * dm.slabs:]
+    b_refs = refs[1 + dm.slabs:1 + dm.slabs + dm.micro]
+    xt_ref, bt_ref, xf = refs[1 + dm.slabs + dm.micro:]
     C, size = dm.C, dm.own * dm.G
     cells = dm.slabs * size
     for e in range(dm.micro):
@@ -381,7 +387,7 @@
 
             @pl.when(q_ref[2] > dm.half)
             def _():
-                bt_ref[:, pl.ds(at, size)] = jnp.transpose(b_refs[block][...])
+                bt_ref[:, pl.ds(at, size)] = jnp.transpose(b_refs[e][r * size:(r + 1) * size, :])
 
     for kz in range(3):
         for ky in range(3):
@@ -396,8 +402,8 @@
 
 def weight_kernel(dm, *refs):
     q_ref, xt_ref, bt_ref = refs[:3]
-    blocks = refs[3:3 + dm.slabs]
-    grad_ref, mix_ref, head_ref, loss_ref, full, held, sums, sems = refs[3 + dm.slabs:]
+    ahead, behind = refs[3:3 + dm.slabs], refs[3 + dm.slabs:3 + 2 * dm.slabs]
+    grad_ref, mix_ref, head_ref, loss_ref, full, held, sums, sems = refs[3 + 2 * dm.slabs:]
     G, C, W = dm.G, dm.C, dm.W
     size = dm.own * G
     span = (W + 2) * G
@@ -406,15 +412,26 @@
         start = e * span
         full[start:start + G, :] = jnp.zeros((G, C), BF)
         full[start + (W + 1) * G:start + span, :] = jnp.zeros((G, C), BF)
-        for r in range(dm.parts):
-            block = blocks[e * dm.parts + r]
-            place = lax.rem(q_ref[0] + (dm.parts - r), dm.parts)
-            at = pl.multiple_of(start + G + place * size, 16)
-            full[pl.ds(at, size), :] = block[0:size, :]
-            carry = block[size:size + CARRY, :].astype(F32)
-            slot = lax.rem(q_ref[1] + (dm.micro - e), dm.micro) * dm.parts + place
-            used = dm.offs + 1
-            sums[slot, 0:used] = (carry[0:used] + carry[used:2 * used]) + carry[2 * used:3 * used]
+
+    def place_blocks(blocks):
+        for e in range(dm.micro):
+            for r in range(dm.parts):
+                block = blocks[e * dm.parts + r]
+                place = lax.rem(q_ref[0] + (dm.parts - r), dm.parts)
+                at = pl.multiple_of(e * span + G + place * size, 16)
+                full[pl.ds(at, size), :] = block[0:size, :]
+                carry = block[size:size + CARRY, :].astype(F32)
+                slot = lax.rem(q_ref[1] + (dm.micro - e), dm.micro) * dm.parts + place
+                used = dm.offs + 1
+                sums[slot, 0:used] = (carry[0:used] + carry[used:2 * used]) + carry[2 * used:3 * used]
+
+    @pl.when(q_ref[2] == 0)
+    def _():
+        place_blocks(behind)
+
+    @pl.when(q_ref[2] != 0)
+    def _():
+        place_blocks(ahead)
 
     def product(lhs_ref, row, count, kx):
         total = None
@@ -508,20 +525,23 @@
         pairs = [(p * micro + i, p * micro + (i + e) % micro) for p in range(parts) for i in range(micro)]
         return lax.ppermute(x, "slab", pairs)
 
-    def gather(block, lowest):
+    def along(x, pairs, first, last):
+        joint = [(s * slabs + i, s * slabs + j) for s in range(first, last) for i, j in pairs]
+        return lax.ppermute(x, ("section", "slab"), joint)
+
+    def turns(block, first, last):
         found = [block]
         for r in range(1, parts):
             pairs = [(p * micro + e, (p + r) % parts * micro + e) for p in range(parts) for e in range(micro)]
-            found.append(along(block, pairs, lowest))
-        blocks = list(found)
+            found.append(along(block, pairs, first, last))
+        return found
+
+    def swaps(blocks, first, last):
+        found = list(blocks)
         for e in range(1, micro):
             pairs = [(p * micro + i, p * micro + (i + e) % micro) for p in range(parts) for i in range(micro)]
-            blocks += [along(b, pairs, lowest) for b in found]
-        return blocks
-
-    def along(x, pairs, lowest):
-        joint = [(s * slabs + i, s * slabs + j) for s in range(lowest, n) for i, j in pairs]
-        return lax.ppermute(x, ("section", "slab"), joint)
+            found += [along(b, pairs, first, last) for b in blocks]
+        return found
 
     source = conv_weight[0].reshape(27 * C, C)
     held_hbm = pl.BlockSpec(memory_space=pltpu.HBM)
@@ -611,7 +631,11 @@
         first = dm.fwd(s) * G
         branch = jnp.where(section == s, mirrors[s][first:first + size], branch)
     branch, _ = lax.optimization_barrier((branch, results[0]))
-    branches = gather(branch, half + 1)
+    branches = call(
+        stack_kernel, [], turns(branch, half + 1, n),
+        [shape(parts * size, C, BF)], [], 1000,
+    )
+    branches = swaps(branches, half + 1, n)
     outs = [
         shape(dm.rows_of(t - 1) + CARRY, C, BF),
         shape(size + CARRY, C, BF),
@@ -629,7 +653,7 @@
     down = hop(results[0], t, t - 1)
     block, held = results[1], results[3]
     skip_grads = {0: hop(results[2], t, 0)}
-    held = gather(held, 0)
+    held = swaps(turns(held, 0, n), 0, n)
     cells_all = micro * W * G
 
     for t in range(n - 2, -1, -1):
@@ -652,6 +676,8 @@
             2 * dm.rows_of(max(t - 1, 0)) * 28 * C * C if t > 0 else 1000,
         )
         block = results[0]
+        if t == 1:
+            later = block
         if t > 0:
             down = hop(results[1], t, t - 1)
             if t > half:
@@ -665,12 +691,12 @@
         [pltpu.VMEM((cells_all + 2 * PAD, C), F32)],
         2 * 10 * cells_all * C * 100,
     )
-    near = [block] + [rotate(block, r) for r in range(1, parts)]
-    *far, xt = lax.optimization_barrier((*near[1:], xt))
-    near = [block] + far
-    blocks = list(near)
-    for e in range(1, micro):
-        blocks += [swap(b, e) for b in near]
+    ahead = turns(later, 1, n)
+    behind = turns(block, 0, 1)
+    *far, xt = lax.optimization_barrier((*ahead[1:], *behind[1:], xt))
+    ahead = swaps([later] + far[:parts - 1], 1, n)
+    behind = swaps([block] + far[parts - 1:], 0, 1)
+    blocks = ahead + behind
     operands = [xt, bt, *blocks]
     scratch = [
         pltpu.VMEM((micro * (W + 2) * G, C), BF),

time: 110 us -> 127 us (1.15)
  the two profiles are of different devices: /device:TPU:7 before, /device:TPU:0 now
where the time goes in v4:
time: 127 us; the launch traced here: 126 us
  waiting for transfers between devices  52.6 us (41%)
  starting transfers between devices  43 us (34%)
  Pallas kernels  24.8 us (20%)
  local copies, waits for them, and re-layouts  4.52 us (4%)
  between operations  1.37 us (1%)
    ppermute x8, waiting for transfers between devices, hop(): return lax.ppermute(x, 'section', [(source, target)])  40.6 us
    ppermute x25, starting transfers between devices, along(): return lax.ppermute(x, ('section', 'slab'), joint)  27.5 us
    pallas_call x13, Pallas kernels, call(): pl.pallas_call(kernel, out_shape=outs, in_specs=[scalar()] * len(scalars)...  12.6 us
    ppermute x25, waiting for transfers between devices, along(): return lax.ppermute(x, ('section', 'slab'), joint)  11 us
    pallas_call x1, Pallas kernels, body(): pl.pallas_call(functools.partial(weight_kernel, dm), name='weights', out_...  10.3 us
    ppermute x8, starting transfers between devices, hop(): return lax.ppermute(x, 'section', [(source, target)])  8.08 us
    ppermute x3, starting transfers between devices, rotate(): return lax.ppermute(x, 'slab', pairs)  6.9 us
    unnamed x12, local copies, waits for them, and re-layouts  4.5 us
  transfers between devices with their start and end apart: 37, of which 8 were waited for; matrix products, arithmetic and copies ran while one was open for 0% of the time, Pallas kernels for 7%

profile of v4, /device:TPU:0, one launch (start us, length us, event | category | flops | bytes accessed | tf_op | source)
XLA Modules:
  0.0 126.4 jit_solution(4943099480236971145)
XLA Ops:
  0.7 0.9 copy-done.2
  1.6 0.7 copy-done.3
  3.4 0.9 collective-permute-done.refs_1_
  4.9 3.0 %collective-permute-start.1 = (bf16[4,32,256]{2,1,0:T(8,128)(2,1)S(1)}, bf16[4,32,256]{2,1,0:T(8,128)(2,1)S(1)}, u32[]{:S(2)}, u32[]{:S(2)}) collective-permute-start(bf16[4,32,256]{2,1,0:T(8,128)(2,1)S(1)} %get-tuple-element.53), channel_id=1, source_target_pairs={{0,2},{1,3},{2,4},{3,5},{4,6},{5,7},{6,0},{7,1},{8,10},{9,11},{10,... | collective-permute-start | bytes 196616 | tf_op jit(solution)/shard_map/ppermute | solution.py:522
  7.9 2.6 %collective-permute-start.2 = (bf16[4,32,256]{2,1,0:T(8,128)(2,1)S(1)}, bf16[4,32,256]{2,1,0:T(8,128)(2,1)S(1)}, u32[]{:S(2)}, u32[]{:S(2)}) collective-permute-start(bf16[4,32,256]{2,1,0:T(8,128)(2,1)S(1)} %get-tuple-element.54), channel_id=1, source_target_pairs={{0,4},{1,5},{2,6},{3,7},{4,0},{5,1},{6,2},{7,3},{8,12},{9,13},{10,... | collective-permute-start | bytes 196616 | tf_op jit(solution)/shard_map/ppermute | solution.py:522
  10.5 1.3 %collective-permute-start.3 = (bf16[4,32,256]{2,1,0:T(8,128)(2,1)S(1)}, bf16[4,32,256]{2,1,0:T(8,128)(2,1)S(1)}, u32[]{:S(2)}, u32[]{:S(2)}) collective-permute-start(bf16[4,32,256]{2,1,0:T(8,128)(2,1)S(1)} %get-tuple-element.55), channel_id=1, source_target_pairs={{0,6},{1,7},{2,0},{3,1},{4,2},{5,3},{6,4},{7,5},{8,14},{9,15},{10,... | collective-permute-start | bytes 196616 | tf_op jit(solution)/shard_map/ppermute | solution.py:522
  11.9 2.0 %copy-done = bf16[1,3,3,3,256,256]{5,4,3,2,1,0:T(8,128)(2,1)S(1)} copy-done((bf16[1,3,3,3,256,256]{5,4,3,2,1,0:T(8,128)(2,1)S(1)}, bf16[1,3,3,3,256,256]{5,4,3,2,1,0:T(8,128)(2,1)}, u32[]{:S(2)}) %copy-start) | copy-done | bytes 3538968
  13.9 0.9 copy-done.1
  14.8 1.9 %load.1 = (bf16[6912,256]{1,0:T(8,128)(2,1)S(1)}, bf16[256,256]{1,0:T(8,128)(2,1)S(1)}) custom-call(bf16[6912,256]{1,0:T(8,128)(2,1)S(1)} %bitcast.14, bf16[256,256]{1,0:T(8,128)(2,1)S(1)} %bitcast.15), custom_call_target="tpu_custom_call" | custom-call | bytes 7077888 | tf_op jit(solution)/shard_map/load/pallas_call | solution.py:548
  16.7 2.5 %shard_map.95 = (bf16[448,256]{1,0:T(8,128)(2,1)S(1)}, f32[256,256]{1,0:T(8,128)S(1)}, bf16[256,256]{1,0:T(8,128)(2,1)S(1)}, bf16[352,256]{1,0:T(8,128)(2,1)S(1)}, f32[16,256]{1,0:T(8,128)S(1)}) custom-call(s32[3]{0:T(128)S(1)} %pad_add_fusion.me_ref.refs_0_, bf16[4,32,256]{2,1,0:T(8,128)(2,1)S(1)} %get-tuple-element.52.refs_1_, ...), custom_call_target="tpu_custom_call" | custom-call | flops 1644167168 | bytes 4751360 | tf_op jit(solution)/shard_map/pallas_call | solution.py:487
  19.3 1.5 %collective-permute-start.4 = (bf16[448,256]{1,0:T(8,128)(2,1)S(1)}, bf16[448,256]{1,0:T(8,128)(2,1)S(1)}, u32[]{:S(2)}, u32[]{:S(2)}) collective-permute-start(bf16[448,256]{1,0:T(8,128)(2,1)S(1)} %get-tuple-element.59), channel_id=1, source_target_pairs={{0,8},{1,9},{2,10},{3,11},{4,12},{5,13},{6,14},{7,15}} | collective-permute-start | bytes 688136 | tf_op jit(solution)/shard_map/ppermute | solution.py:518
  20.8 4.4 %collective-permute-done.4.refs_1_ = bf16[448,256]{1,0:T(8,128)(2,1)S(1)} collective-permute-done((bf16[448,256]{1,0:T(8,128)(2,1)S(1)}, bf16[448,256]{1,0:T(8,128)(2,1)S(1)}, u32[]{:S(2)}, u32[]{:S(2)}) %collective-permute-start.4) | collective-permute-done | bytes 229408 | tf_op jit(solution)/shard_map/ppermute | solution.py:518
  25.8 0.7 collective-permute-start.5
  27.0 0.7 collective-permute-start.6
  27.7 1.3 %collective-permute-start.7 = (bf16[352,256]{1,0:T(8,128)(2,1)S(1)}, bf16[352,256]{1,0:T(8,128)(2,1)S(1)}, u32[]{:S(2)}, u32[]{:S(2)}) collective-permute-start(bf16[352,256]{1,0:T(8,128)(2,1)S(1)} %get-tuple-element.65), channel_id=1, source_target_pairs={{0,24},{1,25},{2,26},{3,27},{4,28},{5,29},{6,30},{7,31}} | collective-permute-start | bytes 540680 | tf_op jit(solution)/shard_map/ppermute | solution.py:518
  29.0 0.8 shard_map.99.refs_8_
  29.8 1.0 shard_map.98.refs_6_.refs_4_
  30.8 1.2 collective-permute-done.7.refs_4_
  32.6 0.7 collective-permute-start.8
  33.3 0.7 collective-permute-start.27
  33.9 0.7 collective-permute-start.26
  34.6 0.7 collective-permute-start.25
  35.4 0.7 collective-permute-start.28
  36.7 0.7 collective-permute-start.9
  37.3 1.3 %collective-permute-start.14 = (bf16[256,256]{1,0:T(8,128)(2,1)S(1)}, bf16[256,256]{1,0:T(8,128)(2,1)S(1)}, u32[]{:S(2)}, u32[]{:S(2)}) collective-permute-start(bf16[256,256]{1,0:T(8,128)(2,1)S(1)} %get-tuple-element.79), channel_id=1, source_target_pairs={{24,0},{25,1},{26,2},{27,3},{28,4},{29,5},{30,6},{31,7}} | collective-permute-start | bytes 393224 | tf_op jit(solution)/shard_map/ppermute | solution.py:518
  38.7 0.7 shard_map.102
  39.5 1.3 %collective-permute-start.13 = (bf16[272,256]{1,0:T(8,128)(2,1)S(1)}, bf16[272,256]{1,0:T(8,128)(2,1)S(1)}, u32[]{:S(2)}, u32[]{:S(2)}) collective-permute-start(bf16[272,256]{1,0:T(8,128)(2,1)S(1)} %get-tuple-element.77), channel_id=1, source_target_pairs={{8,0},{9,1},{10,2},{11,3},{12,4},{13,5},{14,6},{15,7}} | collective-permute-start | bytes 417800 | tf_op jit(solution)/shard_map/ppermute | solution.py:518
  40.8 1.0 collective-permute-start.20
  41.8 35.0 %collective-permute-done.14.refs_4_ = bf16[256,256]{1,0:T(8,128)(2,1)S(1)} collective-permute-done((bf16[256,256]{1,0:T(8,128)(2,1)S(1)}, bf16[256,256]{1,0:T(8,128)(2,1)S(1)}, u32[]{:S(2)}, u32[]{:S(2)}) %collective-permute-start.14) | collective-permute-done | bytes 131104 | tf_op jit(solution)/shard_map/ppermute | solution.py:518
  77.0 0.7 collective-permute-start.18
  78.4 8.0 %collective-permute-done.19.refs_3_ = bf16[256,256]{1,0:T(8,128)(2,1)S(1)} collective-permute-done((bf16[256,256]{1,0:T(8,128)(2,1)S(1)}, bf16[256,256]{1,0:T(8,128)(2,1)S(1)}, u32[]{:S(2)}, u32[]{:S(2)}) %collective-permute-start.19) | collective-permute-done | bytes 131104 | tf_op jit(solution)/shard_map/ppermute | solution.py:530
  87.0 0.7 shard_map.103.refs_11_
  88.4 0.7 collective-permute-start.10
  89.1 2.7 %collective-permute-start.17 = (bf16[272,256]{1,0:T(8,128)(2,1)S(1)}, bf16[272,256]{1,0:T(8,128)(2,1)S(1)}, u32[]{:S(2)}, u32[]{:S(2)}) collective-permute-start(bf16[272,256]{1,0:T(8,128)(2,1)S(1)} %shard_map.103.refs_11_), channel_id=1, source_target_pairs={{0,6},{1,7},{2,0},{3,1},{4,2},{5,3},{6,4},{7,5}} | collective-permute-start | bytes 417800 | tf_op jit(solution)/shard_map/ppermute | solution.py:530
  91.8 2.8 %collective-permute-start.16 = (bf16[272,256]{1,0:T(8,128)(2,1)S(1)}, bf16[272,256]{1,0:T(8,128)(2,1)S(1)}, u32[]{:S(2)}, u32[]{:S(2)}) collective-permute-start(bf16[272,256]{1,0:T(8,128)(2,1)S(1)} %shard_map.103.refs_11_), channel_id=1, source_target_pairs={{0,4},{1,5},{2,6},{3,7},{4,0},{5,1},{6,2},{7,3}} | collective-permute-start | bytes 417800 | tf_op jit(solution)/shard_map/ppermute | solution.py:530
  94.6 3.9 %collective-permute-start.15 = (bf16[272,256]{1,0:T(8,128)(2,1)S(1)}, bf16[272,256]{1,0:T(8,128)(2,1)S(1)}, u32[]{:S(2)}, u32[]{:S(2)}) collective-permute-start(bf16[272,256]{1,0:T(8,128)(2,1)S(1)} %shard_map.103.refs_11_), channel_id=1, source_target_pairs={{0,2},{1,3},{2,4},{3,5},{4,6},{5,7},{6,0},{7,1}} | collective-permute-start | bytes 417800 | tf_op jit(solution)/shard_map/ppermute | solution.py:530
  98.5 3.4 %shard_map.105 = (bf16[2304,2048]{1,0:T(8,128)(2,1)S(1)}, bf16[256,2048]{1,0:T(8,128)(2,1)S(1)}) custom-call(s32[3]{0:T(128)S(1)} %pad_add_fusion.me_ref.refs_0_, bf16[256,256]{1,0:T(8,128)(2,1)S(1)} %get-tuple-element.81.refs_1_, bf16[256,256]{1,0:T(8,128)(2,1)S(1)} %collective-permute-done.18.refs_2_, ...), custom_call_target="tpu_custom_call" | custom-call | flops 1048576000 | bytes 12582912 | tf_op jit(solution)/shard_map/pallas_call | solution.py:487
  102.0 0.7 collective-permute-start.29
  102.7 1.9 %collective-permute-start.33 = (bf16[272,256]{1,0:T(8,128)(2,1)S(1)}, bf16[272,256]{1,0:T(8,128)(2,1)S(1)}, u32[]{:S(2)}, u32[]{:S(2)}) collective-permute-start(bf16[272,256]{1,0:T(8,128)(2,1)S(1)} %shard_map.103.refs_11_), channel_id=1, source_target_pairs={{0,1},{1,0},{2,3},{3,2},{4,5},{5,4},{6,7},{7,6}} | collective-permute-start | bytes 417800 | tf_op jit(solution)/shard_map/ppermute | solution.py:530
  104.6 1.7 %collective-permute-done.16.refs_13_ = bf16[272,256]{1,0:T(8,128)(2,1)S(1)} collective-permute-done((bf16[272,256]{1,0:T(8,128)(2,1)S(1)}, bf16[272,256]{1,0:T(8,128)(2,1)S(1)}, u32[]{:S(2)}, u32[]{:S(2)}) %collective-permute-start.16) | collective-permute-done | bytes 139296 | tf_op jit(solution)/shard_map/ppermute | solution.py:530
  106.3 0.7 collective-permute-start.30
  106.9 0.7 collective-permute-start.31
  107.6 0.7 collective-permute-start.32
  108.3 1.9 %collective-permute-start.34 = (bf16[272,256]{1,0:T(8,128)(2,1)S(1)}, bf16[272,256]{1,0:T(8,128)(2,1)S(1)}, u32[]{:S(2)}, u32[]{:S(2)}) collective-permute-start(bf16[272,256]{1,0:T(8,128)(2,1)S(1)} %collective-permute-done.15.refs_12_), channel_id=1, source_target_pairs={{0,1},{1,0},{2,3},{3,2},{4,5},{5,4},{6,7},{7,6}} | collective-permute-start | bytes 417800 | tf_op jit(solution)/shard_map/ppermute | solution.py:530
  110.2 2.4 %collective-permute-start.35 = (bf16[272,256]{1,0:T(8,128)(2,1)S(1)}, bf16[272,256]{1,0:T(8,128)(2,1)S(1)}, u32[]{:S(2)}, u32[]{:S(2)}) collective-permute-start(bf16[272,256]{1,0:T(8,128)(2,1)S(1)} %collective-permute-done.16.refs_13_), channel_id=1, source_target_pairs={{0,1},{1,0},{2,3},{3,2},{4,5},{5,4},{6,7},{7,6}} | collective-permute-start | bytes 417800 | tf_op jit(solution)/shard_map/ppermute | solution.py:530
  112.7 1.9 %collective-permute-start.36 = (bf16[272,256]{1,0:T(8,128)(2,1)S(1)}, bf16[272,256]{1,0:T(8,128)(2,1)S(1)}, u32[]{:S(2)}, u32[]{:S(2)}) collective-permute-start(bf16[272,256]{1,0:T(8,128)(2,1)S(1)} %collective-permute-done.17.refs_14_), channel_id=1, source_target_pairs={{0,1},{1,0},{2,3},{3,2},{4,5},{5,4},{6,7},{7,6}} | collective-permute-start | bytes 417800 | tf_op jit(solution)/shard_map/ppermute | solution.py:530
  114.6 1.3 %collective-permute-done.36.refs_18_ = bf16[272,256]{1,0:T(8,128)(2,1)S(1)} collective-permute-done((bf16[272,256]{1,0:T(8,128)(2,1)S(1)}, bf16[272,256]{1,0:T(8,128)(2,1)S(1)}, u32[]{:S(2)}, u32[]{:S(2)}) %collective-permute-start.36) | collective-permute-done | bytes 139296 | tf_op jit(solution)/shard_map/ppermute | solution.py:530
  115.9 10.3 %weights.1 = (f32[9,3,256,256]{3,2,1,0:T(8,128)}, f32[256,256]{1,0:T(8,128)}, f32[3,256]{1,0:T(4,128)}, f32[1,1]{1,0:T(1,128)}) custom-call(s32[3]{0:T(128)S(1)} %pad_add_fusion.me_ref.refs_0_, bf16[2304,2048]{1,0:T(8,128)(2,1)S(1)} %get-tuple-element.84.refs_1_, bf16[256,2048]{1,0:T(8,128)(2,1)S(1)} %get-tuple-element.85.refs_2_, ...), custom_call_target="tpu_custom_call" | custom-call | flops 7516192768 | bytes 20057092 | tf_op jit(solution)/shard_map/weights/pallas_call | solution.py:714
  (56 shorter events, 6.4 us)
Async XLA Ops:
  0.7 0.9 copy-start.2
  1.6 0.7 copy-start.3
  2.9 1.5 %collective-permute-start = (bf16[144,256]{1,0:T(8,128)(2,1)S(1)}, bf16[144,256]{1,0:T(8,128)(2,1)S(1)}, u32[]{:S(2)}, u32[]{:S(2)}) collective-permute-start(bf16[144,256]{1,0:T(8,128)(2,1)S(1)} %get-tuple-element.51), channel_id=1, source_target_pairs={{0,1},{1,0},{2,3},{3,2},{4,5},{5,4},{6,7},{7,6},{8,9},{9,8},{10,11... | collective-permute-start | bytes 221192 | tf_op jit(solution)/shard_map/ppermute | solution.py:526
  4.9 11.8 %collective-permute-start.1 = (bf16[4,32,256]{2,1,0:T(8,128)(2,1)S(1)}, bf16[4,32,256]{2,1,0:T(8,128)(2,1)S(1)}, u32[]{:S(2)}, u32[]{:S(2)}) collective-permute-start(bf16[4,32,256]{2,1,0:T(8,128)(2,1)S(1)} %get-tuple-element.53), channel_id=1, source_target_pairs={{0,2},{1,3},{2,4},{3,5},{4,6},{5,7},{6,0},{7,1},{8,10},{9,11},{10,... | collective-permute-start | bytes 196616 | tf_op jit(solution)/shard_map/ppermute | solution.py:522
  7.9 8.8 %collective-permute-start.2 = (bf16[4,32,256]{2,1,0:T(8,128)(2,1)S(1)}, bf16[4,32,256]{2,1,0:T(8,128)(2,1)S(1)}, u32[]{:S(2)}, u32[]{:S(2)}) collective-permute-start(bf16[4,32,256]{2,1,0:T(8,128)(2,1)S(1)} %get-tuple-element.54), channel_id=1, source_target_pairs={{0,4},{1,5},{2,6},{3,7},{4,0},{5,1},{6,2},{7,3},{8,12},{9,13},{10,... | collective-permute-start | bytes 196616 | tf_op jit(solution)/shard_map/ppermute | solution.py:522
  10.5 6.2 %collective-permute-start.3 = (bf16[4,32,256]{2,1,0:T(8,128)(2,1)S(1)}, bf16[4,32,256]{2,1,0:T(8,128)(2,1)S(1)}, u32[]{:S(2)}, u32[]{:S(2)}) collective-permute-start(bf16[4,32,256]{2,1,0:T(8,128)(2,1)S(1)} %get-tuple-element.55), channel_id=1, source_target_pairs={{0,6},{1,7},{2,0},{3,1},{4,2},{5,3},{6,4},{7,5},{8,14},{9,15},{10,... | collective-permute-start | bytes 196616 | tf_op jit(solution)/shard_map/ppermute | solution.py:522
  11.9 2.0 %copy-start = (bf16[1,3,3,3,256,256]{5,4,3,2,1,0:T(8,128)(2,1)S(1)}, bf16[1,3,3,3,256,256]{5,4,3,2,1,0:T(8,128)(2,1)}, u32[]{:S(2)}) copy-start(bf16[1,3,3,3,256,256]{5,4,3,2,1,0:T(8,128)(2,1)} %param.9) | copy-start | bytes 10616836
  13.9 0.9 copy-start.1
  19.3 5.9 %collective-permute-start.4 = (bf16[448,256]{1,0:T(8,128)(2,1)S(1)}, bf16[448,256]{1,0:T(8,128)(2,1)S(1)}, u32[]{:S(2)}, u32[]{:S(2)}) collective-permute-start(bf16[448,256]{1,0:T(8,128)(2,1)S(1)} %get-tuple-element.59), channel_id=1, source_target_pairs={{0,8},{1,9},{2,10},{3,11},{4,12},{5,13},{6,14},{7,15}} | collective-permute-start | bytes 688136 | tf_op jit(solution)/shard_map/ppermute | solution.py:518
  25.7 3.3 %copy-start.5 = (bf16[256,3]{0,1:T(4,128)(2,1)S(1)}, bf16[256,3]{0,1:T(4,128)(2,1)}, u32[]{:S(2)}) copy-start(bf16[256,3]{0,1:T(4,128)(2,1)} %param.11) | copy-start | bytes 4612
  25.7 3.3 %copy-start.4 = (s32[3,3]{1,0:T(4,128)S(1)}, s32[3,3]{1,0:T(4,128)}, u32[]{:S(2)}) copy-start(s32[3,3]{1,0:T(4,128)} %off_ref.1) | copy-start | bytes 112
  25.8 0.7 collective-permute-start.5
  27.0 5.0 %collective-permute-start.6 = (bf16[384,256]{1,0:T(8,128)(2,1)S(1)}, bf16[384,256]{1,0:T(8,128)(2,1)S(1)}, u32[]{:S(2)}, u32[]{:S(2)}) collective-permute-start(bf16[384,256]{1,0:T(8,128)(2,1)S(1)} %get-tuple-element.64), channel_id=1, source_target_pairs={{16,24},{17,25},{18,26},{19,27},{20,28},{21,29},{22,30},{23,31}} | collective-permute-start | bytes 589832 | tf_op jit(solution)/shard_map/ppermute | solution.py:518
  27.7 4.3 %collective-permute-start.7 = (bf16[352,256]{1,0:T(8,128)(2,1)S(1)}, bf16[352,256]{1,0:T(8,128)(2,1)S(1)}, u32[]{:S(2)}, u32[]{:S(2)}) collective-permute-start(bf16[352,256]{1,0:T(8,128)(2,1)S(1)} %get-tuple-element.65), channel_id=1, source_target_pairs={{0,24},{1,25},{2,26},{3,27},{4,28},{5,29},{6,30},{7,31}} | collective-permute-start | bytes 540680 | tf_op jit(solution)/shard_map/ppermute | solution.py:518
  32.6 3.5 %collective-permute-start.8 = (bf16[336,256]{1,0:T(8,128)(2,1)S(1)}, bf16[336,256]{1,0:T(8,128)(2,1)S(1)}, u32[]{:S(2)}, u32[]{:S(2)}) collective-permute-start(bf16[336,256]{1,0:T(8,128)(2,1)S(1)} %get-tuple-element.70), channel_id=1, source_target_pairs={{24,16},{25,17},{26,18},{27,19},{28,20},{29,21},{30,22},{31,23}} | collective-permute-start | bytes 516104 | tf_op jit(solution)/shard_map/ppermute | solution.py:518
  33.3 2.0 %collective-permute-start.27 = (bf16[256,256]{1,0:T(8,128)(2,1)S(1)}, bf16[256,256]{1,0:T(8,128)(2,1)S(1)}, u32[]{:S(2)}, u32[]{:S(2)}) collective-permute-start(bf16[256,256]{1,0:T(8,128)(2,1)S(1)} %slice.4.refs_0_), channel_id=1, source_target_pairs={{24,30},{25,31},{26,24},{27,25},{28,26},{29,27},{30,28},{31,29}} | collective-permute-start | bytes 393224 | tf_op jit(solution)/shard_map/ppermute | solution.py:530
  33.9 1.4 %collective-permute-start.26 = (bf16[256,256]{1,0:T(8,128)(2,1)S(1)}, bf16[256,256]{1,0:T(8,128)(2,1)S(1)}, u32[]{:S(2)}, u32[]{:S(2)}) collective-permute-start(bf16[256,256]{1,0:T(8,128)(2,1)S(1)} %slice.4.refs_0_), channel_id=1, source_target_pairs={{24,28},{25,29},{26,30},{27,31},{28,24},{29,25},{30,26},{31,27}} | collective-permute-start | bytes 393224 | tf_op jit(solution)/shard_map/ppermute | solution.py:530
  34.6 0.7 collective-permute-start.25
  35.4 56.4 %collective-permute-start.28 = (bf16[1024,256]{1,0:T(8,128)(2,1)S(1)}, bf16[1024,256]{1,0:T(8,128)(2,1)S(1)}, u32[]{:S(2)}, u32[]{:S(2)}) collective-permute-start(bf16[1024,256]{1,0:T(8,128)(2,1)S(1)} %shard_map.104.refs_9_), channel_id=1, source_target_pairs={{24,25},{25,24},{26,27},{27,26},{28,29},{29,28},{30,31},{31,30}} | collective-permute-start | bytes 1572872 | tf_op jit(solution)/shard_map/ppermute | solution.py:530
  36.7 2.1 %collective-permute-start.9 = (bf16[304,256]{1,0:T(8,128)(2,1)S(1)}, bf16[304,256]{1,0:T(8,128)(2,1)S(1)}, u32[]{:S(2)}, u32[]{:S(2)}) collective-permute-start(bf16[304,256]{1,0:T(8,128)(2,1)S(1)} %get-tuple-element.73), channel_id=1, source_target_pairs={{16,8},{17,9},{18,10},{19,11},{20,12},{21,13},{22,14},{23,15}} | collective-permute-start | bytes 466952 | tf_op jit(solution)/shard_map/ppermute | solution.py:518
  37.3 39.5 %collective-permute-start.14 = (bf16[256,256]{1,0:T(8,128)(2,1)S(1)}, bf16[256,256]{1,0:T(8,128)(2,1)S(1)}, u32[]{:S(2)}, u32[]{:S(2)}) collective-permute-start(bf16[256,256]{1,0:T(8,128)(2,1)S(1)} %get-tuple-element.79), channel_id=1, source_target_pairs={{24,0},{25,1},{26,2},{27,3},{28,4},{29,5},{30,6},{31,7}} | collective-permute-start | bytes 393224 | tf_op jit(solution)/shard_map/ppermute | solution.py:518
  38.6 38.4 %collective-permute-start.21 = (bf16[256,256]{1,0:T(8,128)(2,1)S(1)}, bf16[256,256]{1,0:T(8,128)(2,1)S(1)}, u32[]{:S(2)}, u32[]{:S(2)}) collective-permute-start(bf16[256,256]{1,0:T(8,128)(2,1)S(1)} %get-tuple-element.81.refs_1_), channel_id=1, source_target_pairs={{0,1},{1,0},{2,3},{3,2},{4,5},{5,4},{6,7},{7,6},{8,9},{9,8},{10,11... | collective-permute-start | bytes 393224 | tf_op jit(solution)/shard_map/ppermute | solution.py:530
  39.5 47.4 %collective-permute-start.13 = (bf16[272,256]{1,0:T(8,128)(2,1)S(1)}, bf16[272,256]{1,0:T(8,128)(2,1)S(1)}, u32[]{:S(2)}, u32[]{:S(2)}) collective-permute-start(bf16[272,256]{1,0:T(8,128)(2,1)S(1)} %get-tuple-element.77), channel_id=1, source_target_pairs={{8,0},{9,1},{10,2},{11,3},{12,4},{13,5},{14,6},{15,7}} | collective-permute-start | bytes 417800 | tf_op jit(solution)/shard_map/ppermute | solution.py:518
  40.8 37.0 %collective-permute-start.20 = (bf16[256,256]{1,0:T(8,128)(2,1)S(1)}, bf16[256,256]{1,0:T(8,128)(2,1)S(1)}, u32[]{:S(2)}, u32[]{:S(2)}) collective-permute-start(bf16[256,256]{1,0:T(8,128)(2,1)S(1)} %get-tuple-element.81.refs_1_), channel_id=1, source_target_pairs={{0,6},{1,7},{2,0},{3,1},{4,2},{5,3},{6,4},{7,5},{8,14},{9,15},{10,... | collective-permute-start | bytes 393224 | tf_op jit(solution)/shard_map/ppermute | solution.py:530
  76.8 9.5 %collective-permute-start.19 = (bf16[256,256]{1,0:T(8,128)(2,1)S(1)}, bf16[256,256]{1,0:T(8,128)(2,1)S(1)}, u32[]{:S(2)}, u32[]{:S(2)}) collective-permute-start(bf16[256,256]{1,0:T(8,128)(2,1)S(1)} %get-tuple-element.81.refs_1_), channel_id=1, source_target_pairs={{0,4},{1,5},{2,6},{3,7},{4,0},{5,1},{6,2},{7,3},{8,12},{9,13},{10,... | collective-permute-start | bytes 393224 | tf_op jit(solution)/shard_map/ppermute | solution.py:530
  77.0 9.4 %collective-permute-start.18 = (bf16[256,256]{1,0:T(8,128)(2,1)S(1)}, bf16[256,256]{1,0:T(8,128)(2,1)S(1)}, u32[]{:S(2)}, u32[]{:S(2)}) collective-permute-start(bf16[256,256]{1,0:T(8,128)(2,1)S(1)} %get-tuple-element.81.refs_1_), channel_id=1, source_target_pairs={{0,2},{1,3},{2,4},{3,5},{4,6},{5,7},{6,0},{7,1},{8,10},{9,11},{10,... | collective-permute-start | bytes 393224 | tf_op jit(solution)/shard_map/ppermute | solution.py:530
  77.8 16.8 %collective-permute-start.12 = (bf16[272,256]{1,0:T(8,128)(2,1)S(1)}, bf16[272,256]{1,0:T(8,128)(2,1)S(1)}, u32[]{:S(2)}, u32[]{:S(2)}) collective-permute-start(bf16[272,256]{1,0:T(8,128)(2,1)S(1)} %get-tuple-element.76.refs_3_), channel_id=1, source_target_pairs={{8,14},{9,15},{10,8},{11,9},{12,10},{13,11},{14,12},{15,13},{16,22... | collective-permute-start | bytes 417800 | tf_op jit(solution)/shard_map/ppermute | solution.py:530
  86.4 1.3 %collective-permute-start.24 = (bf16[256,256]{1,0:T(8,128)(2,1)S(1)}, bf16[256,256]{1,0:T(8,128)(2,1)S(1)}, u32[]{:S(2)}, u32[]{:S(2)}) collective-permute-start(bf16[256,256]{1,0:T(8,128)(2,1)S(1)} %collective-permute-done.20.refs_4_), channel_id=1, source_target_pairs={{0,1},{1,0},{2,3},{3,2},{4,5},{5,4},{6,7},{7,6},{8,9},{9,8},{10,11... | collective-permute-start | bytes 393224 | tf_op jit(solution)/shard_map/ppermute | solution.py:530
  86.4 2.0 %collective-permute-start.23 = (bf16[256,256]{1,0:T(8,128)(2,1)S(1)}, bf16[256,256]{1,0:T(8,128)(2,1)S(1)}, u32[]{:S(2)}, u32[]{:S(2)}) collective-permute-start(bf16[256,256]{1,0:T(8,128)(2,1)S(1)} %collective-permute-done.19.refs_3_), channel_id=1, source_target_pairs={{0,1},{1,0},{2,3},{3,2},{4,5},{5,4},{6,7},{7,6},{8,9},{9,8},{10,11... | collective-permute-start | bytes 393224 | tf_op jit(solution)/shard_map/ppermute | solution.py:530
  86.9 2.2 %collective-permute-start.22 = (bf16[256,256]{1,0:T(8,128)(2,1)S(1)}, bf16[256,256]{1,0:T(8,128)(2,1)S(1)}, u32[]{:S(2)}, u32[]{:S(2)}) collective-permute-start(bf16[256,256]{1,0:T(8,128)(2,1)S(1)} %collective-permute-done.18.refs_2_), channel_id=1, source_target_pairs={{0,1},{1,0},{2,3},{3,2},{4,5},{5,4},{6,7},{7,6},{8,9},{9,8},{10,11... | collective-permute-start | bytes 393224 | tf_op jit(solution)/shard_map/ppermute | solution.py:530
  87.7 14.2 %collective-permute-start.11 = (bf16[272,256]{1,0:T(8,128)(2,1)S(1)}, bf16[272,256]{1,0:T(8,128)(2,1)S(1)}, u32[]{:S(2)}, u32[]{:S(2)}) collective-permute-start(bf16[272,256]{1,0:T(8,128)(2,1)S(1)} %get-tuple-element.76.refs_3_), channel_id=1, source_target_pairs={{8,12},{9,13},{10,14},{11,15},{12,8},{13,9},{14,10},{15,11},{16,20... | collective-permute-start | bytes 417800 | tf_op jit(solution)/shard_map/ppermute | solution.py:530
  88.4 14.2 %collective-permute-start.10 = (bf16[272,256]{1,0:T(8,128)(2,1)S(1)}, bf16[272,256]{1,0:T(8,128)(2,1)S(1)}, u32[]{:S(2)}, u32[]{:S(2)}) collective-permute-start(bf16[272,256]{1,0:T(8,128)(2,1)S(1)} %get-tuple-element.76.refs_3_), channel_id=1, source_target_pairs={{8,10},{9,11},{10,12},{11,13},{12,14},{13,15},{14,8},{15,9},{16,18... | collective-permute-start | bytes 417800 | tf_op jit(solution)/shard_map/ppermute | solution.py:530
  89.1 15.5 %collective-permute-start.17 = (bf16[272,256]{1,0:T(8,128)(2,1)S(1)}, bf16[272,256]{1,0:T(8,128)(2,1)S(1)}, u32[]{:S(2)}, u32[]{:S(2)}) collective-permute-start(bf16[272,256]{1,0:T(8,128)(2,1)S(1)} %shard_map.103.refs_11_), channel_id=1, source_target_pairs={{0,6},{1,7},{2,0},{3,1},{4,2},{5,3},{6,4},{7,5}} | collective-permute-start | bytes 417800 | tf_op jit(solution)/shard_map/ppermute | solution.py:530
  91.8 14.5 %collective-permute-start.16 = (bf16[272,256]{1,0:T(8,128)(2,1)S(1)}, bf16[272,256]{1,0:T(8,128)(2,1)S(1)}, u32[]{:S(2)}, u32[]{:S(2)}) collective-permute-start(bf16[272,256]{1,0:T(8,128)(2,1)S(1)} %shard_map.103.refs_11_), channel_id=1, source_target_pairs={{0,4},{1,5},{2,6},{3,7},{4,0},{5,1},{6,2},{7,3}} | collective-permute-start | bytes 417800 | tf_op jit(solution)/shard_map/ppermute | solution.py:530
  94.6 11.7 %collective-permute-start.15 = (bf16[272,256]{1,0:T(8,128)(2,1)S(1)}, bf16[272,256]{1,0:T(8,128)(2,1)S(1)}, u32[]{:S(2)}, u32[]{:S(2)}) collective-permute-start(bf16[272,256]{1,0:T(8,128)(2,1)S(1)} %shard_map.103.refs_11_), channel_id=1, source_target_pairs={{0,2},{1,3},{2,4},{3,5},{4,6},{5,7},{6,0},{7,1}} | collective-permute-start | bytes 417800 | tf_op jit(solution)/shard_map/ppermute | solution.py:530
  102.0 6.3 %collective-permute-start.29 = (bf16[272,256]{1,0:T(8,128)(2,1)S(1)}, bf16[272,256]{1,0:T(8,128)(2,1)S(1)}, u32[]{:S(2)}, u32[]{:S(2)}) collective-permute-start(bf16[272,256]{1,0:T(8,128)(2,1)S(1)} %get-tuple-element.76.refs_3_), channel_id=1, source_target_pairs={{8,9},{9,8},{10,11},{11,10},{12,13},{13,12},{14,15},{15,14},{16,17... | collective-permute-start | bytes 417800 | tf_op jit(solution)/shard_map/ppermute | solution.py:530
  102.7 7.6 %collective-permute-start.33 = (bf16[272,256]{1,0:T(8,128)(2,1)S(1)}, bf16[272,256]{1,0:T(8,128)(2,1)S(1)}, u32[]{:S(2)}, u32[]{:S(2)}) collective-permute-start(bf16[272,256]{1,0:T(8,128)(2,1)S(1)} %shard_map.103.refs_11_), channel_id=1, source_target_pairs={{0,1},{1,0},{2,3},{3,2},{4,5},{5,4},{6,7},{7,6}} | collective-permute-start | bytes 417800 | tf_op jit(solution)/shard_map/ppermute | solution.py:530
  106.3 6.4 %collective-permute-start.30 = (bf16[272,256]{1,0:T(8,128)(2,1)S(1)}, bf16[272,256]{1,0:T(8,128)(2,1)S(1)}, u32[]{:S(2)}, u32[]{:S(2)}) collective-permute-start(bf16[272,256]{1,0:T(8,128)(2,1)S(1)} %collective-permute-done.10.refs_4_), channel_id=1, source_target_pairs={{8,9},{9,8},{10,11},{11,10},{12,13},{13,12},{14,15},{15,14},{16,17... | collective-permute-start | bytes 417800 | tf_op jit(solution)/shard_map/ppermute | solution.py:530
  106.9 7.7 %collective-permute-start.31 = (bf16[272,256]{1,0:T(8,128)(2,1)S(1)}, bf16[272,256]{1,0:T(8,128)(2,1)S(1)}, u32[]{:S(2)}, u32[]{:S(2)}) collective-permute-start(bf16[272,256]{1,0:T(8,128)(2,1)S(1)} %collective-permute-done.11.refs_5_), channel_id=1, source_target_pairs={{8,9},{9,8},{10,11},{11,10},{12,13},{13,12},{14,15},{15,14},{16,17... | collective-permute-start | bytes 417800 | tf_op jit(solution)/shard_map/ppermute | solution.py:530
  107.6 7.0 %collective-permute-start.32 = (bf16[272,256]{1,0:T(8,128)(2,1)S(1)}, bf16[272,256]{1,0:T(8,128)(2,1)S(1)}, u32[]{:S(2)}, u32[]{:S(2)}) collective-permute-start(bf16[272,256]{1,0:T(8,128)(2,1)S(1)} %collective-permute-done.12.refs_6_), channel_id=1, source_target_pairs={{8,9},{9,8},{10,11},{11,10},{12,13},{13,12},{14,15},{15,14},{16,17... | collective-permute-start | bytes 417800 | tf_op jit(solution)/shard_map/ppermute | solution.py:530
  108.3 6.3 %collective-permute-start.34 = (bf16[272,256]{1,0:T(8,128)(2,1)S(1)}, bf16[272,256]{1,0:T(8,128)(2,1)S(1)}, u32[]{:S(2)}, u32[]{:S(2)}) collective-permute-start(bf16[272,256]{1,0:T(8,128)(2,1)S(1)} %collective-permute-done.15.refs_12_), channel_id=1, source_target_pairs={{0,1},{1,0},{2,3},{3,2},{4,5},{5,4},{6,7},{7,6}} | collective-permute-start | bytes 417800 | tf_op jit(solution)/shard_map/ppermute | solution.py:530
  110.2 4.4 %collective-permute-start.35 = (bf16[272,256]{1,0:T(8,128)(2,1)S(1)}, bf16[272,256]{1,0:T(8,128)(2,1)S(1)}, u32[]{:S(2)}, u32[]{:S(2)}) collective-permute-start(bf16[272,256]{1,0:T(8,128)(2,1)S(1)} %collective-permute-done.16.refs_13_), channel_id=1, source_target_pairs={{0,1},{1,0},{2,3},{3,2},{4,5},{5,4},{6,7},{7,6}} | collective-permute-start | bytes 417800 | tf_op jit(solution)/shard_map/ppermute | solution.py:530
  112.7 3.3 %collective-permute-start.36 = (bf16[272,256]{1,0:T(8,128)(2,1)S(1)}, bf16[272,256]{1,0:T(8,128)(2,1)S(1)}, u32[]{:S(2)}, u32[]{:S(2)}) collective-permute-start(bf16[272,256]{1,0:T(8,128)(2,1)S(1)} %collective-permute-done.17.refs_14_), channel_id=1, source_target_pairs={{0,1},{1,0},{2,3},{3,2},{4,5},{5,4},{6,7},{7,6}} | collective-permute-start | bytes 417800 | tf_op jit(solution)/shard_map/ppermute | solution.py:530

commit v5 on v3

--- a/solution.py
+++ b/solution.py
@@ -91,21 +91,23 @@
     return dot(x27[0:ro, :], w_ref[...]) + dot(branch, b_ref[...])
 
 
-def silu_masked(dm, base, k, pre):
+def logistic(value):
+    return 1.0 / (1.0 + jnp.exp(-value))
+
+
+def inside(dm, base, k, value):
     width = dm.own + 2 * k
-    value = pre * (1.0 / (1.0 + jnp.exp(-pre)))
     value = value.reshape(width, dm.G, dm.C)
     value = jnp.where(column_mask(dm, base, k, width), value, 0.0)
     return value.reshape(width * dm.G, dm.C).astype(BF)
 
 
-def pre_gradient(dm, base, k, upstream, pre):
-    width = dm.own + 2 * k
-    sig = 1.0 / (1.0 + jnp.exp(-pre))
-    value = upstream * (sig * (1.0 + pre * (1.0 - sig)))
-    value = value.reshape(width, dm.G, dm.C)
-    value = jnp.where(column_mask(dm, base, k, width), value, 0.0)
-    return value.reshape(width * dm.G, dm.C).astype(BF)
+def silu_masked(dm, base, k, pre, sig):
+    return inside(dm, base, k, pre * sig)
+
+
+def pre_gradient(dm, base, k, upstream, pre, sig):
+    return inside(dm, base, k, upstream * (sig * (1.0 + pre * (1.0 - sig))))
 
 
 def forward_kernel(dm, t, has_skip_in, has_mirror, *refs):
@@ -151,7 +153,7 @@
         pre = preact(dm, t, xf, x27, skip_ref, w_ref, b_ref)
         first = (k - t) * dm.G
         pre_ref[...] = pre[first:first + dm.rows_of(t)]
-        y = silu_masked(dm, base, k, pre)
+        y = silu_masked(dm, base, k, pre, logistic(pre))
         y_ref[...] = y
         if has_mirror:
             keep = dm.fwd(dm.sections - 1 - t)
@@ -205,17 +207,9 @@
     xf[PAD:PAD + rows, :] = cells[0:rows]
 
 
-def load_kernel(chunks, w_ref, b_ref, out_ref, out_b_ref, sems):
-    rows = w_ref.shape[0] // chunks
-    copies = []
-    for i in range(chunks):
-        part = pl.ds(i * rows, rows)
-        copies.append(pltpu.make_async_copy(w_ref.at[part], out_ref.at[part], sems.at[i]))
-        copies[i].start()
-    copies.append(pltpu.make_async_copy(b_ref, out_b_ref, sems.at[chunks]))
-    copies[chunks].start()
-    for copy in copies:
-        copy.wait()
+def load_kernel(w_ref, b_ref, out_ref, out_b_ref):
+    out_ref[...] = w_ref[...]
+    out_b_ref[...] = b_ref[...]
 
 
 def flip_kernel(C, w_ref, out_ref):
@@ -283,7 +277,8 @@
         own_ref[...] = x_ref[mid + G:mid + G + size, :]
         stage(xf, x_ref[...], dm.rows_of(t + 1))
         pre = preact(dm, t, xf, x27, skip_ref, w_ref, b_ref)
-        y = silu_masked(dm, base, t, pre)
+        gate = logistic(pre)
+        y = silu_masked(dm, base, t, pre, gate)
         logits = dot_nt(head_ref[...], y)
         target = target_ref[...]
         live = lax.broadcasted_iota(jnp.int32, logits.shape, 0) < dm.offs
@@ -304,7 +299,7 @@
             rest = rest - piece
         carry = lines[...].astype(BF)
         upstream = dot_tn(lg, head_ref[...])
-        pg = pre_gradient(dm, base, t, upstream, pre)
+        pg = pre_gradient(dm, base, t, upstream, pre, gate)
         pgx_ref[0:size, :] = pg[mid:mid + size]
         pgx_ref[size:size + CARRY, :] = carry
         back_conv(dm, t, pg, xf, x27, wt_ref, b_ref, msg_ref)
@@ -346,7 +341,8 @@
         upstream = down_ref[0:ro, :].astype(F32)
         if has_skip_in:
             upstream = upstream + skip_ref[0:ro, :].astype(F32)
-        pg = pre_gradient(dm, base, t, upstream, pre_ref[...])
+        pre = pre_ref[...]
+        pg = pre_gradient(dm, base, t, upstream, pre, logistic(pre))
         mid, size = t * dm.G, dm.own * dm.G
         carry = down_ref[ro:ro + CARRY, :]
         pgx_ref[0:size, :] = pg[mid:mid + size]
@@ -524,17 +520,10 @@
         return lax.ppermute(x, ("section", "slab"), joint)
 
     source = conv_weight[0].reshape(27 * C, C)
-    held_hbm = pl.BlockSpec(memory_space=pltpu.HBM)
-    kernel, mixing = pl.pallas_call(
-        functools.partial(load_kernel, 9),
-        name="load",
-        out_shape=[shape(27 * C, C, BF), shape(C, C, BF)],
-        in_specs=[held_hbm, held_hbm],
-        out_specs=[whole(), whole()],
-        scratch_shapes=[pltpu.SemaphoreType.DMA((10,))],
-        compiler_params=pltpu.CompilerParams(vmem_limit_bytes=27 * C * C * 2 + SPARE),
-        cost_estimate=pl.CostEstimate(flops=0, bytes_accessed=27 * C * C * 4, transcendentals=0),
-    )(source, branch_weight[0])
+    kernel, mixing = call(
+        load_kernel, [], [source, branch_weight[0]],
+        [shape(27 * C, C, BF), shape(C, C, BF)], [], 0,
+    )
 
     wing = dm.fwd(0) + 1
     wide = own + 2 * wing
@@ -611,7 +600,7 @@
         first = dm.fwd(s) * G
         branch = jnp.where(section == s, mirrors[s][first:first + size], branch)
     branch, _ = lax.optimization_barrier((branch, results[0]))
-    branches = gather(branch, half + 1)
+    branches = gather(branch, 0)
     outs = [
         shape(dm.rows_of(t - 1) + CARRY, C, BF),
         shape(size + CARRY, C, BF),

time: 110 us -> 104 us (0.945)
  starting transfers between devices: 45.9 us -> 37.9 us
  waiting for transfers between devices: 29.1 us -> 33.6 us
  Pallas kernels: 28.6 us -> 26.9 us
    ppermute x14, starting transfers between devices: 26.6 us -> 17.9 us  [along(): return lax.ppermute(x, ('section', 'slab'), joint)]
    ppermute x14, waiting for transfers between devices: 4.5 us -> 7.74 us  [along(): return lax.ppermute(x, ('section', 'slab'), joint)]
    pallas_call x1 -> x0, Pallas kernels: 1.94 us -> none  [body(): pl.pallas_call(functools.partial(load_kernel, 9), name='load', out_shape=...]
    pallas_call x12 -> x13, Pallas kernels: 16.7 us -> 16.9 us  [call(): pl.pallas_call(kernel, out_shape=outs, in_specs=[scalar()] * len(scalars)...]
  transfers between devices with their start and end apart: 33 -> 33, of which waited for: 9 -> 12; matrix products, arithmetic and copies ran while one was open for 0% -> 0% of each run, Pallas kernels for 9% -> 8%
where the time goes in v5:
time: 104 us
  starting transfers between devices  37.9 us (36%)
  waiting for transfers between devices  33.6 us (32%)
  Pallas kernels  26.9 us (26%)
  local copies, waits for them, and re-layouts  4.52 us (4%)
  between operations  1.11 us (1%)
    ppermute x14, starting transfers between devices, along(): return lax.ppermute(x, ('section', 'slab'), joint)  17.9 us
    ppermute x8, waiting for transfers between devices, hop(): return lax.ppermute(x, 'section', [(source, target)])  17.3 us
    pallas_call x13, Pallas kernels, call(): pl.pallas_call(kernel, out_shape=outs, in_specs=[scalar()] * len(scalars)...  16.9 us
    pallas_call x1, Pallas kernels, body(): pl.pallas_call(functools.partial(weight_kernel, dm), name='weights', out_...  10 us
    ppermute x6, starting transfers between devices, rotate(): return lax.ppermute(x, 'slab', pairs)  8.54 us
    ppermute x8, starting transfers between devices, hop(): return lax.ppermute(x, 'section', [(source, target)])  7.87 us
    ppermute x14, waiting for transfers between devices, along(): return lax.ppermute(x, ('section', 'slab'), joint)  7.74 us
    ppermute x6, waiting for transfers between devices, rotate(): return lax.ppermute(x, 'slab', pairs)  6.58 us
  transfers between devices with their start and end apart: 33, of which 12 were waited for; matrix products, arithmetic and copies ran while one was open for 0% of the time, Pallas kernels for 8%

profile of v5, /device:TPU:7, one launch (start us, length us, event | category | flops | bytes accessed | tf_op | source)
XLA Modules:
  0.0 104.1 jit_solution(10542542655986116397)
XLA Ops:
  0.7 0.9 copy-done.2
  1.6 0.7 copy-done.3
  2.3 0.6 shard_map.93
  2.9 0.7 collective-permute-start
  3.6 0.9 collective-permute-done.refs_1_
  4.5 0.6 shard_map.94
  5.1 1.3 %collective-permute-start.1 = (bf16[4,32,256]{2,1,0:T(8,128)(2,1)S(1)}, bf16[4,32,256]{2,1,0:T(8,128)(2,1)S(1)}, u32[]{:S(2)}, u32[]{:S(2)}) collective-permute-start(bf16[4,32,256]{2,1,0:T(8,128)(2,1)S(1)} %get-tuple-element.50), channel_id=1, source_target_pairs={{0,2},{1,3},{2,4},{3,5},{4,6},{5,7},{6,0},{7,1},{8,10},{9,11},{10,... | collective-permute-start | bytes 196616 | tf_op jit(solution)/shard_map/ppermute | solution.py:501
  6.5 2.3 %collective-permute-start.2 = (bf16[4,32,256]{2,1,0:T(8,128)(2,1)S(1)}, bf16[4,32,256]{2,1,0:T(8,128)(2,1)S(1)}, u32[]{:S(2)}, u32[]{:S(2)}) collective-permute-start(bf16[4,32,256]{2,1,0:T(8,128)(2,1)S(1)} %get-tuple-element.51), channel_id=1, source_target_pairs={{0,4},{1,5},{2,6},{3,7},{4,0},{5,1},{6,2},{7,3},{8,12},{9,13},{10,... | collective-permute-start | bytes 196616 | tf_op jit(solution)/shard_map/ppermute | solution.py:501
  8.8 1.1 %collective-permute-start.3 = (bf16[4,32,256]{2,1,0:T(8,128)(2,1)S(1)}, bf16[4,32,256]{2,1,0:T(8,128)(2,1)S(1)}, u32[]{:S(2)}, u32[]{:S(2)}) collective-permute-start(bf16[4,32,256]{2,1,0:T(8,128)(2,1)S(1)} %get-tuple-element.52), channel_id=1, source_target_pairs={{0,6},{1,7},{2,0},{3,1},{4,2},{5,3},{6,4},{7,5},{8,14},{9,15},{10,... | collective-permute-start | bytes 196616 | tf_op jit(solution)/shard_map/ppermute | solution.py:501
  9.9 2.0 %copy-done = bf16[1,3,3,3,256,256]{5,4,3,2,1,0:T(8,128)(2,1)S(1)} copy-done((bf16[1,3,3,3,256,256]{5,4,3,2,1,0:T(8,128)(2,1)S(1)}, bf16[1,3,3,3,256,256]{5,4,3,2,1,0:T(8,128)(2,1)}, u32[]{:S(2)}) %copy-start) | copy-done | bytes 3538968
  11.9 0.9 copy-done.1
  13.0 0.9 collective-permute-done.2.refs_3_
  13.9 0.6 shard_map.96
  14.5 0.7 collective-permute-start.4
  15.2 0.6 shard_map.97
  15.8 0.7 collective-permute-start.5
  16.5 0.6 shard_map.98
  17.0 1.3 %collective-permute-start.6 = (bf16[384,256]{1,0:T(8,128)(2,1)S(1)}, bf16[384,256]{1,0:T(8,128)(2,1)S(1)}, u32[]{:S(2)}, u32[]{:S(2)}) collective-permute-start(bf16[384,256]{1,0:T(8,128)(2,1)S(1)} %get-tuple-element.61), channel_id=1, source_target_pairs={{16,24},{17,25},{18,26},{19,27},{20,28},{21,29},{22,30},{23,31}} | collective-permute-start | bytes 589832 | tf_op jit(solution)/shard_map/ppermute | solution.py:497
  18.3 1.3 %collective-permute-start.7 = (bf16[352,256]{1,0:T(8,128)(2,1)S(1)}, bf16[352,256]{1,0:T(8,128)(2,1)S(1)}, u32[]{:S(2)}, u32[]{:S(2)}) collective-permute-start(bf16[352,256]{1,0:T(8,128)(2,1)S(1)} %get-tuple-element.62), channel_id=1, source_target_pairs={{0,24},{1,25},{2,26},{3,27},{4,28},{5,29},{6,30},{7,31}} | collective-permute-start | bytes 540680 | tf_op jit(solution)/shard_map/ppermute | solution.py:497
  19.7 0.8 shard_map.100.refs_8_
  20.5 1.0 shard_map.99.refs_6_.refs_4_
  21.4 7.8 %collective-permute-done.7.refs_4_ = bf16[352,256]{1,0:T(8,128)(2,1)S(1)} collective-permute-done((bf16[352,256]{1,0:T(8,128)(2,1)S(1)}, bf16[352,256]{1,0:T(8,128)(2,1)S(1)}, u32[]{:S(2)}, u32[]{:S(2)}) %collective-permute-start.7) | collective-permute-done | bytes 180256 | tf_op jit(solution)/shard_map/ppermute | solution.py:497
  29.2 9.3 %collective-permute-done.6.refs_1_ = bf16[384,256]{1,0:T(8,128)(2,1)S(1)} collective-permute-done((bf16[384,256]{1,0:T(8,128)(2,1)S(1)}, bf16[384,256]{1,0:T(8,128)(2,1)S(1)}, u32[]{:S(2)}, u32[]{:S(2)}) %collective-permute-start.6) | collective-permute-done | bytes 196640 | tf_op jit(solution)/shard_map/ppermute | solution.py:497
  38.5 6.1 %shard_map.101 = (bf16[336,256]{1,0:T(8,128)(2,1)S(1)}, bf16[272,256]{1,0:T(8,128)(2,1)S(1)}, bf16[256,256]{1,0:T(8,128)(2,1)S(1)}, bf16[256,256]{1,0:T(8,128)(2,1)S(1)}) custom-call(s32[3]{0:T(128)S(1)} %pad_add_fusion.me_ref.refs_0_, bf16[384,256]{1,0:T(8,128)(2,1)S(1)} %collective-permute-done.6.refs_1_, ...), custom_call_target="tpu_custom_call" | custom-call | flops 2583691264 | bytes 8305664 | tf_op jit(solution)/shard_map/pallas_call | solution.py:466
  44.6 1.3 %collective-permute-start.8 = (bf16[336,256]{1,0:T(8,128)(2,1)S(1)}, bf16[336,256]{1,0:T(8,128)(2,1)S(1)}, u32[]{:S(2)}, u32[]{:S(2)}) collective-permute-start(bf16[336,256]{1,0:T(8,128)(2,1)S(1)} %get-tuple-element.67), channel_id=1, source_target_pairs={{24,16},{25,17},{26,18},{27,19},{28,20},{29,21},{30,22},{31,23}} | collective-permute-start | bytes 516104 | tf_op jit(solution)/shard_map/ppermute | solution.py:497
  46.0 3.9 %collective-permute-start.23 = (bf16[256,256]{1,0:T(8,128)(2,1)S(1)}, bf16[256,256]{1,0:T(8,128)(2,1)S(1)}, u32[]{:S(2)}, u32[]{:S(2)}) collective-permute-start(bf16[256,256]{1,0:T(8,128)(2,1)S(1)} %slice.4.refs_9_), channel_id=1, source_target_pairs={{0,4},{1,5},{2,6},{3,7},{4,0},{5,1},{6,2},{7,3},{8,12},{9,13},{10,... | collective-permute-start | bytes 393224 | tf_op jit(solution)/shard_map/ppermute | solution.py:520
  49.9 0.6 shard_map.102
  50.5 0.7 collective-permute-start.9
  51.1 3.0 %collective-permute-start.25 = (bf16[256,256]{1,0:T(8,128)(2,1)S(1)}, bf16[256,256]{1,0:T(8,128)(2,1)S(1)}, u32[]{:S(2)}, u32[]{:S(2)}) collective-permute-start(bf16[256,256]{1,0:T(8,128)(2,1)S(1)} %slice.4.refs_9_), channel_id=1, source_target_pairs={{0,1},{1,0},{2,3},{3,2},{4,5},{5,4},{6,7},{7,6},{8,9},{9,8},{10,11... | collective-permute-start | bytes 393224 | tf_op jit(solution)/shard_map/ppermute | solution.py:520
  54.2 1.1 %collective-permute-start.22 = (bf16[256,256]{1,0:T(8,128)(2,1)S(1)}, bf16[256,256]{1,0:T(8,128)(2,1)S(1)}, u32[]{:S(2)}, u32[]{:S(2)}) collective-permute-start(bf16[256,256]{1,0:T(8,128)(2,1)S(1)} %slice.4.refs_9_), channel_id=1, source_target_pairs={{0,2},{1,3},{2,4},{3,5},{4,6},{5,7},{6,0},{7,1},{8,10},{9,11},{10,... | collective-permute-start | bytes 393224 | tf_op jit(solution)/shard_map/ppermute | solution.py:520
  55.6 2.0 %collective-permute-done.23.refs_11_ = bf16[256,256]{1,0:T(8,128)(2,1)S(1)} collective-permute-done((bf16[256,256]{1,0:T(8,128)(2,1)S(1)}, bf16[256,256]{1,0:T(8,128)(2,1)S(1)}, u32[]{:S(2)}, u32[]{:S(2)}) %collective-permute-start.23) | collective-permute-done | bytes 131104 | tf_op jit(solution)/shard_map/ppermute | solution.py:520
  57.6 5.2 %collective-permute-start.27 = (bf16[256,256]{1,0:T(8,128)(2,1)S(1)}, bf16[256,256]{1,0:T(8,128)(2,1)S(1)}, u32[]{:S(2)}, u32[]{:S(2)}) collective-permute-start(bf16[256,256]{1,0:T(8,128)(2,1)S(1)} %collective-permute-done.23.refs_11_), channel_id=1, source_target_pairs={{0,1},{1,0},{2,3},{3,2},{4,5},{5,4},{6,7},{7,6},{8,9},{9,8},{10,11... | collective-permute-start | bytes 393224 | tf_op jit(solution)/shard_map/ppermute | solution.py:520
  62.9 1.3 %collective-permute-start.11 = (bf16[256,256]{1,0:T(8,128)(2,1)S(1)}, bf16[256,256]{1,0:T(8,128)(2,1)S(1)}, u32[]{:S(2)}, u32[]{:S(2)}) collective-permute-start(bf16[256,256]{1,0:T(8,128)(2,1)S(1)} %get-tuple-element.76), channel_id=1, source_target_pairs={{24,0},{25,1},{26,2},{27,3},{28,4},{29,5},{30,6},{31,7}} | collective-permute-start | bytes 393224 | tf_op jit(solution)/shard_map/ppermute | solution.py:497
  64.2 0.7 shard_map.103
  64.9 0.7 collective-permute-start.10
  65.6 1.4 %collective-permute-start.15 = (bf16[256,256]{1,0:T(8,128)(2,1)S(1)}, bf16[256,256]{1,0:T(8,128)(2,1)S(1)}, u32[]{:S(2)}, u32[]{:S(2)}) collective-permute-start(bf16[256,256]{1,0:T(8,128)(2,1)S(1)} %get-tuple-element.78.refs_1_), channel_id=1, source_target_pairs={{0,2},{1,3},{2,4},{3,5},{4,6},{5,7},{6,0},{7,1},{8,10},{9,11},{10,... | collective-permute-start | bytes 393224 | tf_op jit(solution)/shard_map/ppermute | solution.py:520
  67.3 0.6 collective-permute-start.26
  67.9 1.1 %collective-permute-done.17.refs_4_ = bf16[256,256]{1,0:T(8,128)(2,1)S(1)} collective-permute-done((bf16[256,256]{1,0:T(8,128)(2,1)S(1)}, bf16[256,256]{1,0:T(8,128)(2,1)S(1)}, u32[]{:S(2)}, u32[]{:S(2)}) %collective-permute-start.17) | collective-permute-done | bytes 131104 | tf_op jit(solution)/shard_map/ppermute | solution.py:520
  69.0 0.9 collective-permute-start.18
  69.9 4.6 %collective-permute-done.16.refs_3_ = bf16[256,256]{1,0:T(8,128)(2,1)S(1)} collective-permute-done((bf16[256,256]{1,0:T(8,128)(2,1)S(1)}, bf16[256,256]{1,0:T(8,128)(2,1)S(1)}, u32[]{:S(2)}, u32[]{:S(2)}) %collective-permute-start.16) | collective-permute-done | bytes 131104 | tf_op jit(solution)/shard_map/ppermute | solution.py:520
  74.4 0.9 collective-permute-start.21
  76.4 2.0 %collective-permute-start.14 = (bf16[272,256]{1,0:T(8,128)(2,1)S(1)}, bf16[272,256]{1,0:T(8,128)(2,1)S(1)}, u32[]{:S(2)}, u32[]{:S(2)}) collective-permute-start(bf16[272,256]{1,0:T(8,128)(2,1)S(1)} %shard_map.104.refs_3_), channel_id=1, source_target_pairs={{0,6},{1,7},{2,0},{3,1},{4,2},{5,3},{6,4},{7,5},{8,14},{9,15},{10,... | collective-permute-start | bytes 417800 | tf_op jit(solution)/shard_map/ppermute | solution.py:501
  78.9 1.4 %collective-permute-start.12 = (bf16[272,256]{1,0:T(8,128)(2,1)S(1)}, bf16[272,256]{1,0:T(8,128)(2,1)S(1)}, u32[]{:S(2)}, u32[]{:S(2)}) collective-permute-start(bf16[272,256]{1,0:T(8,128)(2,1)S(1)} %shard_map.104.refs_3_), channel_id=1, source_target_pairs={{0,2},{1,3},{2,4},{3,5},{4,6},{5,7},{6,0},{7,1},{8,10},{9,11},{10,... | collective-permute-start | bytes 417800 | tf_op jit(solution)/shard_map/ppermute | solution.py:501
  80.2 1.3 %collective-permute-start.29 = (bf16[272,256]{1,0:T(8,128)(2,1)S(1)}, bf16[272,256]{1,0:T(8,128)(2,1)S(1)}, u32[]{:S(2)}, u32[]{:S(2)}) collective-permute-start(bf16[272,256]{1,0:T(8,128)(2,1)S(1)} %shard_map.104.refs_3_), channel_id=1, source_target_pairs={{0,1},{1,0},{2,3},{3,2},{4,5},{5,4},{6,7},{7,6},{8,9},{9,8},{10,11... | collective-permute-start | bytes 417800 | tf_op jit(solution)/shard_map/ppermute | solution.py:505
  81.5 4.1 %shard_map.105 = (bf16[2304,2048]{1,0:T(8,128)(2,1)S(1)}, bf16[256,2048]{1,0:T(8,128)(2,1)S(1)}) custom-call(s32[3]{0:T(128)S(1)} %pad_add_fusion.me_ref.refs_0_, bf16[256,256]{1,0:T(8,128)(2,1)S(1)} %get-tuple-element.78.refs_1_, bf16[256,256]{1,0:T(8,128)(2,1)S(1)} %collective-permute-done.15.refs_2_, ...), custom_call_target="tpu_custom_call" | custom-call | flops 1048576000 | bytes 12582912 | tf_op jit(solution)/shard_map/pallas_call | solution.py:466
  85.6 5.7 %collective-permute-done.13.refs_5_ = bf16[272,256]{1,0:T(8,128)(2,1)S(1)} collective-permute-done((bf16[272,256]{1,0:T(8,128)(2,1)S(1)}, bf16[272,256]{1,0:T(8,128)(2,1)S(1)}, u32[]{:S(2)}, u32[]{:S(2)}) %collective-permute-start.13) | collective-permute-done | bytes 139296 | tf_op jit(solution)/shard_map/ppermute | solution.py:501
  91.3 1.0 collective-permute-start.30
  93.9 10.0 %weights.1 = (f32[9,3,256,256]{3,2,1,0:T(8,128)}, f32[256,256]{1,0:T(8,128)}, f32[3,256]{1,0:T(4,128)}, f32[1,1]{1,0:T(1,128)}) custom-call(s32[3]{0:T(128)S(1)} %pad_add_fusion.me_ref.refs_0_, bf16[2304,2048]{1,0:T(8,128)(2,1)S(1)} %get-tuple-element.81.refs_1_, bf16[256,2048]{1,0:T(8,128)(2,1)S(1)} %get-tuple-element.82.refs_2_, ...), custom_call_target="tpu_custom_call" | custom-call | flops 7516192768 | bytes 18942980 | tf_op jit(solution)/shard_map/weights/pallas_call | solution.py:677
  (47 shorter events, 4.2 us)
Async XLA Ops:
  0.7 0.9 copy-start.2
  1.6 0.7 copy-start.3
  2.9 1.7 %collective-permute-start = (bf16[144,256]{1,0:T(8,128)(2,1)S(1)}, bf16[144,256]{1,0:T(8,128)(2,1)S(1)}, u32[]{:S(2)}, u32[]{:S(2)}) collective-permute-start(bf16[144,256]{1,0:T(8,128)(2,1)S(1)} %get-tuple-element.48), channel_id=1, source_target_pairs={{0,1},{1,0},{2,3},{3,2},{4,5},{5,4},{6,7},{7,6},{8,9},{9,8},{10,11... | collective-permute-start | bytes 221192 | tf_op jit(solution)/shard_map/ppermute | solution.py:505
  5.1 7.9 %collective-permute-start.1 = (bf16[4,32,256]{2,1,0:T(8,128)(2,1)S(1)}, bf16[4,32,256]{2,1,0:T(8,128)(2,1)S(1)}, u32[]{:S(2)}, u32[]{:S(2)}) collective-permute-start(bf16[4,32,256]{2,1,0:T(8,128)(2,1)S(1)} %get-tuple-element.50), channel_id=1, source_target_pairs={{0,2},{1,3},{2,4},{3,5},{4,6},{5,7},{6,0},{7,1},{8,10},{9,11},{10,... | collective-permute-start | bytes 196616 | tf_op jit(solution)/shard_map/ppermute | solution.py:501
  6.5 7.4 %collective-permute-start.2 = (bf16[4,32,256]{2,1,0:T(8,128)(2,1)S(1)}, bf16[4,32,256]{2,1,0:T(8,128)(2,1)S(1)}, u32[]{:S(2)}, u32[]{:S(2)}) collective-permute-start(bf16[4,32,256]{2,1,0:T(8,128)(2,1)S(1)} %get-tuple-element.51), channel_id=1, source_target_pairs={{0,4},{1,5},{2,6},{3,7},{4,0},{5,1},{6,2},{7,3},{8,12},{9,13},{10,... | collective-permute-start | bytes 196616 | tf_op jit(solution)/shard_map/ppermute | solution.py:501
  8.8 5.1 %collective-permute-start.3 = (bf16[4,32,256]{2,1,0:T(8,128)(2,1)S(1)}, bf16[4,32,256]{2,1,0:T(8,128)(2,1)S(1)}, u32[]{:S(2)}, u32[]{:S(2)}) collective-permute-start(bf16[4,32,256]{2,1,0:T(8,128)(2,1)S(1)} %get-tuple-element.52), channel_id=1, source_target_pairs={{0,6},{1,7},{2,0},{3,1},{4,2},{5,3},{6,4},{7,5},{8,14},{9,15},{10,... | collective-permute-start | bytes 196616 | tf_op jit(solution)/shard_map/ppermute | solution.py:501
  9.9 2.0 %copy-start = (bf16[1,3,3,3,256,256]{5,4,3,2,1,0:T(8,128)(2,1)S(1)}, bf16[1,3,3,3,256,256]{5,4,3,2,1,0:T(8,128)(2,1)}, u32[]{:S(2)}) copy-start(bf16[1,3,3,3,256,256]{5,4,3,2,1,0:T(8,128)(2,1)} %param.9) | copy-start | bytes 10616836
  11.9 0.9 copy-start.1
  14.5 0.7 collective-permute-start.4
  15.7 3.9 %copy-start.5 = (bf16[256,3]{0,1:T(4,128)(2,1)S(1)}, bf16[256,3]{0,1:T(4,128)(2,1)}, u32[]{:S(2)}) copy-start(bf16[256,3]{0,1:T(4,128)(2,1)} %param.11) | copy-start | bytes 4612
  15.8 3.9 %copy-start.4 = (s32[3,3]{1,0:T(4,128)S(1)}, s32[3,3]{1,0:T(4,128)}, u32[]{:S(2)}) copy-start(s32[3,3]{1,0:T(4,128)} %off_ref.1) | copy-start | bytes 112
  15.8 0.7 collective-permute-start.5
  17.0 21.4 %collective-permute-start.6 = (bf16[384,256]{1,0:T(8,128)(2,1)S(1)}, bf16[384,256]{1,0:T(8,128)(2,1)S(1)}, u32[]{:S(2)}, u32[]{:S(2)}) collective-permute-start(bf16[384,256]{1,0:T(8,128)(2,1)S(1)} %get-tuple-element.61), channel_id=1, source_target_pairs={{16,24},{17,25},{18,26},{19,27},{20,28},{21,29},{22,30},{23,31}} | collective-permute-start | bytes 589832 | tf_op jit(solution)/shard_map/ppermute | solution.py:497
  18.3 10.9 %collective-permute-start.7 = (bf16[352,256]{1,0:T(8,128)(2,1)S(1)}, bf16[352,256]{1,0:T(8,128)(2,1)S(1)}, u32[]{:S(2)}, u32[]{:S(2)}) collective-permute-start(bf16[352,256]{1,0:T(8,128)(2,1)S(1)} %get-tuple-element.62), channel_id=1, source_target_pairs={{0,24},{1,25},{2,26},{3,27},{4,28},{5,29},{6,30},{7,31}} | collective-permute-start | bytes 540680 | tf_op jit(solution)/shard_map/ppermute | solution.py:497
  44.6 5.3 %collective-permute-start.8 = (bf16[336,256]{1,0:T(8,128)(2,1)S(1)}, bf16[336,256]{1,0:T(8,128)(2,1)S(1)}, u32[]{:S(2)}, u32[]{:S(2)}) collective-permute-start(bf16[336,256]{1,0:T(8,128)(2,1)S(1)} %get-tuple-element.67), channel_id=1, source_target_pairs={{24,16},{25,17},{26,18},{27,19},{28,20},{29,21},{30,22},{31,23}} | collective-permute-start | bytes 516104 | tf_op jit(solution)/shard_map/ppermute | solution.py:497
  45.9 9.3 %collective-permute-start.24 = (bf16[256,256]{1,0:T(8,128)(2,1)S(1)}, bf16[256,256]{1,0:T(8,128)(2,1)S(1)}, u32[]{:S(2)}, u32[]{:S(2)}) collective-permute-start(bf16[256,256]{1,0:T(8,128)(2,1)S(1)} %slice.4.refs_9_), channel_id=1, source_target_pairs={{0,6},{1,7},{2,0},{3,1},{4,2},{5,3},{6,4},{7,5},{8,14},{9,15},{10,... | collective-permute-start | bytes 393224 | tf_op jit(solution)/shard_map/ppermute | solution.py:520
  46.0 11.6 %collective-permute-start.23 = (bf16[256,256]{1,0:T(8,128)(2,1)S(1)}, bf16[256,256]{1,0:T(8,128)(2,1)S(1)}, u32[]{:S(2)}, u32[]{:S(2)}) collective-permute-start(bf16[256,256]{1,0:T(8,128)(2,1)S(1)} %slice.4.refs_9_), channel_id=1, source_target_pairs={{0,4},{1,5},{2,6},{3,7},{4,0},{5,1},{6,2},{7,3},{8,12},{9,13},{10,... | collective-permute-start | bytes 393224 | tf_op jit(solution)/shard_map/ppermute | solution.py:520
  50.5 12.4 %collective-permute-start.9 = (bf16[304,256]{1,0:T(8,128)(2,1)S(1)}, bf16[304,256]{1,0:T(8,128)(2,1)S(1)}, u32[]{:S(2)}, u32[]{:S(2)}) collective-permute-start(bf16[304,256]{1,0:T(8,128)(2,1)S(1)} %get-tuple-element.70), channel_id=1, source_target_pairs={{16,8},{17,9},{18,10},{19,11},{20,12},{21,13},{22,14},{23,15}} | collective-permute-start | bytes 466952 | tf_op jit(solution)/shard_map/ppermute | solution.py:497
  51.1 11.6 %collective-permute-start.25 = (bf16[256,256]{1,0:T(8,128)(2,1)S(1)}, bf16[256,256]{1,0:T(8,128)(2,1)S(1)}, u32[]{:S(2)}, u32[]{:S(2)}) collective-permute-start(bf16[256,256]{1,0:T(8,128)(2,1)S(1)} %slice.4.refs_9_), channel_id=1, source_target_pairs={{0,1},{1,0},{2,3},{3,2},{4,5},{5,4},{6,7},{7,6},{8,9},{9,8},{10,11... | collective-permute-start | bytes 393224 | tf_op jit(solution)/shard_map/ppermute | solution.py:520
  54.2 8.6 %collective-permute-start.22 = (bf16[256,256]{1,0:T(8,128)(2,1)S(1)}, bf16[256,256]{1,0:T(8,128)(2,1)S(1)}, u32[]{:S(2)}, u32[]{:S(2)}) collective-permute-start(bf16[256,256]{1,0:T(8,128)(2,1)S(1)} %slice.4.refs_9_), channel_id=1, source_target_pairs={{0,2},{1,3},{2,4},{3,5},{4,6},{5,7},{6,0},{7,1},{8,10},{9,11},{10,... | collective-permute-start | bytes 393224 | tf_op jit(solution)/shard_map/ppermute | solution.py:520
  55.3 9.7 %collective-permute-start.28 = (bf16[256,256]{1,0:T(8,128)(2,1)S(1)}, bf16[256,256]{1,0:T(8,128)(2,1)S(1)}, u32[]{:S(2)}, u32[]{:S(2)}) collective-permute-start(bf16[256,256]{1,0:T(8,128)(2,1)S(1)} %collective-permute-done.24.refs_12_), channel_id=1, source_target_pairs={{0,1},{1,0},{2,3},{3,2},{4,5},{5,4},{6,7},{7,6},{8,9},{9,8},{10,11... | collective-permute-start | bytes 393224 | tf_op jit(solution)/shard_map/ppermute | solution.py:520
  57.6 8.0 %collective-permute-start.27 = (bf16[256,256]{1,0:T(8,128)(2,1)S(1)}, bf16[256,256]{1,0:T(8,128)(2,1)S(1)}, u32[]{:S(2)}, u32[]{:S(2)}) collective-permute-start(bf16[256,256]{1,0:T(8,128)(2,1)S(1)} %collective-permute-done.23.refs_11_), channel_id=1, source_target_pairs={{0,1},{1,0},{2,3},{3,2},{4,5},{5,4},{6,7},{7,6},{8,9},{9,8},{10,11... | collective-permute-start | bytes 393224 | tf_op jit(solution)/shard_map/ppermute | solution.py:520
  62.8 6.2 %collective-permute-start.17 = (bf16[256,256]{1,0:T(8,128)(2,1)S(1)}, bf16[256,256]{1,0:T(8,128)(2,1)S(1)}, u32[]{:S(2)}, u32[]{:S(2)}) collective-permute-start(bf16[256,256]{1,0:T(8,128)(2,1)S(1)} %get-tuple-element.78.refs_1_), channel_id=1, source_target_pairs={{0,6},{1,7},{2,0},{3,1},{4,2},{5,3},{6,4},{7,5},{8,14},{9,15},{10,... | collective-permute-start | bytes 393224 | tf_op jit(solution)/shard_map/ppermute | solution.py:520
  62.8 11.7 %collective-permute-start.16 = (bf16[256,256]{1,0:T(8,128)(2,1)S(1)}, bf16[256,256]{1,0:T(8,128)(2,1)S(1)}, u32[]{:S(2)}, u32[]{:S(2)}) collective-permute-start(bf16[256,256]{1,0:T(8,128)(2,1)S(1)} %get-tuple-element.78.refs_1_), channel_id=1, source_target_pairs={{0,4},{1,5},{2,6},{3,7},{4,0},{5,1},{6,2},{7,3},{8,12},{9,13},{10,... | collective-permute-start | bytes 393224 | tf_op jit(solution)/shard_map/ppermute | solution.py:520
  62.9 4.4 %collective-permute-start.11 = (bf16[256,256]{1,0:T(8,128)(2,1)S(1)}, bf16[256,256]{1,0:T(8,128)(2,1)S(1)}, u32[]{:S(2)}, u32[]{:S(2)}) collective-permute-start(bf16[256,256]{1,0:T(8,128)(2,1)S(1)} %get-tuple-element.76), channel_id=1, source_target_pairs={{24,0},{25,1},{26,2},{27,3},{28,4},{29,5},{30,6},{31,7}} | collective-permute-start | bytes 393224 | tf_op jit(solution)/shard_map/ppermute | solution.py:497
  64.9 10.4 %collective-permute-start.10 = (bf16[272,256]{1,0:T(8,128)(2,1)S(1)}, bf16[272,256]{1,0:T(8,128)(2,1)S(1)}, u32[]{:S(2)}, u32[]{:S(2)}) collective-permute-start(bf16[272,256]{1,0:T(8,128)(2,1)S(1)} %get-tuple-element.73), channel_id=1, source_target_pairs={{8,0},{9,1},{10,2},{11,3},{12,4},{13,5},{14,6},{15,7}} | collective-permute-start | bytes 417800 | tf_op jit(solution)/shard_map/ppermute | solution.py:497
  65.6 9.7 %collective-permute-start.15 = (bf16[256,256]{1,0:T(8,128)(2,1)S(1)}, bf16[256,256]{1,0:T(8,128)(2,1)S(1)}, u32[]{:S(2)}, u32[]{:S(2)}) collective-permute-start(bf16[256,256]{1,0:T(8,128)(2,1)S(1)} %get-tuple-element.78.refs_1_), channel_id=1, source_target_pairs={{0,2},{1,3},{2,4},{3,5},{4,6},{5,7},{6,0},{7,1},{8,10},{9,11},{10,... | collective-permute-start | bytes 393224 | tf_op jit(solution)/shard_map/ppermute | solution.py:520
  67.3 9.1 %collective-permute-start.26 = (bf16[256,256]{1,0:T(8,128)(2,1)S(1)}, bf16[256,256]{1,0:T(8,128)(2,1)S(1)}, u32[]{:S(2)}, u32[]{:S(2)}) collective-permute-start(bf16[256,256]{1,0:T(8,128)(2,1)S(1)} %collective-permute-done.22.refs_10_), channel_id=1, source_target_pairs={{0,1},{1,0},{2,3},{3,2},{4,5},{5,4},{6,7},{7,6},{8,9},{9,8},{10,11... | collective-permute-start | bytes 393224 | tf_op jit(solution)/shard_map/ppermute | solution.py:520
  69.0 9.4 %collective-permute-start.18 = (bf16[256,256]{1,0:T(8,128)(2,1)S(1)}, bf16[256,256]{1,0:T(8,128)(2,1)S(1)}, u32[]{:S(2)}, u32[]{:S(2)}) collective-permute-start(bf16[256,256]{1,0:T(8,128)(2,1)S(1)} %get-tuple-element.78.refs_1_), channel_id=1, source_target_pairs={{0,1},{1,0},{2,3},{3,2},{4,5},{5,4},{6,7},{7,6},{8,9},{9,8},{10,11... | collective-permute-start | bytes 393224 | tf_op jit(solution)/shard_map/ppermute | solution.py:520
  74.4 4.4 %collective-permute-start.21 = (bf16[256,256]{1,0:T(8,128)(2,1)S(1)}, bf16[256,256]{1,0:T(8,128)(2,1)S(1)}, u32[]{:S(2)}, u32[]{:S(2)}) collective-permute-start(bf16[256,256]{1,0:T(8,128)(2,1)S(1)} %collective-permute-done.17.refs_4_), channel_id=1, source_target_pairs={{0,1},{1,0},{2,3},{3,2},{4,5},{5,4},{6,7},{7,6},{8,9},{9,8},{10,11... | collective-permute-start | bytes 393224 | tf_op jit(solution)/shard_map/ppermute | solution.py:520
  75.3 4.9 %collective-permute-start.20 = (bf16[256,256]{1,0:T(8,128)(2,1)S(1)}, bf16[256,256]{1,0:T(8,128)(2,1)S(1)}, u32[]{:S(2)}, u32[]{:S(2)}) collective-permute-start(bf16[256,256]{1,0:T(8,128)(2,1)S(1)} %collective-permute-done.16.refs_3_), channel_id=1, source_target_pairs={{0,1},{1,0},{2,3},{3,2},{4,5},{5,4},{6,7},{7,6},{8,9},{9,8},{10,11... | collective-permute-start | bytes 393224 | tf_op jit(solution)/shard_map/ppermute | solution.py:520
  75.3 6.2 %collective-permute-start.19 = (bf16[256,256]{1,0:T(8,128)(2,1)S(1)}, bf16[256,256]{1,0:T(8,128)(2,1)S(1)}, u32[]{:S(2)}, u32[]{:S(2)}) collective-permute-start(bf16[256,256]{1,0:T(8,128)(2,1)S(1)} %collective-permute-done.15.refs_2_), channel_id=1, source_target_pairs={{0,1},{1,0},{2,3},{3,2},{4,5},{5,4},{6,7},{7,6},{8,9},{9,8},{10,11... | collective-permute-start | bytes 393224 | tf_op jit(solution)/shard_map/ppermute | solution.py:520
  76.4 9.2 %collective-permute-start.14 = (bf16[272,256]{1,0:T(8,128)(2,1)S(1)}, bf16[272,256]{1,0:T(8,128)(2,1)S(1)}, u32[]{:S(2)}, u32[]{:S(2)}) collective-permute-start(bf16[272,256]{1,0:T(8,128)(2,1)S(1)} %shard_map.104.refs_3_), channel_id=1, source_target_pairs={{0,6},{1,7},{2,0},{3,1},{4,2},{5,3},{6,4},{7,5},{8,14},{9,15},{10,... | collective-permute-start | bytes 417800 | tf_op jit(solution)/shard_map/ppermute | solution.py:501
  78.4 12.9 %collective-permute-start.13 = (bf16[272,256]{1,0:T(8,128)(2,1)S(1)}, bf16[272,256]{1,0:T(8,128)(2,1)S(1)}, u32[]{:S(2)}, u32[]{:S(2)}) collective-permute-start(bf16[272,256]{1,0:T(8,128)(2,1)S(1)} %shard_map.104.refs_3_), channel_id=1, source_target_pairs={{0,4},{1,5},{2,6},{3,7},{4,0},{5,1},{6,2},{7,3},{8,12},{9,13},{10,... | collective-permute-start | bytes 417800 | tf_op jit(solution)/shard_map/ppermute | solution.py:501
  78.9 12.5 %collective-permute-start.12 = (bf16[272,256]{1,0:T(8,128)(2,1)S(1)}, bf16[272,256]{1,0:T(8,128)(2,1)S(1)}, u32[]{:S(2)}, u32[]{:S(2)}) collective-permute-start(bf16[272,256]{1,0:T(8,128)(2,1)S(1)} %shard_map.104.refs_3_), channel_id=1, source_target_pairs={{0,2},{1,3},{2,4},{3,5},{4,6},{5,7},{6,0},{7,1},{8,10},{9,11},{10,... | collective-permute-start | bytes 417800 | tf_op jit(solution)/shard_map/ppermute | solution.py:501
  80.2 12.6 %collective-permute-start.29 = (bf16[272,256]{1,0:T(8,128)(2,1)S(1)}, bf16[272,256]{1,0:T(8,128)(2,1)S(1)}, u32[]{:S(2)}, u32[]{:S(2)}) collective-permute-start(bf16[272,256]{1,0:T(8,128)(2,1)S(1)} %shard_map.104.refs_3_), channel_id=1, source_target_pairs={{0,1},{1,0},{2,3},{3,2},{4,5},{5,4},{6,7},{7,6},{8,9},{9,8},{10,11... | collective-permute-start | bytes 417800 | tf_op jit(solution)/shard_map/ppermute | solution.py:505
  91.3 2.0 %collective-permute-start.30 = (bf16[272,256]{1,0:T(8,128)(2,1)S(1)}, bf16[272,256]{1,0:T(8,128)(2,1)S(1)}, u32[]{:S(2)}, u32[]{:S(2)}) collective-permute-start(bf16[272,256]{1,0:T(8,128)(2,1)S(1)} %collective-permute-done.12.refs_4_), channel_id=1, source_target_pairs={{0,1},{1,0},{2,3},{3,2},{4,5},{5,4},{6,7},{7,6},{8,9},{9,8},{10,11... | collective-permute-start | bytes 417800 | tf_op jit(solution)/shard_map/ppermute | solution.py:505
  92.4 1.4 %collective-permute-start.31 = (bf16[272,256]{1,0:T(8,128)(2,1)S(1)}, bf16[272,256]{1,0:T(8,128)(2,1)S(1)}, u32[]{:S(2)}, u32[]{:S(2)}) collective-permute-start(bf16[272,256]{1,0:T(8,128)(2,1)S(1)} %collective-permute-done.13.refs_5_), channel_id=1, source_target_pairs={{0,1},{1,0},{2,3},{3,2},{4,5},{5,4},{6,7},{7,6},{8,9},{9,8},{10,11... | collective-permute-start | bytes 417800 | tf_op jit(solution)/shard_map/ppermute | solution.py:505
  92.4 1.6 %collective-permute-start.32 = (bf16[272,256]{1,0:T(8,128)(2,1)S(1)}, bf16[272,256]{1,0:T(8,128)(2,1)S(1)}, u32[]{:S(2)}, u32[]{:S(2)}) collective-permute-start(bf16[272,256]{1,0:T(8,128)(2,1)S(1)} %collective-permute-done.14.refs_6_), channel_id=1, source_target_pairs={{0,1},{1,0},{2,3},{3,2},{4,5},{5,4},{6,7},{7,6},{8,9},{9,8},{10,11... | collective-permute-start | bytes 417800 | tf_op jit(solution)/shard_map/ppermute | solution.py:505

commit v6 on v3

--- a/solution.py
+++ b/solution.py
@@ -611,7 +611,7 @@
         first = dm.fwd(s) * G
         branch = jnp.where(section == s, mirrors[s][first:first + size], branch)
     branch, _ = lax.optimization_barrier((branch, results[0]))
-    branches = gather(branch, half + 1)
+    branches = gather(branch, 0)
     outs = [
         shape(dm.rows_of(t - 1) + CARRY, C, BF),
         shape(size + CARRY, C, BF),
@@ -665,7 +665,9 @@
         [pltpu.VMEM((cells_all + 2 * PAD, C), F32)],
         2 * 10 * cells_all * C * 100,
     )
-    near = [block] + [rotate(block, r) for r in range(1, parts)]
+    near = [block]
+    for r in range(1, parts):
+        near.append(rotate(block, r))
     *far, xt = lax.optimization_barrier((*near[1:], xt))
     near = [block] + far
     blocks = list(near)

time: 110 us -> 104 us (0.945)
  starting transfers between devices: 45.9 us -> 38.9 us
    ppermute x14, starting transfers between devices: 26.6 us -> 19 us  [along(): return lax.ppermute(x, ('section', 'slab'), joint)]
    ppermute x14, waiting for transfers between devices: 4.5 us -> 5.76 us  [along(): return lax.ppermute(x, ('section', 'slab'), joint)]
  transfers between devices with their start and end apart: 33 -> 33, of which waited for: 9 -> 10; matrix products, arithmetic and copies ran while one was open for 0% -> 0% of each run, Pallas kernels for 9% -> 9%
where the time goes in v6:
time: 104 us; the launch traced here: 103 us
  starting transfers between devices  38.9 us (37%)
  waiting for transfers between devices  30 us (29%)
  Pallas kernels  28.6 us (28%)
  local copies, waits for them, and re-layouts  4.52 us (4%)
  between operations  1.12 us (1%)
    ppermute x14, starting transfers between devices, along(): return lax.ppermute(x, ('section', 'slab'), joint)  19 us
    pallas_call x12, Pallas kernels, call(): pl.pallas_call(kernel, out_shape=outs, in_specs=[scalar()] * len(scalars)...  16.7 us
    ppermute x8, waiting for transfers between devices, hop(): return lax.ppermute(x, 'section', [(source, target)])  16.6 us
    pallas_call x1, Pallas kernels, body(): pl.pallas_call(functools.partial(weight_kernel, dm), name='weights', out_...  10 us
    ppermute x6, starting transfers between devices, rotate(): return lax.ppermute(x, 'slab', pairs)  8.54 us
    ppermute x8, starting transfers between devices, hop(): return lax.ppermute(x, 'section', [(source, target)])  7.87 us
    ppermute x14, waiting for transfers between devices, along(): return lax.ppermute(x, ('section', 'slab'), joint)  5.76 us
    ppermute x6, waiting for transfers between devices, rotate(): return lax.ppermute(x, 'slab', pairs)  5.73 us
  transfers between devices with their start and end apart: 33, of which 10 were waited for; matrix products, arithmetic and copies ran while one was open for 0% of the time, Pallas kernels for 9%

profile of v6, /device:TPU:7, one launch (start us, length us, event | category | flops | bytes accessed | tf_op | source)
XLA Modules:
  0.0 103.3 jit_solution(17284037580096572773)
XLA Ops:
  0.7 0.9 copy-done.2
  1.6 0.7 copy-done.3
  2.3 0.6 shard_map.93
  2.9 0.7 collective-permute-start
  3.6 0.9 collective-permute-done.refs_1_
  4.5 0.6 shard_map.94
  5.1 1.3 %collective-permute-start.1 = (bf16[4,32,256]{2,1,0:T(8,128)(2,1)S(1)}, bf16[4,32,256]{2,1,0:T(8,128)(2,1)S(1)}, u32[]{:S(2)}, u32[]{:S(2)}) collective-permute-start(bf16[4,32,256]{2,1,0:T(8,128)(2,1)S(1)} %get-tuple-element.50), channel_id=1, source_target_pairs={{0,2},{1,3},{2,4},{3,5},{4,6},{5,7},{6,0},{7,1},{8,10},{9,11},{10,... | collective-permute-start | bytes 196616 | tf_op jit(solution)/shard_map/ppermute | solution.py:505
  6.5 2.3 %collective-permute-start.2 = (bf16[4,32,256]{2,1,0:T(8,128)(2,1)S(1)}, bf16[4,32,256]{2,1,0:T(8,128)(2,1)S(1)}, u32[]{:S(2)}, u32[]{:S(2)}) collective-permute-start(bf16[4,32,256]{2,1,0:T(8,128)(2,1)S(1)} %get-tuple-element.51), channel_id=1, source_target_pairs={{0,4},{1,5},{2,6},{3,7},{4,0},{5,1},{6,2},{7,3},{8,12},{9,13},{10,... | collective-permute-start | bytes 196616 | tf_op jit(solution)/shard_map/ppermute | solution.py:505
  8.8 1.1 %collective-permute-start.3 = (bf16[4,32,256]{2,1,0:T(8,128)(2,1)S(1)}, bf16[4,32,256]{2,1,0:T(8,128)(2,1)S(1)}, u32[]{:S(2)}, u32[]{:S(2)}) collective-permute-start(bf16[4,32,256]{2,1,0:T(8,128)(2,1)S(1)} %get-tuple-element.52), channel_id=1, source_target_pairs={{0,6},{1,7},{2,0},{3,1},{4,2},{5,3},{6,4},{7,5},{8,14},{9,15},{10,... | collective-permute-start | bytes 196616 | tf_op jit(solution)/shard_map/ppermute | solution.py:505
  9.9 2.0 %copy-done = bf16[1,3,3,3,256,256]{5,4,3,2,1,0:T(8,128)(2,1)S(1)} copy-done((bf16[1,3,3,3,256,256]{5,4,3,2,1,0:T(8,128)(2,1)S(1)}, bf16[1,3,3,3,256,256]{5,4,3,2,1,0:T(8,128)(2,1)}, u32[]{:S(2)}) %copy-start) | copy-done | bytes 3538968
  11.9 0.9 copy-done.1
  12.8 1.9 %load.1 = (bf16[6912,256]{1,0:T(8,128)(2,1)S(1)}, bf16[256,256]{1,0:T(8,128)(2,1)S(1)}) custom-call(bf16[6912,256]{1,0:T(8,128)(2,1)S(1)} %bitcast.14, bf16[256,256]{1,0:T(8,128)(2,1)S(1)} %bitcast.15), custom_call_target="tpu_custom_call" | custom-call | bytes 7077888 | tf_op jit(solution)/shard_map/load/pallas_call | solution.py:528
  14.8 0.6 shard_map.95
  15.4 0.7 collective-permute-start.4
  16.1 0.6 shard_map.96
  16.6 0.7 collective-permute-start.5
  17.3 0.6 shard_map.97
  17.9 1.3 %collective-permute-start.6 = (bf16[384,256]{1,0:T(8,128)(2,1)S(1)}, bf16[384,256]{1,0:T(8,128)(2,1)S(1)}, u32[]{:S(2)}, u32[]{:S(2)}) collective-permute-start(bf16[384,256]{1,0:T(8,128)(2,1)S(1)} %get-tuple-element.61), channel_id=1, source_target_pairs={{16,24},{17,25},{18,26},{19,27},{20,28},{21,29},{22,30},{23,31}} | collective-permute-start | bytes 589832 | tf_op jit(solution)/shard_map/ppermute | solution.py:501
  19.2 1.3 %collective-permute-start.7 = (bf16[352,256]{1,0:T(8,128)(2,1)S(1)}, bf16[352,256]{1,0:T(8,128)(2,1)S(1)}, u32[]{:S(2)}, u32[]{:S(2)}) collective-permute-start(bf16[352,256]{1,0:T(8,128)(2,1)S(1)} %get-tuple-element.62), channel_id=1, source_target_pairs={{0,24},{1,25},{2,26},{3,27},{4,28},{5,29},{6,30},{7,31}} | collective-permute-start | bytes 540680 | tf_op jit(solution)/shard_map/ppermute | solution.py:501
  20.5 0.8 shard_map.99.refs_8_
  21.3 1.0 shard_map.98.refs_6_.refs_4_
  22.3 7.0 %collective-permute-done.7.refs_4_ = bf16[352,256]{1,0:T(8,128)(2,1)S(1)} collective-permute-done((bf16[352,256]{1,0:T(8,128)(2,1)S(1)}, bf16[352,256]{1,0:T(8,128)(2,1)S(1)}, u32[]{:S(2)}, u32[]{:S(2)}) %collective-permute-start.7) | collective-permute-done | bytes 180256 | tf_op jit(solution)/shard_map/ppermute | solution.py:501
  29.3 9.3 %collective-permute-done.6.refs_1_ = bf16[384,256]{1,0:T(8,128)(2,1)S(1)} collective-permute-done((bf16[384,256]{1,0:T(8,128)(2,1)S(1)}, bf16[384,256]{1,0:T(8,128)(2,1)S(1)}, u32[]{:S(2)}, u32[]{:S(2)}) %collective-permute-start.6) | collective-permute-done | bytes 196640 | tf_op jit(solution)/shard_map/ppermute | solution.py:501
  38.6 6.1 %shard_map.100 = (bf16[336,256]{1,0:T(8,128)(2,1)S(1)}, bf16[272,256]{1,0:T(8,128)(2,1)S(1)}, bf16[256,256]{1,0:T(8,128)(2,1)S(1)}, bf16[256,256]{1,0:T(8,128)(2,1)S(1)}) custom-call(s32[3]{0:T(128)S(1)} %pad_add_fusion.me_ref.refs_0_, bf16[384,256]{1,0:T(8,128)(2,1)S(1)} %collective-permute-done.6.refs_1_, ...), custom_call_target="tpu_custom_call" | custom-call | flops 2583691264 | bytes 8305664 | tf_op jit(solution)/shard_map/pallas_call | solution.py:470
  44.8 1.3 %collective-permute-start.8 = (bf16[336,256]{1,0:T(8,128)(2,1)S(1)}, bf16[336,256]{1,0:T(8,128)(2,1)S(1)}, u32[]{:S(2)}, u32[]{:S(2)}) collective-permute-start(bf16[336,256]{1,0:T(8,128)(2,1)S(1)} %get-tuple-element.67), channel_id=1, source_target_pairs={{24,16},{25,17},{26,18},{27,19},{28,20},{29,21},{30,22},{31,23}} | collective-permute-start | bytes 516104 | tf_op jit(solution)/shard_map/ppermute | solution.py:501
  46.1 2.8 %collective-permute-start.23 = (bf16[256,256]{1,0:T(8,128)(2,1)S(1)}, bf16[256,256]{1,0:T(8,128)(2,1)S(1)}, u32[]{:S(2)}, u32[]{:S(2)}) collective-permute-start(bf16[256,256]{1,0:T(8,128)(2,1)S(1)} %slice.4.refs_9_), channel_id=1, source_target_pairs={{0,4},{1,5},{2,6},{3,7},{4,0},{5,1},{6,2},{7,3},{8,12},{9,13},{10,... | collective-permute-start | bytes 393224 | tf_op jit(solution)/shard_map/ppermute | solution.py:524
  48.9 0.6 shard_map.101
  49.5 0.7 collective-permute-start.9
  50.2 3.6 %collective-permute-start.25 = (bf16[256,256]{1,0:T(8,128)(2,1)S(1)}, bf16[256,256]{1,0:T(8,128)(2,1)S(1)}, u32[]{:S(2)}, u32[]{:S(2)}) collective-permute-start(bf16[256,256]{1,0:T(8,128)(2,1)S(1)} %slice.4.refs_9_), channel_id=1, source_target_pairs={{0,1},{1,0},{2,3},{3,2},{4,5},{5,4},{6,7},{7,6},{8,9},{9,8},{10,11... | collective-permute-start | bytes 393224 | tf_op jit(solution)/shard_map/ppermute | solution.py:524
  53.8 1.1 %collective-permute-start.22 = (bf16[256,256]{1,0:T(8,128)(2,1)S(1)}, bf16[256,256]{1,0:T(8,128)(2,1)S(1)}, u32[]{:S(2)}, u32[]{:S(2)}) collective-permute-start(bf16[256,256]{1,0:T(8,128)(2,1)S(1)} %slice.4.refs_9_), channel_id=1, source_target_pairs={{0,2},{1,3},{2,4},{3,5},{4,6},{5,7},{6,0},{7,1},{8,10},{9,11},{10,... | collective-permute-start | bytes 393224 | tf_op jit(solution)/shard_map/ppermute | solution.py:524
  54.9 1.0 collective-permute-start.28
  55.9 6.1 %collective-permute-start.27 = (bf16[256,256]{1,0:T(8,128)(2,1)S(1)}, bf16[256,256]{1,0:T(8,128)(2,1)S(1)}, u32[]{:S(2)}, u32[]{:S(2)}) collective-permute-start(bf16[256,256]{1,0:T(8,128)(2,1)S(1)} %collective-permute-done.23.refs_11_), channel_id=1, source_target_pairs={{0,1},{1,0},{2,3},{3,2},{4,5},{5,4},{6,7},{7,6},{8,9},{9,8},{10,11... | collective-permute-start | bytes 393224 | tf_op jit(solution)/shard_map/ppermute | solution.py:524
  62.1 1.3 %collective-permute-start.11 = (bf16[256,256]{1,0:T(8,128)(2,1)S(1)}, bf16[256,256]{1,0:T(8,128)(2,1)S(1)}, u32[]{:S(2)}, u32[]{:S(2)}) collective-permute-start(bf16[256,256]{1,0:T(8,128)(2,1)S(1)} %get-tuple-element.76), channel_id=1, source_target_pairs={{24,0},{25,1},{26,2},{27,3},{28,4},{29,5},{30,6},{31,7}} | collective-permute-start | bytes 393224 | tf_op jit(solution)/shard_map/ppermute | solution.py:501
  63.4 0.7 shard_map.102
  64.2 0.7 collective-permute-start.10
  64.8 1.4 %collective-permute-start.15 = (bf16[256,256]{1,0:T(8,128)(2,1)S(1)}, bf16[256,256]{1,0:T(8,128)(2,1)S(1)}, u32[]{:S(2)}, u32[]{:S(2)}) collective-permute-start(bf16[256,256]{1,0:T(8,128)(2,1)S(1)} %get-tuple-element.78.refs_1_), channel_id=1, source_target_pairs={{0,2},{1,3},{2,4},{3,5},{4,6},{5,7},{6,0},{7,1},{8,10},{9,11},{10,... | collective-permute-start | bytes 393224 | tf_op jit(solution)/shard_map/ppermute | solution.py:524
  66.5 0.6 collective-permute-start.26
  67.1 1.1 %collective-permute-done.17.refs_4_ = bf16[256,256]{1,0:T(8,128)(2,1)S(1)} collective-permute-done((bf16[256,256]{1,0:T(8,128)(2,1)S(1)}, bf16[256,256]{1,0:T(8,128)(2,1)S(1)}, u32[]{:S(2)}, u32[]{:S(2)}) %collective-permute-start.17) | collective-permute-done | bytes 131104 | tf_op jit(solution)/shard_map/ppermute | solution.py:524
  68.2 0.9 collective-permute-start.18
  69.1 4.6 %collective-permute-done.16.refs_3_ = bf16[256,256]{1,0:T(8,128)(2,1)S(1)} collective-permute-done((bf16[256,256]{1,0:T(8,128)(2,1)S(1)}, bf16[256,256]{1,0:T(8,128)(2,1)S(1)}, u32[]{:S(2)}, u32[]{:S(2)}) %collective-permute-start.16) | collective-permute-done | bytes 131104 | tf_op jit(solution)/shard_map/ppermute | solution.py:524
  73.7 0.9 collective-permute-start.21
  75.6 2.0 %collective-permute-start.14 = (bf16[272,256]{1,0:T(8,128)(2,1)S(1)}, bf16[272,256]{1,0:T(8,128)(2,1)S(1)}, u32[]{:S(2)}, u32[]{:S(2)}) collective-permute-start(bf16[272,256]{1,0:T(8,128)(2,1)S(1)} %shard_map.103.refs_3_), channel_id=1, source_target_pairs={{0,6},{1,7},{2,0},{3,1},{4,2},{5,3},{6,4},{7,5},{8,14},{9,15},{10,... | collective-permute-start | bytes 417800 | tf_op jit(solution)/shard_map/ppermute | solution.py:505
  78.1 1.4 %collective-permute-start.12 = (bf16[272,256]{1,0:T(8,128)(2,1)S(1)}, bf16[272,256]{1,0:T(8,128)(2,1)S(1)}, u32[]{:S(2)}, u32[]{:S(2)}) collective-permute-start(bf16[272,256]{1,0:T(8,128)(2,1)S(1)} %shard_map.103.refs_3_), channel_id=1, source_target_pairs={{0,2},{1,3},{2,4},{3,5},{4,6},{5,7},{6,0},{7,1},{8,10},{9,11},{10,... | collective-permute-start | bytes 417800 | tf_op jit(solution)/shard_map/ppermute | solution.py:505
  79.5 1.3 %collective-permute-start.29 = (bf16[272,256]{1,0:T(8,128)(2,1)S(1)}, bf16[272,256]{1,0:T(8,128)(2,1)S(1)}, u32[]{:S(2)}, u32[]{:S(2)}) collective-permute-start(bf16[272,256]{1,0:T(8,128)(2,1)S(1)} %shard_map.103.refs_3_), channel_id=1, source_target_pairs={{0,1},{1,0},{2,3},{3,2},{4,5},{5,4},{6,7},{7,6},{8,9},{9,8},{10,11... | collective-permute-start | bytes 417800 | tf_op jit(solution)/shard_map/ppermute | solution.py:509
  80.7 4.1 %shard_map.104 = (bf16[2304,2048]{1,0:T(8,128)(2,1)S(1)}, bf16[256,2048]{1,0:T(8,128)(2,1)S(1)}) custom-call(s32[3]{0:T(128)S(1)} %pad_add_fusion.me_ref.refs_0_, bf16[256,256]{1,0:T(8,128)(2,1)S(1)} %get-tuple-element.78.refs_1_, bf16[256,256]{1,0:T(8,128)(2,1)S(1)} %collective-permute-done.15.refs_2_, ...), custom_call_target="tpu_custom_call" | custom-call | flops 1048576000 | bytes 12582912 | tf_op jit(solution)/shard_map/pallas_call | solution.py:470
  84.8 5.7 %collective-permute-done.13.refs_5_ = bf16[272,256]{1,0:T(8,128)(2,1)S(1)} collective-permute-done((bf16[272,256]{1,0:T(8,128)(2,1)S(1)}, bf16[272,256]{1,0:T(8,128)(2,1)S(1)}, u32[]{:S(2)}, u32[]{:S(2)}) %collective-permute-start.13) | collective-permute-done | bytes 139296 | tf_op jit(solution)/shard_map/ppermute | solution.py:505
  90.6 1.0 collective-permute-start.30
  93.1 10.0 %weights.1 = (f32[9,3,256,256]{3,2,1,0:T(8,128)}, f32[256,256]{1,0:T(8,128)}, f32[3,256]{1,0:T(4,128)}, f32[1,1]{1,0:T(1,128)}) custom-call(s32[3]{0:T(128)S(1)} %pad_add_fusion.me_ref.refs_0_, bf16[2304,2048]{1,0:T(8,128)(2,1)S(1)} %get-tuple-element.81.refs_1_, bf16[256,2048]{1,0:T(8,128)(2,1)S(1)} %get-tuple-element.82.refs_2_, ...), custom_call_target="tpu_custom_call" | custom-call | flops 7516192768 | bytes 18942980 | tf_op jit(solution)/shard_map/weights/pallas_call | solution.py:690
  (47 shorter events, 3.6 us)
Async XLA Ops:
  0.7 0.9 copy-start.2
  1.6 0.7 copy-start.3
  2.9 1.7 %collective-permute-start = (bf16[144,256]{1,0:T(8,128)(2,1)S(1)}, bf16[144,256]{1,0:T(8,128)(2,1)S(1)}, u32[]{:S(2)}, u32[]{:S(2)}) collective-permute-start(bf16[144,256]{1,0:T(8,128)(2,1)S(1)} %get-tuple-element.48), channel_id=1, source_target_pairs={{0,1},{1,0},{2,3},{3,2},{4,5},{5,4},{6,7},{7,6},{8,9},{9,8},{10,11... | collective-permute-start | bytes 221192 | tf_op jit(solution)/shard_map/ppermute | solution.py:509
  5.1 9.6 %collective-permute-start.1 = (bf16[4,32,256]{2,1,0:T(8,128)(2,1)S(1)}, bf16[4,32,256]{2,1,0:T(8,128)(2,1)S(1)}, u32[]{:S(2)}, u32[]{:S(2)}) collective-permute-start(bf16[4,32,256]{2,1,0:T(8,128)(2,1)S(1)} %get-tuple-element.50), channel_id=1, source_target_pairs={{0,2},{1,3},{2,4},{3,5},{4,6},{5,7},{6,0},{7,1},{8,10},{9,11},{10,... | collective-permute-start | bytes 196616 | tf_op jit(solution)/shard_map/ppermute | solution.py:505
  6.5 8.3 %collective-permute-start.2 = (bf16[4,32,256]{2,1,0:T(8,128)(2,1)S(1)}, bf16[4,32,256]{2,1,0:T(8,128)(2,1)S(1)}, u32[]{:S(2)}, u32[]{:S(2)}) collective-permute-start(bf16[4,32,256]{2,1,0:T(8,128)(2,1)S(1)} %get-tuple-element.51), channel_id=1, source_target_pairs={{0,4},{1,5},{2,6},{3,7},{4,0},{5,1},{6,2},{7,3},{8,12},{9,13},{10,... | collective-permute-start | bytes 196616 | tf_op jit(solution)/shard_map/ppermute | solution.py:505
  8.8 6.0 %collective-permute-start.3 = (bf16[4,32,256]{2,1,0:T(8,128)(2,1)S(1)}, bf16[4,32,256]{2,1,0:T(8,128)(2,1)S(1)}, u32[]{:S(2)}, u32[]{:S(2)}) collective-permute-start(bf16[4,32,256]{2,1,0:T(8,128)(2,1)S(1)} %get-tuple-element.52), channel_id=1, source_target_pairs={{0,6},{1,7},{2,0},{3,1},{4,2},{5,3},{6,4},{7,5},{8,14},{9,15},{10,... | collective-permute-start | bytes 196616 | tf_op jit(solution)/shard_map/ppermute | solution.py:505
  9.9 2.0 %copy-start = (bf16[1,3,3,3,256,256]{5,4,3,2,1,0:T(8,128)(2,1)S(1)}, bf16[1,3,3,3,256,256]{5,4,3,2,1,0:T(8,128)(2,1)}, u32[]{:S(2)}) copy-start(bf16[1,3,3,3,256,256]{5,4,3,2,1,0:T(8,128)(2,1)} %param.9) | copy-start | bytes 10616836
  11.9 0.9 copy-start.1
  15.4 0.7 collective-permute-start.4
  16.6 3.9 %copy-start.5 = (bf16[256,3]{0,1:T(4,128)(2,1)S(1)}, bf16[256,3]{0,1:T(4,128)(2,1)}, u32[]{:S(2)}) copy-start(bf16[256,3]{0,1:T(4,128)(2,1)} %param.11) | copy-start | bytes 4612
  16.6 3.9 %copy-start.4 = (s32[3,3]{1,0:T(4,128)S(1)}, s32[3,3]{1,0:T(4,128)}, u32[]{:S(2)}) copy-start(s32[3,3]{1,0:T(4,128)} %off_ref.1) | copy-start | bytes 112
  16.6 0.7 collective-permute-start.5
  17.9 20.7 %collective-permute-start.6 = (bf16[384,256]{1,0:T(8,128)(2,1)S(1)}, bf16[384,256]{1,0:T(8,128)(2,1)S(1)}, u32[]{:S(2)}, u32[]{:S(2)}) collective-permute-start(bf16[384,256]{1,0:T(8,128)(2,1)S(1)} %get-tuple-element.61), channel_id=1, source_target_pairs={{16,24},{17,25},{18,26},{19,27},{20,28},{21,29},{22,30},{23,31}} | collective-permute-start | bytes 589832 | tf_op jit(solution)/shard_map/ppermute | solution.py:501
  19.2 10.1 %collective-permute-start.7 = (bf16[352,256]{1,0:T(8,128)(2,1)S(1)}, bf16[352,256]{1,0:T(8,128)(2,1)S(1)}, u32[]{:S(2)}, u32[]{:S(2)}) collective-permute-start(bf16[352,256]{1,0:T(8,128)(2,1)S(1)} %get-tuple-element.62), channel_id=1, source_target_pairs={{0,24},{1,25},{2,26},{3,27},{4,28},{5,29},{6,30},{7,31}} | collective-permute-start | bytes 540680 | tf_op jit(solution)/shard_map/ppermute | solution.py:501
  44.8 4.2 %collective-permute-start.8 = (bf16[336,256]{1,0:T(8,128)(2,1)S(1)}, bf16[336,256]{1,0:T(8,128)(2,1)S(1)}, u32[]{:S(2)}, u32[]{:S(2)}) collective-permute-start(bf16[336,256]{1,0:T(8,128)(2,1)S(1)} %get-tuple-element.67), channel_id=1, source_target_pairs={{24,16},{25,17},{26,18},{27,19},{28,20},{29,21},{30,22},{31,23}} | collective-permute-start | bytes 516104 | tf_op jit(solution)/shard_map/ppermute | solution.py:501
  46.1 8.8 %collective-permute-start.24 = (bf16[256,256]{1,0:T(8,128)(2,1)S(1)}, bf16[256,256]{1,0:T(8,128)(2,1)S(1)}, u32[]{:S(2)}, u32[]{:S(2)}) collective-permute-start(bf16[256,256]{1,0:T(8,128)(2,1)S(1)} %slice.4.refs_9_), channel_id=1, source_target_pairs={{0,6},{1,7},{2,0},{3,1},{4,2},{5,3},{6,4},{7,5},{8,14},{9,15},{10,... | collective-permute-start | bytes 393224 | tf_op jit(solution)/shard_map/ppermute | solution.py:524
  46.1 9.8 %collective-permute-start.23 = (bf16[256,256]{1,0:T(8,128)(2,1)S(1)}, bf16[256,256]{1,0:T(8,128)(2,1)S(1)}, u32[]{:S(2)}, u32[]{:S(2)}) collective-permute-start(bf16[256,256]{1,0:T(8,128)(2,1)S(1)} %slice.4.refs_9_), channel_id=1, source_target_pairs={{0,4},{1,5},{2,6},{3,7},{4,0},{5,1},{6,2},{7,3},{8,12},{9,13},{10,... | collective-permute-start | bytes 393224 | tf_op jit(solution)/shard_map/ppermute | solution.py:524
  49.5 12.6 %collective-permute-start.9 = (bf16[304,256]{1,0:T(8,128)(2,1)S(1)}, bf16[304,256]{1,0:T(8,128)(2,1)S(1)}, u32[]{:S(2)}, u32[]{:S(2)}) collective-permute-start(bf16[304,256]{1,0:T(8,128)(2,1)S(1)} %get-tuple-element.70), channel_id=1, source_target_pairs={{16,8},{17,9},{18,10},{19,11},{20,12},{21,13},{22,14},{23,15}} | collective-permute-start | bytes 466952 | tf_op jit(solution)/shard_map/ppermute | solution.py:501
  50.2 11.8 %collective-permute-start.25 = (bf16[256,256]{1,0:T(8,128)(2,1)S(1)}, bf16[256,256]{1,0:T(8,128)(2,1)S(1)}, u32[]{:S(2)}, u32[]{:S(2)}) collective-permute-start(bf16[256,256]{1,0:T(8,128)(2,1)S(1)} %slice.4.refs_9_), channel_id=1, source_target_pairs={{0,1},{1,0},{2,3},{3,2},{4,5},{5,4},{6,7},{7,6},{8,9},{9,8},{10,11... | collective-permute-start | bytes 393224 | tf_op jit(solution)/shard_map/ppermute | solution.py:524
  53.8 8.2 %collective-permute-start.22 = (bf16[256,256]{1,0:T(8,128)(2,1)S(1)}, bf16[256,256]{1,0:T(8,128)(2,1)S(1)}, u32[]{:S(2)}, u32[]{:S(2)}) collective-permute-start(bf16[256,256]{1,0:T(8,128)(2,1)S(1)} %slice.4.refs_9_), channel_id=1, source_target_pairs={{0,2},{1,3},{2,4},{3,5},{4,6},{5,7},{6,0},{7,1},{8,10},{9,11},{10,... | collective-permute-start | bytes 393224 | tf_op jit(solution)/shard_map/ppermute | solution.py:524
  54.9 9.2 %collective-permute-start.28 = (bf16[256,256]{1,0:T(8,128)(2,1)S(1)}, bf16[256,256]{1,0:T(8,128)(2,1)S(1)}, u32[]{:S(2)}, u32[]{:S(2)}) collective-permute-start(bf16[256,256]{1,0:T(8,128)(2,1)S(1)} %collective-permute-done.24.refs_12_), channel_id=1, source_target_pairs={{0,1},{1,0},{2,3},{3,2},{4,5},{5,4},{6,7},{7,6},{8,9},{9,8},{10,11... | collective-permute-start | bytes 393224 | tf_op jit(solution)/shard_map/ppermute | solution.py:524
  55.9 8.9 %collective-permute-start.27 = (bf16[256,256]{1,0:T(8,128)(2,1)S(1)}, bf16[256,256]{1,0:T(8,128)(2,1)S(1)}, u32[]{:S(2)}, u32[]{:S(2)}) collective-permute-start(bf16[256,256]{1,0:T(8,128)(2,1)S(1)} %collective-permute-done.23.refs_11_), channel_id=1, source_target_pairs={{0,1},{1,0},{2,3},{3,2},{4,5},{5,4},{6,7},{7,6},{8,9},{9,8},{10,11... | collective-permute-start | bytes 393224 | tf_op jit(solution)/shard_map/ppermute | solution.py:524
  62.0 6.2 %collective-permute-start.17 = (bf16[256,256]{1,0:T(8,128)(2,1)S(1)}, bf16[256,256]{1,0:T(8,128)(2,1)S(1)}, u32[]{:S(2)}, u32[]{:S(2)}) collective-permute-start(bf16[256,256]{1,0:T(8,128)(2,1)S(1)} %get-tuple-element.78.refs_1_), channel_id=1, source_target_pairs={{0,6},{1,7},{2,0},{3,1},{4,2},{5,3},{6,4},{7,5},{8,14},{9,15},{10,... | collective-permute-start | bytes 393224 | tf_op jit(solution)/shard_map/ppermute | solution.py:524
  62.0 11.7 %collective-permute-start.16 = (bf16[256,256]{1,0:T(8,128)(2,1)S(1)}, bf16[256,256]{1,0:T(8,128)(2,1)S(1)}, u32[]{:S(2)}, u32[]{:S(2)}) collective-permute-start(bf16[256,256]{1,0:T(8,128)(2,1)S(1)} %get-tuple-element.78.refs_1_), channel_id=1, source_target_pairs={{0,4},{1,5},{2,6},{3,7},{4,0},{5,1},{6,2},{7,3},{8,12},{9,13},{10,... | collective-permute-start | bytes 393224 | tf_op jit(solution)/shard_map/ppermute | solution.py:524
  62.1 4.4 %collective-permute-start.11 = (bf16[256,256]{1,0:T(8,128)(2,1)S(1)}, bf16[256,256]{1,0:T(8,128)(2,1)S(1)}, u32[]{:S(2)}, u32[]{:S(2)}) collective-permute-start(bf16[256,256]{1,0:T(8,128)(2,1)S(1)} %get-tuple-element.76), channel_id=1, source_target_pairs={{24,0},{25,1},{26,2},{27,3},{28,4},{29,5},{30,6},{31,7}} | collective-permute-start | bytes 393224 | tf_op jit(solution)/shard_map/ppermute | solution.py:501
  64.2 10.4 %collective-permute-start.10 = (bf16[272,256]{1,0:T(8,128)(2,1)S(1)}, bf16[272,256]{1,0:T(8,128)(2,1)S(1)}, u32[]{:S(2)}, u32[]{:S(2)}) collective-permute-start(bf16[272,256]{1,0:T(8,128)(2,1)S(1)} %get-tuple-element.73), channel_id=1, source_target_pairs={{8,0},{9,1},{10,2},{11,3},{12,4},{13,5},{14,6},{15,7}} | collective-permute-start | bytes 417800 | tf_op jit(solution)/shard_map/ppermute | solution.py:501
  64.8 9.7 %collective-permute-start.15 = (bf16[256,256]{1,0:T(8,128)(2,1)S(1)}, bf16[256,256]{1,0:T(8,128)(2,1)S(1)}, u32[]{:S(2)}, u32[]{:S(2)}) collective-permute-start(bf16[256,256]{1,0:T(8,128)(2,1)S(1)} %get-tuple-element.78.refs_1_), channel_id=1, source_target_pairs={{0,2},{1,3},{2,4},{3,5},{4,6},{5,7},{6,0},{7,1},{8,10},{9,11},{10,... | collective-permute-start | bytes 393224 | tf_op jit(solution)/shard_map/ppermute | solution.py:524
  66.5 9.1 %collective-permute-start.26 = (bf16[256,256]{1,0:T(8,128)(2,1)S(1)}, bf16[256,256]{1,0:T(8,128)(2,1)S(1)}, u32[]{:S(2)}, u32[]{:S(2)}) collective-permute-start(bf16[256,256]{1,0:T(8,128)(2,1)S(1)} %collective-permute-done.22.refs_10_), channel_id=1, source_target_pairs={{0,1},{1,0},{2,3},{3,2},{4,5},{5,4},{6,7},{7,6},{8,9},{9,8},{10,11... | collective-permute-start | bytes 393224 | tf_op jit(solution)/shard_map/ppermute | solution.py:524
  68.2 9.4 %collective-permute-start.18 = (bf16[256,256]{1,0:T(8,128)(2,1)S(1)}, bf16[256,256]{1,0:T(8,128)(2,1)S(1)}, u32[]{:S(2)}, u32[]{:S(2)}) collective-permute-start(bf16[256,256]{1,0:T(8,128)(2,1)S(1)} %get-tuple-element.78.refs_1_), channel_id=1, source_target_pairs={{0,1},{1,0},{2,3},{3,2},{4,5},{5,4},{6,7},{7,6},{8,9},{9,8},{10,11... | collective-permute-start | bytes 393224 | tf_op jit(solution)/shard_map/ppermute | solution.py:524
  73.7 4.4 %collective-permute-start.21 = (bf16[256,256]{1,0:T(8,128)(2,1)S(1)}, bf16[256,256]{1,0:T(8,128)(2,1)S(1)}, u32[]{:S(2)}, u32[]{:S(2)}) collective-permute-start(bf16[256,256]{1,0:T(8,128)(2,1)S(1)} %collective-permute-done.17.refs_4_), channel_id=1, source_target_pairs={{0,1},{1,0},{2,3},{3,2},{4,5},{5,4},{6,7},{7,6},{8,9},{9,8},{10,11... | collective-permute-start | bytes 393224 | tf_op jit(solution)/shard_map/ppermute | solution.py:524
  74.5 4.9 %collective-permute-start.20 = (bf16[256,256]{1,0:T(8,128)(2,1)S(1)}, bf16[256,256]{1,0:T(8,128)(2,1)S(1)}, u32[]{:S(2)}, u32[]{:S(2)}) collective-permute-start(bf16[256,256]{1,0:T(8,128)(2,1)S(1)} %collective-permute-done.16.refs_3_), channel_id=1, source_target_pairs={{0,1},{1,0},{2,3},{3,2},{4,5},{5,4},{6,7},{7,6},{8,9},{9,8},{10,11... | collective-permute-start | bytes 393224 | tf_op jit(solution)/shard_map/ppermute | solution.py:524
  74.5 6.2 %collective-permute-start.19 = (bf16[256,256]{1,0:T(8,128)(2,1)S(1)}, bf16[256,256]{1,0:T(8,128)(2,1)S(1)}, u32[]{:S(2)}, u32[]{:S(2)}) collective-permute-start(bf16[256,256]{1,0:T(8,128)(2,1)S(1)} %collective-permute-done.15.refs_2_), channel_id=1, source_target_pairs={{0,1},{1,0},{2,3},{3,2},{4,5},{5,4},{6,7},{7,6},{8,9},{9,8},{10,11... | collective-permute-start | bytes 393224 | tf_op jit(solution)/shard_map/ppermute | solution.py:524
  75.6 9.2 %collective-permute-start.14 = (bf16[272,256]{1,0:T(8,128)(2,1)S(1)}, bf16[272,256]{1,0:T(8,128)(2,1)S(1)}, u32[]{:S(2)}, u32[]{:S(2)}) collective-permute-start(bf16[272,256]{1,0:T(8,128)(2,1)S(1)} %shard_map.103.refs_3_), channel_id=1, source_target_pairs={{0,6},{1,7},{2,0},{3,1},{4,2},{5,3},{6,4},{7,5},{8,14},{9,15},{10,... | collective-permute-start | bytes 417800 | tf_op jit(solution)/shard_map/ppermute | solution.py:505
  77.6 12.9 %collective-permute-start.13 = (bf16[272,256]{1,0:T(8,128)(2,1)S(1)}, bf16[272,256]{1,0:T(8,128)(2,1)S(1)}, u32[]{:S(2)}, u32[]{:S(2)}) collective-permute-start(bf16[272,256]{1,0:T(8,128)(2,1)S(1)} %shard_map.103.refs_3_), channel_id=1, source_target_pairs={{0,4},{1,5},{2,6},{3,7},{4,0},{5,1},{6,2},{7,3},{8,12},{9,13},{10,... | collective-permute-start | bytes 417800 | tf_op jit(solution)/shard_map/ppermute | solution.py:505
  78.1 12.5 %collective-permute-start.12 = (bf16[272,256]{1,0:T(8,128)(2,1)S(1)}, bf16[272,256]{1,0:T(8,128)(2,1)S(1)}, u32[]{:S(2)}, u32[]{:S(2)}) collective-permute-start(bf16[272,256]{1,0:T(8,128)(2,1)S(1)} %shard_map.103.refs_3_), channel_id=1, source_target_pairs={{0,2},{1,3},{2,4},{3,5},{4,6},{5,7},{6,0},{7,1},{8,10},{9,11},{10,... | collective-permute-start | bytes 417800 | tf_op jit(solution)/shard_map/ppermute | solution.py:505
  79.5 12.6 %collective-permute-start.29 = (bf16[272,256]{1,0:T(8,128)(2,1)S(1)}, bf16[272,256]{1,0:T(8,128)(2,1)S(1)}, u32[]{:S(2)}, u32[]{:S(2)}) collective-permute-start(bf16[272,256]{1,0:T(8,128)(2,1)S(1)} %shard_map.103.refs_3_), channel_id=1, source_target_pairs={{0,1},{1,0},{2,3},{3,2},{4,5},{5,4},{6,7},{7,6},{8,9},{9,8},{10,11... | collective-permute-start | bytes 417800 | tf_op jit(solution)/shard_map/ppermute | solution.py:509
  90.6 2.0 %collective-permute-start.30 = (bf16[272,256]{1,0:T(8,128)(2,1)S(1)}, bf16[272,256]{1,0:T(8,128)(2,1)S(1)}, u32[]{:S(2)}, u32[]{:S(2)}) collective-permute-start(bf16[272,256]{1,0:T(8,128)(2,1)S(1)} %collective-permute-done.12.refs_4_), channel_id=1, source_target_pairs={{0,1},{1,0},{2,3},{3,2},{4,5},{5,4},{6,7},{7,6},{8,9},{9,8},{10,11... | collective-permute-start | bytes 417800 | tf_op jit(solution)/shard_map/ppermute | solution.py:509
  91.6 1.4 %collective-permute-start.31 = (bf16[272,256]{1,0:T(8,128)(2,1)S(1)}, bf16[272,256]{1,0:T(8,128)(2,1)S(1)}, u32[]{:S(2)}, u32[]{:S(2)}) collective-permute-start(bf16[272,256]{1,0:T(8,128)(2,1)S(1)} %collective-permute-done.13.refs_5_), channel_id=1, source_target_pairs={{0,1},{1,0},{2,3},{3,2},{4,5},{5,4},{6,7},{7,6},{8,9},{9,8},{10,11... | collective-permute-start | bytes 417800 | tf_op jit(solution)/shard_map/ppermute | solution.py:509
  91.6 1.6 %collective-permute-start.32 = (bf16[272,256]{1,0:T(8,128)(2,1)S(1)}, bf16[272,256]{1,0:T(8,128)(2,1)S(1)}, u32[]{:S(2)}, u32[]{:S(2)}) collective-permute-start(bf16[272,256]{1,0:T(8,128)(2,1)S(1)} %collective-permute-done.14.refs_6_), channel_id=1, source_target_pairs={{0,1},{1,0},{2,3},{3,2},{4,5},{5,4},{6,7},{7,6},{8,9},{9,8},{10,11... | collective-permute-start | bytes 417800 | tf_op jit(solution)/shard_map/ppermute | solution.py:509
